TPU v7x, 32 devices: a whole 2x2x4 slice. The times are simulated.
32 devices in a mesh: grp: 2 (over y), col: 8 (over z, x), row: 2 (over core).
Axes of the slice: x: 2, y: 2, z: 4, core: 2. Of those that a mesh axis runs over, the one named last changes fastest.
Arguments:
- pair_block: float32 [4, 16, 1152, 128], P('grp', 'row', 'col'), parts along dimension 0, may hold values from -260 to 260
- query_single: bfloat16 [4, 16, 768], P('grp', 'row'), parts along dimension 0, may hold values from -70 to 70
- key_single: bfloat16 [2304, 768], P(('grp', 'col')), parts along dimension 0, may hold values from -70 to 70
- query_chain: int32 [4, 16], P('grp', 'row'), parts along dimension 0, may hold values from 0 to 23
- key_chain: int32 [2304], P(('grp', 'col')), parts along dimension 0, may hold values from 0 to 23, never falling along the last dimension, each value on 1 to 144 neighbouring positions
- query_mask: int32 [4, 16], P('grp', 'row'), parts along dimension 0, may hold values 0 or 1
- key_mask: int32 [2304], P(('grp', 'col')), parts along dimension 0, may hold values 0 or 1
- timestep: int32 [2], P('grp'), parts along dimension 0, may hold values from 0 to 49
- time_table: bfloat16 [50, 768], replicated, may hold values from -6 to 6
- norm_gain: float32 [768], replicated, may hold values from 0.1 to 1.9
- left_proj: bfloat16 [768, 8], replicated, may hold values from -0.21875 to 0.21875
- right_proj: bfloat16 [768, 8], replicated, may hold values from -0.21875 to 0.21875
- outer_proj: bfloat16 [64, 128], replicated, may hold values from -0.75 to 0.75
- bias_proj: float32 [128, 12], replicated, may hold values from -0.75 to 0.75
- chain_weight: float32 [12], replicated, may hold values from -2 to 2
- query_proj: bfloat16 [768, 1536], P(None, 'col'), may hold values from -0.21875 to 0.21875
- kv_proj: bfloat16 [768, 1536], P(None, 'row'), may hold values from -0.21875 to 0.21875
- out_proj: bfloat16 [768, 768], replicated, may hold values from -0.75 to 0.75
Outputs:
- new_pair: float32 [4, 16, 1152, 128], P('grp', 'row', 'col'), parts along dimension 0
- single_update: bfloat16 [4, 16, 768], P('grp', 'row'), parts along dimension 0
There are 2 independent parts, one for each index of `grp`. A program takes and returns all parts, laid end to end along the dimension named above; an argument that names none is the same for every part. Nothing has to cross between parts.
Inputs may be any that keep to these rules, and one draw needn't show every extreme that they name: `key_chain`: never falling along the residues; each of the 24 chains holds at least one residue.
All inputs are finite; a program needn't handle non-finite values. No bound on the sum of `query_mask` or of `key_mask` on one device may be relied on, other than what follows from the above.
Results may differ from a plain program's by a relative error of at most 0.0082.
Values may be sent and summed in bfloat16 or wider, within the bound.
No kernel may reach another device: no remote copies, remote signals or barrier semaphores. Data moves between devices by JAX's collectives and lax.ppermute only.
A program may use at most 64 MiB of HBM per device.

v0:
```python
import math

import jax
import jax.numpy as jnp
from jax import lax
from jax.sharding import PartitionSpec as P

EPSILON = 1e-05
HIGHEST = lax.Precision.HIGHEST


def combined_all(part, axis, combine):
    gathered = jax.tree.map(lambda a: lax.all_gather(a, axis), part)

    def take(source):
        return jax.tree.map(lambda a: lax.dynamic_index_in_dim(a, source, 0, False), gathered)

    return lax.fori_loop(
        1, lax.axis_size(axis), lambda source, state: combine(state, take(source)), take(0)
    )


def normalize(features, norm_gain):
    average = jnp.mean(features, axis=-1, keepdims=True)
    centred = features - average
    spread = jnp.mean(centred * centred, axis=-1, keepdims=True)
    return (centred * lax.rsqrt(spread + EPSILON) * norm_gain).astype(jnp.bfloat16)


def flat_dot(left, right):
    flat_left = left.reshape(-1, left.shape[-1])
    product = jnp.dot(flat_left, right, preferred_element_type=jnp.float32)
    return product.reshape(left.shape[:-1] + (right.shape[-1],))


def combine_parts(former, latter):
    peak_former, total_former, summed_former = former
    peak_latter, total_latter, summed_latter = latter
    peak_joint = jnp.maximum(peak_former, peak_latter)
    scale_former = jnp.exp(peak_former - peak_joint)
    scale_latter = jnp.exp(peak_latter - peak_joint)
    head_width = summed_former.shape[-1] // peak_joint.shape[-1]
    total_joint = total_former * scale_former + total_latter * scale_latter
    summed_joint = summed_former * jnp.repeat(
        scale_former, head_width, axis=-1
    ) + summed_latter * jnp.repeat(scale_latter, head_width, axis=-1)
    return (peak_joint, total_joint, summed_joint)


def local_parts(query_heads, key_heads, value_heads, logit_bias):
    scores = (
        jnp.einsum("srhd,jhd->srhj", query_heads, key_heads, preferred_element_type=jnp.float32)
        * (1.0 / math.sqrt(query_heads.shape[-1]))
        + logit_bias
    )
    maxima = jnp.max(scores, axis=-1)
    exponent = jnp.exp(scores - maxima[..., None])
    totals = jnp.sum(exponent, axis=-1)
    summed = jnp.einsum(
        "srhj,jhd->srhd",
        exponent.astype(jnp.bfloat16),
        value_heads,
        preferred_element_type=jnp.float32,
    )
    return (maxima, totals, summed.reshape(summed.shape[0], summed.shape[1], -1))


def finish(partials, gate_factor, out_proj, heads):
    maxima, totals, summed = combined_all(partials, "col", combine_parts)
    head_width = summed.shape[-1] // heads
    attended = (summed / jnp.repeat(totals, head_width, axis=-1) * gate_factor).astype(jnp.bfloat16)
    return flat_dot(attended, out_proj).astype(jnp.bfloat16)


def on_device(
    pair_block,
    query_single,
    key_single,
    query_chain,
    key_chain,
    query_mask,
    key_mask,
    timestep,
    time_table,
    norm_gain,
    left_proj,
    right_proj,
    outer_proj,
    bias_proj,
    chain_weight,
    query_proj,
    kv_proj,
    out_proj,
):
    step_count = time_table.shape[0]
    picked = jnp.arange(step_count, dtype=jnp.int32) == timestep[0]
    time_row = jnp.sum(
        jnp.where(picked[:, None], time_table.astype(jnp.float32), jnp.float32(0.0)), axis=0
    )
    query_norm = normalize(
        query_single.astype(jnp.float32) + query_mask[:, :, None].astype(jnp.float32) * time_row,
        norm_gain,
    )
    key_norm = normalize(
        key_single.astype(jnp.float32) + key_mask[:, None].astype(jnp.float32) * time_row, norm_gain
    )
    query_part = flat_dot(query_norm, query_proj).astype(jnp.bfloat16)
    query_gate = lax.all_gather(query_part, "col", axis=2, tiled=True)
    half_projected = jnp.dot(key_norm, kv_proj, preferred_element_type=jnp.float32).astype(
        jnp.bfloat16
    )
    keys_values = lax.all_gather(half_projected, "row", axis=1, tiled=True)
    rank = left_proj.shape[1]
    channels = outer_proj.shape[1]
    left_factor = flat_dot(query_norm, left_proj)
    right_factor = jnp.dot(key_norm, right_proj, preferred_element_type=jnp.float32)
    mixer = jnp.einsum(
        "sra,abc->srbc",
        left_factor,
        outer_proj.astype(jnp.float32).reshape(rank, rank, channels),
        precision=HIGHEST,
    )
    new_pair = pair_block + jnp.einsum("jb,srbc->srjc", right_factor, mixer, precision=HIGHEST)
    differ = (query_chain[:, :, None] != key_chain[None, None, :]).astype(jnp.float32)
    logit_bias = (
        jnp.einsum("srjc,ch->srhj", new_pair, bias_proj, precision=HIGHEST)
        + chain_weight[None, None, :, None] * differ[:, :, None, :]
    )
    heads = chain_weight.shape[0]
    model_width = query_norm.shape[-1]
    head_size = model_width // heads
    slab_count = query_gate.shape[0]
    slab_rows = query_gate.shape[1]
    key_count = keys_values.shape[0]
    query_heads = query_gate[:, :, :model_width].reshape(slab_count, slab_rows, heads, head_size)
    gate_factor = jax.nn.sigmoid(query_gate[:, :, model_width:].astype(jnp.float32))
    key_heads = keys_values[:, :model_width].reshape(key_count, heads, head_size)
    value_heads = keys_values[:, model_width:].reshape(key_count, heads, head_size)
    single_update = finish(
        local_parts(query_heads, key_heads, value_heads, logit_bias), gate_factor, out_proj, heads
    )
    return (new_pair, single_update)


def solution(mesh):
    return jax.shard_map(
        on_device,
        mesh=mesh,
        in_specs=(
            P("grp", "row", "col", None),
            P("grp", "row", None),
            P(("grp", "col"), None),
            P("grp", "row"),
            P(("grp", "col")),
            P("grp", "row"),
            P(("grp", "col")),
            P("grp"),
            P(),
            P(),
            P(),
            P(),
            P(),
            P(),
            P(),
            P(None, "col"),
            P(None, "row"),
            P(),
        ),
        out_specs=(P("grp", "row", "col", None), P("grp", "row", None)),
        check_vma=False,
    )
```

profile of v0, /device:TPU:0, one launch (start us, length us, event | category | flops | bytes accessed | tf_op | source)
XLA Modules:
  0.0 153.0 jit_solution(936284778297747066)
XLA Ops:
  1.5 0.7 convert_element_type.50
  2.1 0.7 convert_element_type.54
  2.8 1.0 select_reduce_fusion
  3.8 1.1 fusion.13
  5.0 1.2 multiply_reduce_fusion
  6.2 0.9 fusion.23
  7.1 0.9 multiply_reduce_fusion.1
  8.0 1.2 convolution_convert_fusion.1
  9.2 1.0 convolution_bitcast_fusion.4
  10.2 0.9 convolution_bitcast_fusion.3
  11.2 0.8 fusion.25
  12.1 0.4 convolution_convert_fusion
  12.6 2.2 %all_gather.21 = bf16[144,1536]{1,0:T(8,128)(2,1)S(1)} all-gather(bf16[144,768]{1,0:T(8,128)(2,1)S(1)} %convolution_convert_fusion), channel_id=1, replica_groups=mesh['grp'=2,'col'=8,'row'=2] {'row'}, dimensions={1}, use_global_device_ids=true | all-gather | bytes 663552 | tf_op jit(solution)/shard_map/all_gather | solution.py:112
  14.8 0.9 copy.40
  15.9 33.9 %all_gather.22 = bf16[2,8,1536]{1,0,2:T(2,128)(2,1)S(1)} all-gather(bf16[2,8,192]{1,0,2:T(2,128)(2,1)S(1)} %copy.34), channel_id=1, replica_groups=mesh['grp'=2,'col'=8,'row'=2] {'col'}, dimensions={2}, use_global_device_ids=true | all-gather | bytes 55296 | tf_op jit(solution)/shard_map/all_gather | solution.py:108
  49.8 0.5 fusion.33
  50.4 0.9 copy.36
  51.6 2.0 %fusion.3 = f32[2,8,144,128]{3,2,1,0:T(8,128)S(1)} fusion(f32[2,8,144,128]{3,2,1,0:T(8,128)S(1)} %copy-done.2, f32[144,8,1,1]{0,1,3,2:T(8,128)} %convolution_bitcast_fusion.3, f32[2,8,8,128]{3,1,2,0:T(8,128)} %fusion.25), kind=kOutput, calls=%fused_computation.9 | convolution fusion | flops 28606464 | bytes 2429440 | tf_op jit(solution)/shard_map/jb,srbc->srjc/dot_general | solution.py:123
  53.6 1.9 %fusion.29 = f32[2,8,144,12]{2,3,1,0:T(8,128)S(1)} fusion(f32[2,8,144,128]{3,2,1,0:T(8,128)S(1)} %fusion.3, f32[128,12]{0,1:T(8,128)S(1)} %copy-done.8), kind=kOutput, calls=%fused_computation.50 | convolution fusion | flops 42467328 | bytes 1296384 | tf_op jit(solution)/shard_map/srjc,ch->srhj/dot_general | solution.py:126
  56.7 30.5 %all-gather.1 = f32[16,8,12]{2,1,0:T(8,128)S(1)} all-gather(f32[2,8,12]{2,1,0:T(8,128)S(1)} %copy.39), channel_id=3, replica_groups=mesh['grp'=2,'col'=8,'row'=2] {'col'}, dimensions={0}, use_global_device_ids=true | all-gather | bytes 6912 | tf_op jit(solution)/shard_map/all_gather | solution.py:13
  87.2 30.5 %all-gather = f32[16,8,12]{2,1,0:T(8,128)S(1)} all-gather(f32[2,8,12]{2,1,0:T(8,128)S(1)} %copy.38), channel_id=2, replica_groups=mesh['grp'=2,'col'=8,'row'=2] {'col'}, dimensions={0}, use_global_device_ids=true | all-gather | bytes 6912 | tf_op jit(solution)/shard_map/all_gather | solution.py:13
  117.7 30.9 %all_gather.27 = f32[8,2,8,768]{3,2,1,0:T(8,128)S(1)} all-gather(f32[1,2,8,768]{3,2,1,0:T(8,128)S(1)} %all_gather_reshape.3), channel_id=1, replica_groups=mesh['grp'=2,'col'=8,'row'=2] {'col'}, dimensions={0}, use_global_device_ids=true | all-gather | bytes 442368 | tf_op jit(solution)/shard_map/all_gather | solution.py:13
  148.7 3.2 %while.19 = (s32[]{:T(128)}, f32[2,8,12]{2,1,0:T(8,128)S(1)}, f32[2,8,12]{2,1,0:T(8,128)S(1)}, f32[2,8,768]{2,1,0:T(8,128)S(1)}, f32[8,2,8,12]{3,2,1,0:T(8,128)S...) while((s32[]{:T(128)}, f32[2,8,12]{2,1,0:T(8,128)S(1)}, ...), condition=%wide.region_8.9_spmd, body=%wide.region_7.8_spmd.sunk | while | flops 38021 | bytes 548495 | solution.py:18
  152.1 0.9 fusion.9
  (92 shorter events, 4.8 us)
Async XLA Ops:
  0.6 11.5 %copy-start = (bf16[768,768]{1,0:T(8,128)(2,1)S(1)}, bf16[768,768]{1,0:T(8,128)(2,1)}, u32[]{:S(2)}) copy-start(bf16[768,768]{1,0:T(8,128)(2,1)} %param.36) | copy-start | bytes 3538948
  0.6 9.6 %copy-start.13 = (f32[768]{0:T(1024)S(1)}, f32[768]{0:T(1024)}, u32[]{:S(2)}) copy-start(f32[768]{0:T(1024)} %param.29) | copy-start | bytes 9220
  0.7 9.5 %copy-start.4 = (bf16[144,768]{1,0:T(8,128)(2,1)S(1)}, bf16[144,768]{1,0:T(8,128)(2,1)}, u32[]{:S(2)}) copy-start(bf16[144,768]{1,0:T(8,128)(2,1)} %param.22) | copy-start | bytes 663556
  0.7 10.5 %copy-start.7 = (bf16[64,128]{1,0:T(8,128)(2,1)S(1)}, bf16[64,128]{1,0:T(8,128)(2,1)}, u32[]{:S(2)}) copy-start(bf16[64,128]{1,0:T(8,128)(2,1)} %param.32) | copy-start | bytes 49156
  0.7 9.5 %copy-start.12 = (bf16[768,8]{0,1:T(8,128)(2,1)S(1)}, bf16[768,8]{0,1:T(8,128)(2,1)}, u32[]{:S(2)}) copy-start(bf16[768,8]{0,1:T(8,128)(2,1)} %param.31) | copy-start | bytes 36868
  0.7 10.4 %copy-start.9 = (s32[144]{0:T(256)S(1)}, s32[144]{0:T(256)}, u32[]{:S(2)}) copy-start(s32[144]{0:T(256)} %param.24) | copy-start | bytes 1732
  0.7 10.4 %copy-start.10 = (s32[2,8]{1,0:T(2,128)S(1)}, s32[2,8]{1,0:T(2,128)}, u32[]{:S(2)}) copy-start(s32[2,8]{1,0:T(2,128)} %param.23) | copy-start | bytes 196
  49.8 1.7 %copy-start.2 = (f32[2,8,144,128]{3,2,1,0:T(8,128)S(1)}, f32[2,8,144,128]{3,2,1,0:T(8,128)}, u32[]{:S(2)}) copy-start(f32[2,8,144,128]{3,2,1,0:T(8,128)} %param.20) | copy-start | bytes 3538948
  51.6 2.0 %copy-start.8 = (f32[128,12]{0,1:T(8,128)S(1)}, f32[128,12]{0,1:T(8,128)}, u32[]{:S(2)}) copy-start(f32[128,12]{0,1:T(8,128)} %param.33) | copy-start | bytes 18436
  53.6 2.6 %copy-start.1 = (f32[2,8,144,128]{3,2,1,0:T(8,128)}, f32[2,8,144,128]{3,2,1,0:T(8,128)S(1)}, u32[]{:S(2)}) copy-start(f32[2,8,144,128]{3,2,1,0:T(8,128)S(1)} %fusion.3) | copy-start | bytes 3538948
  53.6 2.0 %copy-start.6 = (bf16[2,8,12,64]{3,1,0,2:T(8,128)(2,1)S(1)}, bf16[2,8,12,64]{3,1,0,2:T(8,128)(2,1)}, u32[]{:S(2)}) copy-start(bf16[2,8,12,64]{3,1,0,2:T(8,128)(2,1)} %copy.36) | copy-start | bytes 73732
  53.6 2.0 %copy-start.11 = (f32[12]{0:T(128)S(1)}, f32[12]{0:T(128)}, u32[]{:S(2)}) copy-start(f32[12]{0:T(128)} %param.34) | copy-start | bytes 148
  53.6 2.2 %copy-start.5 = (bf16[144,768]{0,1:T(8,128)(2,1)S(1)}, bf16[144,768]{0,1:T(8,128)(2,1)}, u32[]{:S(2)}) copy-start(bf16[144,768]{0,1:T(8,128)(2,1)} %copy.40) | copy-start | bytes 663556
  148.7 3.4 %copy-start.3 = (bf16[768,768]{1,0:T(8,128)(2,1)S(1)}, bf16[768,768]{1,0:T(8,128)(2,1)}, u32[]{:S(2)}) copy-start(bf16[768,768]{1,0:T(8,128)(2,1)} %param.37) | copy-start | bytes 3538948
where the time goes:
time: 154 us; the launch traced here: 153 us
  blocking collectives  128 us (83%)
  matrix products  9.65 us (6%)
  other arithmetic  7.11 us (5%)
  local copies, waits for them, and re-layouts  5.97 us (4%)
  between operations  1.64 us (1%)
    all_gather x3, blocking collectives, combined_all(): gathered = jax.tree.map(lambda a: lax.all_gather(a, axis), part)  92 us
    all_gather x1, blocking collectives, on_device(): query_gate = lax.all_gather(query_part, 'col', axis=2, tiled=True)  33.9 us
    dot_general x3, matrix products, flat_dot(): product = jnp.dot(flat_left, right, preferred_element_type=jnp.float32)  3.08 us

commit v1 on v0

v1 whole, which is shorter than its diff:
```python
import functools
import math

import jax
import jax.numpy as jnp
from jax import lax
from jax.experimental import pallas as pl
from jax.experimental.pallas import tpu as pltpu
from jax.sharding import PartitionSpec as P

EPSILON = 1e-05
HIGHEST = lax.Precision.HIGHEST
LANES = 128
VMEM = pl.BlockSpec(memory_space=pltpu.VMEM)
SMEM = pl.BlockSpec(memory_space=pltpu.SMEM)
F32 = jnp.float32
BF16 = jnp.bfloat16


def dot(left, right, precision=None):
    return jnp.dot(left, right, preferred_element_type=F32, precision=precision)


def dot_nt(left, right):
    return lax.dot_general(left, right, (((1,), (1,)), ((), ())), preferred_element_type=F32)


def dot_tn(left, right):
    return lax.dot_general(left, right, (((0,), (0,)), ((), ())), preferred_element_type=F32)


def iota(shape, axis):
    return lax.broadcasted_iota(jnp.int32, shape, axis)


def split(value):
    high = value.astype(BF16)
    return high, (value - high.astype(F32)).astype(BF16)


def pick_time(step_ref, table_ref):
    table = table_ref[...].astype(F32)
    return jnp.sum(jnp.where(iota(table.shape, 0) == step_ref[0], table, 0.0), axis=0, keepdims=True)


def normalized(features, gain):
    average = jnp.mean(features, axis=-1, keepdims=True)
    centred = features - average
    spread = jnp.mean(centred * centred, axis=-1, keepdims=True)
    return (centred * lax.rsqrt(spread + EPSILON) * gain).astype(BF16)


def column_of(row):
    count = row.shape[1]
    square = (count, count)
    return jnp.sum(jnp.where(iota(square, 0) == iota(square, 1), row, 0), axis=1, keepdims=True)


def query_kernel(step, mask, single, table, gain, proj, part_out, norm_out):
    slabs, rows, width = single.shape
    count = slabs * rows
    features = single[...].astype(F32).reshape(count, width)
    place = iota((count, 1), 0)
    kept = jnp.zeros((count, 1), F32)
    for index in range(count):
        kept = jnp.where(place == index, mask[index // rows, index % rows].astype(F32), kept)
    norm = normalized(features + kept * pick_time(step, table), gain[...])
    norm_out[...] = norm
    part_out[...] = dot(norm, proj[...]).astype(BF16)


def key_kernel(step, mask, single, table, gain, proj, right_proj, half_out, right_out):
    kept = column_of(mask[...].astype(F32))
    features = single[...].astype(F32) + kept * pick_time(step, table)
    norm = normalized(features, gain[...])
    half_out[...] = dot(norm, proj[...]).astype(BF16)
    right_out[...] = dot(norm, right_proj[...])


def pair_kernel(
    chain_weight,
    query_chain,
    query_norm,
    left_proj,
    outer_proj,
    bias_proj,
    right,
    key_chain,
    pair,
    pair_out,
    bias_out,
    mixer_scratch,
    spread_scratch,
    weight_scratch,
):
    step = pl.program_id(0)
    count = query_norm.shape[0]
    rank = left_proj.shape[1]
    channels, heads = bias_proj.shape
    key_count = right.shape[0]
    lanes = heads * count
    block = pair.shape[1]

    @pl.when(step == 0)
    def _():
        left = dot(query_norm[...], left_proj[...])
        repeated = (iota((rank, rank * rank), 1) // rank == iota((rank, rank * rank), 0)).astype(F32)
        wide = dot(left, repeated, HIGHEST)
        tall = jnp.broadcast_to(wide[:, None, :], (count, rank, rank * rank))
        tall = tall.reshape(count * rank, rank * rank)
        spot = (count * rank, rank * rank)
        tall = jnp.where(iota(spot, 0) % rank == iota(spot, 1) % rank, tall, 0.0)
        mixer = dot(tall, outer_proj[...].astype(F32), HIGHEST).reshape(count, rank, channels)
        high, low = split(mixer)
        mixer_scratch[:, :rank, :] = high.astype(F32)
        mixer_scratch[:, rank : 2 * rank, :] = high.astype(F32)
        mixer_scratch[:, 2 * rank :, :] = low.astype(F32)
        high, low = split(right[...])
        spread_scratch[...] = jnp.concatenate(
            [high.astype(F32), low.astype(F32), high.astype(F32)], axis=1
        )
        expand = (iota((heads, lanes), 1) // count == iota((heads, lanes), 0)).astype(F32)
        high, low = split(dot(bias_proj[...], expand, HIGHEST))
        weight_scratch[0] = high
        weight_scratch[1] = low
        lane = iota((1, lanes), 1)
        weights = jnp.zeros((1, lanes), F32)
        for head in range(heads):
            weights = jnp.where(lane // count == head, chain_weight[head], weights)
        chains = jnp.zeros((1, lanes), jnp.int32)
        rows = query_chain.shape[1]
        for index in range(count):
            chains = jnp.where(lane % count == index, query_chain[index // rows, index % rows], chains)
        own = column_of(key_chain[...])
        bias_out[...] = jnp.where(own != chains, weights, 0.0)

    lane = iota((key_count, lanes), 1)
    spread = spread_scratch[...].astype(BF16)
    total = bias_out[...]
    for index in range(block):
        mixer = mixer_scratch[step * block + index].astype(BF16)
        fresh = pair[0, index] + dot(spread, mixer)
        pair_out[0, index] = fresh
        high, low = split(fresh)
        here = dot(high, weight_scratch[0]) + dot(high, weight_scratch[1]) + dot(low, weight_scratch[0])
        total = jnp.where(lane % count == step * block + index, total + here, total)
    bias_out[...] = total


def attend_kernel(place, pieces, own, other, bias, part_out, heads, count, mask_count):
    col, row = place[0], place[1]
    model = own.shape[1]
    head = model // heads
    share = pieces[0].shape[1]
    if len(pieces) > 1:
        blocks = []
        for target in range(model // share):
            chosen = pieces[0][...]
            for index in range(1, len(pieces)):
                chosen = jnp.where((col ^ target) == index, pieces[index][...], chosen)
            blocks.append(chosen)
        query = jnp.concatenate(blocks, axis=1)
    else:
        query = pieces[0][:, :model]
    first, second = own[...], other[...]
    keys = jnp.where(row == 0, first, second)
    values = jnp.where(row == 0, second, first)
    lane = iota((count, model), 1)
    spread = jnp.concatenate(
        [jnp.where(lane // head == index, query, jnp.zeros_like(query)) for index in range(heads)],
        axis=0,
    )
    scores = dot_nt(keys, spread) * (1.0 / math.sqrt(head)) + bias[...]
    peak = jnp.max(scores, axis=0, keepdims=True)
    exponent = jnp.exp(scores - peak)
    total = jnp.sum(exponent, axis=0, keepdims=True)
    summed = dot_tn(exponent.astype(BF16), values)
    lanes = heads * count
    spot = (count, lanes)
    keep = iota(spot, 1) % count == iota(spot, 0)
    gather = (iota((lanes, LANES), 0) // count == iota((lanes, LANES), 1)).astype(F32)
    stats = jnp.concatenate([jnp.where(keep, peak, 0.0), jnp.where(keep, total, 0.0)], axis=0)
    stats = dot(stats, gather, HIGHEST)
    taken = jnp.zeros((count, model), F32)
    for index in range(heads):
        taken = jnp.where(lane // head == index, summed[index * count : (index + 1) * count], taken)
    part_out[:, :model] = taken
    part_out[:, model : model + LANES] = stats[:count]
    part_out[:, model + LANES :] = stats[count:]


def merged(parts, heads):
    model = parts[0].shape[1] - 2 * LANES
    count = parts[0].shape[0]
    peak = functools.reduce(jnp.maximum, [part[:, model : model + LANES] for part in parts])
    scales = [jnp.exp(part[:, model : model + LANES] - peak) for part in parts]
    total = sum(scale * part[:, model + LANES :] for scale, part in zip(scales, parts))
    widen = (iota((LANES, model), 1) // (model // heads) == iota((LANES, model), 0)).astype(F32)
    wide = dot(jnp.concatenate(scales + [total], axis=0), widen, HIGHEST)
    summed = sum(
        wide[index * count : (index + 1) * count] * part[:, :model] for index, part in enumerate(parts)
    )
    return summed, peak, total, wide[len(parts) * count :]


def join_kernel(first, second, part_out, heads):
    summed, peak, total, _ = merged([first[...], second[...]], heads)
    model = summed.shape[1]
    part_out[:, :model] = summed
    part_out[:, model : model + LANES] = peak
    part_out[:, model + LANES :] = total


def finish_kernel(place, pieces, parts, out_proj, update_out, heads):
    col = place[0]
    model = out_proj.shape[0]
    share = pieces[0].shape[1]
    if len(pieces) > 1:
        blocks = []
        for target in range(model // share, 2 * model // share):
            chosen = pieces[0][...]
            for index in range(1, len(pieces)):
                chosen = jnp.where((col ^ target) == index, pieces[index][...], chosen)
            blocks.append(chosen)
        gate = jnp.concatenate(blocks, axis=1)
    else:
        gate = pieces[0][:, model:]
    values = []
    for part in parts:
        values += [part[...]] if len(part.shape) == 2 else [part[i] for i in range(part.shape[0])]
    summed, _, _, total = merged(values, heads)
    attended = (summed / total * jax.nn.sigmoid(gate.astype(F32))).astype(BF16)
    update_out[...] = dot(attended, out_proj[...]).astype(BF16)


def exchanged(value, axis, flip):
    size = lax.axis_size(axis)
    return lax.ppermute(value, axis, [(index, index ^ flip) for index in range(size)])


def on_device(
    pair_block,
    query_single,
    key_single,
    query_chain,
    key_chain,
    query_mask,
    key_mask,
    timestep,
    time_table,
    norm_gain,
    left_proj,
    right_proj,
    outer_proj,
    bias_proj,
    chain_weight,
    query_proj,
    kv_proj,
    out_proj,
):
    slabs, rows, model = query_single.shape
    count = slabs * rows
    key_count = key_single.shape[0]
    heads = chain_weight.shape[0]
    channels = pair_block.shape[-1]
    rank = left_proj.shape[1]
    lanes = heads * count
    cols = lax.axis_size("col")
    gain = norm_gain.reshape(1, model)
    place = jnp.stack([lax.axis_index("col"), lax.axis_index("row")]).astype(jnp.int32)

    query_part, query_norm = pl.pallas_call(
        query_kernel,
        out_shape=(
            jax.ShapeDtypeStruct((count, query_proj.shape[1]), BF16),
            jax.ShapeDtypeStruct((count, model), BF16),
        ),
        in_specs=[SMEM, SMEM] + [VMEM] * 4,
        out_specs=(VMEM, VMEM),
        name="query",
    )(timestep, query_mask, query_single, time_table, gain, query_proj)

    half, right = pl.pallas_call(
        key_kernel,
        out_shape=(
            jax.ShapeDtypeStruct((key_count, kv_proj.shape[1]), BF16),
            jax.ShapeDtypeStruct((key_count, rank), F32),
        ),
        in_specs=[SMEM] + [VMEM] * 6,
        out_specs=(VMEM, VMEM),
        name="keys",
    )(
        timestep,
        key_mask.reshape(1, key_count),
        key_single,
        time_table,
        gain,
        kv_proj,
        right_proj,
    )
    other = exchanged(half, "row", 1)

    direct = cols == 8
    if direct:
        near = exchanged(query_part, "col", 1)
        both = jnp.stack([query_part, near])
        pieces = [query_part, near]
        for flip in (2, 4, 6):
            far = exchanged(both, "col", flip)
            pieces += [far[0], far[1]]
    else:
        pieces = [lax.all_gather(query_part, "col", axis=1, tiled=True)]

    steps = 4
    block = count // steps
    per_slab = rows // block
    whole = lambda *shape: pl.BlockSpec(shape, lambda i: (0,) * len(shape))
    pair_spec = pl.BlockSpec(
        (1, block, key_count, channels), lambda i: (i // per_slab, i % per_slab, 0, 0)
    )
    new_pair, bias = pl.pallas_call(
        pair_kernel,
        grid=(steps,),
        out_shape=(
            jax.ShapeDtypeStruct(pair_block.shape, F32),
            jax.ShapeDtypeStruct((key_count, lanes), F32),
        ),
        in_specs=[
            SMEM,
            SMEM,
            whole(count, model),
            whole(model, rank),
            whole(rank * rank, channels),
            whole(channels, heads),
            whole(key_count, rank),
            whole(1, key_count),
            pair_spec,
        ],
        out_specs=(pair_spec, whole(key_count, lanes)),
        scratch_shapes=[
            pltpu.VMEM((count, 3 * rank, channels), F32),
            pltpu.VMEM((key_count, 3 * rank), F32),
            pltpu.VMEM((2, channels, lanes), BF16),
        ],
        name="pairs",
    )(
        chain_weight,
        query_chain,
        query_norm,
        left_proj,
        outer_proj,
        bias_proj,
        right,
        key_chain.reshape(1, key_count),
        pair_block,
    )

    part_shape = jax.ShapeDtypeStruct((count, model + 2 * LANES), F32)

    def attend_body(place, *refs):
        n = len(pieces)
        attend_kernel(place, refs[:n], *refs[n:], heads, count, None)

    part = pl.pallas_call(
        attend_body,
        out_shape=part_shape,
        in_specs=[SMEM] + [VMEM] * (len(pieces) + 3),
        out_specs=VMEM,
        name="attend",
    )(place, *pieces, half, other, bias)

    if direct:
        part = pl.pallas_call(
            functools.partial(join_kernel, heads=heads),
            out_shape=part_shape,
            in_specs=[VMEM, VMEM],
            out_specs=VMEM,
            name="join",
        )(part, exchanged(part, "col", 1))
        parts = [part] + [exchanged(part, "col", flip) for flip in (6, 4, 2)]
    else:
        parts = [lax.all_gather(part, "col")]

    def finish_body(place, *refs):
        n, k = len(pieces), len(parts)
        finish_kernel(place, refs[:n], refs[n : n + k], *refs[n + k :], heads)

    update = pl.pallas_call(
        finish_body,
        out_shape=jax.ShapeDtypeStruct((count, model), BF16),
        in_specs=[SMEM] + [VMEM] * (len(pieces) + len(parts) + 1),
        out_specs=VMEM,
        name="finish",
    )(place, *pieces, *parts, out_proj)
    return (new_pair, update.reshape(slabs, rows, model))


def solution(mesh):
    return jax.shard_map(
        on_device,
        mesh=mesh,
        in_specs=(
            P("grp", "row", "col", None),
            P("grp", "row", None),
            P(("grp", "col"), None),
            P("grp", "row"),
            P(("grp", "col")),
            P("grp", "row"),
            P(("grp", "col")),
            P("grp"),
            P(),
            P(),
            P(),
            P(),
            P(),
            P(),
            P(),
            P(None, "col"),
            P(None, "row"),
            P(),
        ),
        out_specs=(P("grp", "row", "col", None), P("grp", "row", None)),
        check_vma=False,
    )
```

time: 154 us -> 52.2 us (0.34)
  blocking collectives: 128 us -> 0 us
  Pallas kernels: 0 us -> 17.5 us
  starting transfers between devices: 0 us -> 12.4 us
  waiting for transfers between devices: 0 us -> 10.6 us
  matrix products: 9.65 us -> 0 us
  other arithmetic: 7.11 us -> 0.62 us
  local copies, waits for them, and re-layouts: 5.97 us -> 9.28 us
    all_gather x5 -> x0, blocking collectives: 128 us -> none  [the longest x3 92 us: combined_all(): gathered = jax.tree.map(lambda a: lax.all_gather(a, axis), part)]
    pallas_call x0 -> x6, Pallas kernels: none -> 17.5 us  [the longest x1 5.38 us: on_device(): pl.pallas_call(pair_kernel, grid=(steps,), out_shape=(jax.ShapeDtypeStruc...]
    ppermute x0 -> x9, starting transfers between devices: none -> 12.4 us  [exchanged(): lax.ppermute(value, axis, [(index, index ^ flip) for index in range(size)])]
    ppermute x0 -> x9, waiting for transfers between devices: none -> 10.6 us  [exchanged(): lax.ppermute(value, axis, [(index, index ^ flip) for index in range(size)])]
    dot_general x8 -> x0, matrix products: 9.11 us -> none  [the longest x3 3.08 us: flat_dot(): product = jnp.dot(flat_left, right, preferred_element_type=jnp.float32)]
    unnamed x29 -> x24, local copies, waits for them, and re-layouts: 0.35 us -> 6.18 us
    reduce_sum x6 -> x0, other arithmetic: 5.35 us -> none  [the longest x2 2.1 us: normalize(): spread = jnp.mean(centred * centred, axis=-1, keepdims=True)]
    squeeze x1 -> x3, local copies, waits for them, and re-layouts: 0.01 us -> 1.81 us  [on_device(): pieces += [far[0], far[1]]]
  transfers between devices with their start and end apart: 0 -> 9, of which waited for: 0 -> 5; matrix products, arithmetic and copies ran while one was open for 0% -> 9% of each run, Pallas kernels for 0% -> 16%
where the time goes in v1:
time: 52.2 us; the launch traced here: 51.8 us
  Pallas kernels  17.5 us (34%)
  starting transfers between devices  12.4 us (24%)
  waiting for transfers between devices  10.6 us (20%)
  local copies, waits for them, and re-layouts  9.28 us (18%)
  between operations  1.35 us (3%)
  other arithmetic  0.62 us (1%)
    ppermute x9, starting transfers between devices, exchanged(): lax.ppermute(value, axis, [(index, index ^ flip) for index in range(size)])  12.4 us
    ppermute x9, waiting for transfers between devices, exchanged(): lax.ppermute(value, axis, [(index, index ^ flip) for index in range(size)])  10.6 us
    unnamed x24, local copies, waits for them, and re-layouts  6.18 us
    pallas_call x1, Pallas kernels, on_device(): pl.pallas_call(pair_kernel, grid=(steps,), out_shape=(jax.ShapeDtypeStruc...  5.38 us
    pallas_call x1, Pallas kernels, on_device(): pl.pallas_call(key_kernel, out_shape=(jax.ShapeDtypeStruct((key_count, kv...  2.82 us
    pallas_call x1, Pallas kernels, on_device(): pl.pallas_call(finish_body, out_shape=jax.ShapeDtypeStruct((count, model)...  2.78 us
    pallas_call x1, Pallas kernels, on_device(): pl.pallas_call(attend_body, out_shape=part_shape, in_specs=[SMEM] + [VMEM...  2.67 us
    pallas_call x1, Pallas kernels, on_device(): pl.pallas_call(query_kernel, out_shape=(jax.ShapeDtypeStruct((count, quer...  2.04 us
  transfers between devices with their start and end apart: 9, of which 5 were waited for; matrix products, arithmetic and copies ran while one was open for 9% of the time, Pallas kernels for 16%

profile of v1, /device:TPU:0, one launch (start us, length us, event | category | flops | bytes accessed | tf_op | source)
XLA Modules:
  0.0 51.8 jit_solution(3235702938128696055)
XLA Ops:
  1.3 1.3 %reshape.16.gain = f32[1,768]{1,0:T(1,128)} reshape(f32[768]{0:T(1024)} %param.27) | data formatting | bytes 6144 | tf_op jit(solution)/shard_map/reshape | solution.py:269
  2.6 1.9 %copy.20.proj = bf16[768,192]{1,0:T(8,128)(2,1)} copy(bf16[768,192]{0,1:T(8,128)(2,1)} %param.33) | data formatting | bytes 589824 | tf_op args[15]
  4.5 2.0 %query.1 = (bf16[16,192]{1,0:T(8,128)(2,1)}, bf16[16,768]{1,0:T(8,128)(2,1)}) custom-call(s32[1]{0:T(128)S(6)} %copy.24.step, s32[2,8]{1,0:T(2,128)} %mask.1, bf16[2,8,768]{2,1,0:T(8,128)(2,1)} %single.2, bf16[50,768]{1,0:T(8,128)(2,1)} %table.3, f32[1,768]{1,0:T(1,128)} %reshape.16.gain, bf16[768,192]{1,0:T(8,128)(2,1)} %copy.20.proj), custom_call_target="tpu_custom_call" | custom-call | tf_op jit(solution)/shard_map/query/pallas_call | solution.py:272
  6.5 3.0 %collective-permute-start = (bf16[16,192]{1,0:T(8,128)(2,1)}, bf16[16,192]{1,0:T(8,128)(2,1)S(1)}, u32[]{:S(2)}, u32[]{:S(2)}) collective-permute-start(bf16[16,192]{1,0:T(8,128)(2,1)} %get-tuple-element.11.refs_0_), channel_id=1, source_target_pairs={{0,2},{2,0},{4,6},{6,4},{8,10},{10,8},{12,14},{14,12},{1,3},{3,1},... | collective-permute-start | bytes 18440 | tf_op jit(solution)/shard_map/ppermute | solution.py:238
  9.5 0.8 %copy.21.right_proj = bf16[768,8]{1,0:T(8,128)(2,1)} copy(bf16[768,8]{0,1:T(8,128)(2,1)S(1)} %copy-done.7) | data formatting | bytes 24576 | tf_op args[11]
  10.3 2.8 %keys.1 = (bf16[144,768]{1,0:T(8,128)(2,1)}, f32[144,8]{1,0:T(8,128)}) custom-call(s32[1]{0:T(128)S(6)} %copy.24.step, s32[1,144]{1,0:T(1,128)} %bitcast.22, bf16[144,768]{1,0:T(8,128)(2,1)} %single.3, bf16[50,768]{1,0:T(8,128)(2,1)} %table.3, f32[1,768]{1,0:T(1,128)} %reshape.16.gain, bf16[768,768]{1,0:T(8,128)(2,1)} %proj.2, bf16[768,8]{1,0:T(8,128)(2,1)} %copy.21.right_proj), custom_call_target="tpu_custom_call" | custom-call | tf_op jit(solution)/shard_map/keys/pallas_call | solution.py:283
  13.2 1.6 %collective-permute-start.1 = (bf16[2,16,192]{2,1,0:T(8,128)(2,1)S(1)}, bf16[2,16,192]{2,1,0:T(8,128)(2,1)S(1)}, u32[]{:S(2)}, u32[]{:S(2)}) collective-permute-start(bf16[2,16,192]{2,1,0:T(8,128)(2,1)S(1)} %pad_maximum_fusion), channel_id=1, source_target_pairs={{0,4},{2,6},{4,0},{6,2},{8,12},{10,14},{12,8},{14,10},{1,5},{3,7},... | collective-permute-start | bytes 36872 | tf_op jit(solution)/shard_map/ppermute | solution.py:238
  14.9 0.6 %pad_add_fusion.place = s32[2]{0:T(128)} fusion(s32[1]{0:T(128)} %bitcast.3, s32[1]{0:T(128)} %bitcast.2), kind=kLoop, calls=%fused_computation.7 | loop fusion | flops 2 | bytes 16 | tf_op jit(solution)/shard_map/stack | solution.py:270
  15.5 0.8 %copy.22.left_proj = bf16[768,8]{1,0:T(8,128)(2,1)} copy(bf16[768,8]{0,1:T(8,128)(2,1)S(1)} %copy-done.8) | data formatting | bytes 24576 | tf_op args[10]
  16.3 0.7 %copy.23.bias_proj = f32[128,12]{1,0:T(8,128)} copy(f32[128,12]{0,1:T(8,128)S(1)} %copy-done.9) | data formatting | bytes 12288 | tf_op args[13]
  17.0 5.4 %pairs.1 = (f32[2,8,144,128]{3,2,1,0:T(8,128)}, f32[144,192]{1,0:T(8,128)}) custom-call(f32[12]{0:T(128)} %chain_weight.1, s32[2,8]{1,0:T(2,128)} %query_chain.1, bf16[16,768]{1,0:T(8,128)(2,1)} %get-tuple-element.8.query_norm, bf16[768,8]{1,0:T(8,128)(2,1)} %copy.22.left_proj, bf16[64,128]{1,0:T(8,128)(2,1)} %outer_proj.1, f32[128,12]{1,0:T(8,128)} %copy.23.bias_proj, ...), custom_call_target="tpu_custom_call" | custom-call | tf_op jit(solution)/shard_map/pairs/pallas_call | solution.py:321
  22.4 2.6 %collective-permute-start.2 = (bf16[2,16,192]{2,1,0:T(8,128)(2,1)S(1)}, bf16[2,16,192]{2,1,0:T(8,128)(2,1)S(1)}, u32[]{:S(2)}, u32[]{:S(2)}) collective-permute-start(bf16[2,16,192]{2,1,0:T(8,128)(2,1)S(1)} %pad_maximum_fusion), channel_id=1, source_target_pairs={{0,8},{2,10},{4,12},{6,14},{8,0},{10,2},{12,4},{14,6},{1,9},{3,11}... | collective-permute-start | bytes 36872 | tf_op jit(solution)/shard_map/ppermute | solution.py:238
  25.8 1.3 %collective-permute-done.2 = bf16[2,16,192]{2,1,0:T(8,128)(2,1)S(1)} collective-permute-done((bf16[2,16,192]{2,1,0:T(8,128)(2,1)S(1)}, bf16[2,16,192]{2,1,0:T(8,128)(2,1)S(1)}, u32[]{:S(2)}, u32[]{:S(2)}) %collective-permute-start.2) | collective-permute-done | bytes 12320 | tf_op jit(solution)/shard_map/ppermute | solution.py:238
  27.7 2.8 %collective-permute-done.3 = bf16[2,16,192]{2,1,0:T(8,128)(2,1)S(1)} collective-permute-done((bf16[2,16,192]{2,1,0:T(8,128)(2,1)S(1)}, bf16[2,16,192]{2,1,0:T(8,128)(2,1)S(1)}, u32[]{:S(2)}, u32[]{:S(2)}) %collective-permute-start.3) | collective-permute-done | bytes 12320 | tf_op jit(solution)/shard_map/ppermute | solution.py:238
  31.1 0.7 %copy-done = bf16[144,768]{1,0:T(8,128)(2,1)} copy-done((bf16[144,768]{1,0:T(8,128)(2,1)}, bf16[144,768]{1,0:T(8,128)(2,1)S(1)}, u32[]{:S(2)}) %copy-start) | copy-done | bytes 221208
  31.8 2.7 %attend.1.first = f32[16,1024]{1,0:T(8,128)} custom-call(s32[2]{0:T(128)} %pad_add_fusion.place, bf16[16,192]{1,0:T(8,128)(2,1)} %get-tuple-element.11.refs_0_, bf16[16,192]{1,0:T(8,128)(2,1)} %copy-done.2, bf16[16,192]{1,0:T(8,128)(2,1)} %get-tuple-element.19.refs_2_, bf16[16,192]{1,0:T(8,128)(2,1)} %get-tuple-element.18.refs_3_, ...), custom_call_target="tpu_custom_call" | custom-call | tf_op jit(solution)/shard_map/attend/pallas_call | solution.py:364
  35.0 3.9 %collective-permute-done.5.second = f32[16,1024]{1,0:T(8,128)S(1)} collective-permute-done((f32[16,1024]{1,0:T(8,128)}, f32[16,1024]{1,0:T(8,128)S(1)}, u32[]{:S(2)}, u32[]{:S(2)}) %collective-permute-start.5) | collective-permute-done | bytes 65568 | tf_op jit(solution)/shard_map/ppermute | solution.py:238
  38.9 0.6 %copy-done.6 = f32[16,1024]{1,0:T(8,128)} copy-done((f32[16,1024]{1,0:T(8,128)}, f32[16,1024]{1,0:T(8,128)S(1)}, u32[]{:S(2)}) %copy-start.6) | copy-done | bytes 65560
  39.6 1.8 %join.1.refs_8_ = f32[16,1024]{1,0:T(8,128)} custom-call(f32[16,1024]{1,0:T(8,128)} %attend.1.first, f32[16,1024]{1,0:T(8,128)} %copy-done.6), custom_call_target="tpu_custom_call" | custom-call | tf_op jit(solution)/shard_map/join/pallas_call | solution.py:373
  41.6 4.2 %collective-permute-start.8 = (f32[16,1024]{1,0:T(8,128)}, f32[16,1024]{1,0:T(8,128)S(1)}, u32[]{:S(2)}, u32[]{:S(2)}) collective-permute-start(f32[16,1024]{1,0:T(8,128)} %join.1.refs_8_), channel_id=1, source_target_pairs={{0,4},{2,6},{4,0},{6,2},{8,12},{10,14},{12,8},{14,10},{1,5},{3,7},... | collective-permute-start | bytes 196616 | tf_op jit(solution)/shard_map/ppermute | solution.py:238
  45.7 1.9 %collective-permute-done.6.refs_9_ = f32[16,1024]{1,0:T(8,128)S(1)} collective-permute-done((f32[16,1024]{1,0:T(8,128)}, f32[16,1024]{1,0:T(8,128)S(1)}, u32[]{:S(2)}, u32[]{:S(2)}) %collective-permute-start.6) | collective-permute-done | bytes 65568 | tf_op jit(solution)/shard_map/ppermute | solution.py:238
  47.7 0.7 %collective-permute-done.8.refs_11_ = f32[16,1024]{1,0:T(8,128)S(1)} collective-permute-done((f32[16,1024]{1,0:T(8,128)}, f32[16,1024]{1,0:T(8,128)S(1)}, u32[]{:S(2)}, u32[]{:S(2)}) %collective-permute-start.8) | collective-permute-done | bytes 65568 | tf_op jit(solution)/shard_map/ppermute | solution.py:238
  48.4 0.6 %copy-done.5 = f32[16,1024]{1,0:T(8,128)} copy-done((f32[16,1024]{1,0:T(8,128)}, f32[16,1024]{1,0:T(8,128)S(1)}, u32[]{:S(2)}) %copy-start.5) | copy-done | bytes 65560
  49.0 2.8 %finish.1 = bf16[16,768]{1,0:T(8,128)(2,1)} custom-call(s32[2]{0:T(128)} %pad_add_fusion.place, bf16[16,192]{1,0:T(8,128)(2,1)} %get-tuple-element.11.refs_0_, bf16[16,192]{1,0:T(8,128)(2,1)} %copy-done.2, bf16[16,192]{1,0:T(8,128)(2,1)} %get-tuple-element.19.refs_2_, bf16[16,192]{1,0:T(8,128)(2,1)} %get-tuple-element.18.refs_3_, ...), custom_call_target="tpu_custom_call" | custom-call | tf_op jit(solution)/shard_map/finish/pallas_call | solution.py:388
  (30 shorter events, 2.9 us)
Async XLA Ops:
  0.6 8.9 %copy-start.7 = (bf16[768,8]{0,1:T(8,128)(2,1)S(1)}, bf16[768,8]{0,1:T(8,128)(2,1)}, u32[]{:S(2)}) copy-start(bf16[768,8]{0,1:T(8,128)(2,1)} %param.29) | copy-start | bytes 36868
  4.5 11.0 %copy-start.8 = (bf16[768,8]{0,1:T(8,128)(2,1)S(1)}, bf16[768,8]{0,1:T(8,128)(2,1)}, u32[]{:S(2)}) copy-start(bf16[768,8]{0,1:T(8,128)(2,1)} %param.28) | copy-start | bytes 36868
  6.5 6.7 %copy-start.1 = (bf16[16,192]{1,0:T(8,128)(2,1)S(1)}, bf16[16,192]{1,0:T(8,128)(2,1)}, u32[]{:S(2)}) copy-start(bf16[16,192]{1,0:T(8,128)(2,1)} %get-tuple-element.11.refs_0_) | copy-start | bytes 18436
  6.5 9.8 %copy-start.9 = (f32[128,12]{0,1:T(8,128)S(1)}, f32[128,12]{0,1:T(8,128)}, u32[]{:S(2)}) copy-start(f32[128,12]{0,1:T(8,128)} %param.31) | copy-start | bytes 18436
  6.5 6.7 %collective-permute-start = (bf16[16,192]{1,0:T(8,128)(2,1)}, bf16[16,192]{1,0:T(8,128)(2,1)S(1)}, u32[]{:S(2)}, u32[]{:S(2)}) collective-permute-start(bf16[16,192]{1,0:T(8,128)(2,1)} %get-tuple-element.11.refs_0_), channel_id=1, source_target_pairs={{0,2},{2,0},{4,6},{6,4},{8,10},{10,8},{12,14},{14,12},{1,3},{3,1},... | collective-permute-start | bytes 18440 | tf_op jit(solution)/shard_map/ppermute | solution.py:238
  13.2 17.9 %collective-permute-start.4 = (bf16[144,768]{1,0:T(8,128)(2,1)}, bf16[144,768]{1,0:T(8,128)(2,1)S(1)}, u32[]{:S(2)}, u32[]{:S(2)}) collective-permute-start(bf16[144,768]{1,0:T(8,128)(2,1)} %get-tuple-element.12.refs_8_), channel_id=1, source_target_pairs={{0,1},{1,0},{2,3},{3,2},{4,5},{5,4},{6,7},{7,6},{8,9},{9,8},{10,11... | collective-permute-start | bytes 663560 | tf_op jit(solution)/shard_map/ppermute | solution.py:238
  13.2 17.9 %copy-start.2 = (bf16[16,192]{1,0:T(8,128)(2,1)}, bf16[16,192]{1,0:T(8,128)(2,1)S(1)}, u32[]{:S(2)}) copy-start(bf16[16,192]{1,0:T(8,128)(2,1)S(1)} %collective-permute-done.refs_1_) | copy-start | bytes 18436
  13.2 12.0 %collective-permute-start.1 = (bf16[2,16,192]{2,1,0:T(8,128)(2,1)S(1)}, bf16[2,16,192]{2,1,0:T(8,128)(2,1)S(1)}, u32[]{:S(2)}, u32[]{:S(2)}) collective-permute-start(bf16[2,16,192]{2,1,0:T(8,128)(2,1)S(1)} %pad_maximum_fusion), channel_id=1, source_target_pairs={{0,4},{2,6},{4,0},{6,2},{8,12},{10,14},{12,8},{14,10},{1,5},{3,7},... | collective-permute-start | bytes 36872 | tf_op jit(solution)/shard_map/ppermute | solution.py:238
  22.4 4.7 %collective-permute-start.2 = (bf16[2,16,192]{2,1,0:T(8,128)(2,1)S(1)}, bf16[2,16,192]{2,1,0:T(8,128)(2,1)S(1)}, u32[]{:S(2)}, u32[]{:S(2)}) collective-permute-start(bf16[2,16,192]{2,1,0:T(8,128)(2,1)S(1)} %pad_maximum_fusion), channel_id=1, source_target_pairs={{0,8},{2,10},{4,12},{6,14},{8,0},{10,2},{12,4},{14,6},{1,9},{3,11}... | collective-permute-start | bytes 36872 | tf_op jit(solution)/shard_map/ppermute | solution.py:238
  25.0 5.5 %collective-permute-start.3 = (bf16[2,16,192]{2,1,0:T(8,128)(2,1)S(1)}, bf16[2,16,192]{2,1,0:T(8,128)(2,1)S(1)}, u32[]{:S(2)}, u32[]{:S(2)}) collective-permute-start(bf16[2,16,192]{2,1,0:T(8,128)(2,1)S(1)} %pad_maximum_fusion), channel_id=1, source_target_pairs={{0,12},{2,14},{4,8},{6,10},{8,4},{10,6},{12,0},{14,2},{1,13},{3,15... | collective-permute-start | bytes 36872 | tf_op jit(solution)/shard_map/ppermute | solution.py:238
  31.1 0.7 %copy-start = (bf16[144,768]{1,0:T(8,128)(2,1)}, bf16[144,768]{1,0:T(8,128)(2,1)S(1)}, u32[]{:S(2)}) copy-start(bf16[144,768]{1,0:T(8,128)(2,1)S(1)} %collective-permute-done.4.refs_9_) | copy-start | bytes 663556
  34.5 4.5 %collective-permute-start.5 = (f32[16,1024]{1,0:T(8,128)}, f32[16,1024]{1,0:T(8,128)S(1)}, u32[]{:S(2)}, u32[]{:S(2)}) collective-permute-start(f32[16,1024]{1,0:T(8,128)} %attend.1.first), channel_id=1, source_target_pairs={{0,2},{2,0},{4,6},{6,4},{8,10},{10,8},{12,14},{14,12},{1,3},{3,1},... | collective-permute-start | bytes 196616 | tf_op jit(solution)/shard_map/ppermute | solution.py:238
  38.9 0.6 %copy-start.6 = (f32[16,1024]{1,0:T(8,128)}, f32[16,1024]{1,0:T(8,128)S(1)}, u32[]{:S(2)}) copy-start(f32[16,1024]{1,0:T(8,128)S(1)} %collective-permute-done.5.second) | copy-start | bytes 196612
  41.3 6.3 %collective-permute-start.6 = (f32[16,1024]{1,0:T(8,128)}, f32[16,1024]{1,0:T(8,128)S(1)}, u32[]{:S(2)}, u32[]{:S(2)}) collective-permute-start(f32[16,1024]{1,0:T(8,128)} %join.1.refs_8_), channel_id=1, source_target_pairs={{0,12},{2,14},{4,8},{6,10},{8,4},{10,6},{12,0},{14,2},{1,13},{3,15... | collective-permute-start | bytes 196616 | tf_op jit(solution)/shard_map/ppermute | solution.py:238
  41.6 6.1 %collective-permute-start.7 = (f32[16,1024]{1,0:T(8,128)}, f32[16,1024]{1,0:T(8,128)S(1)}, u32[]{:S(2)}, u32[]{:S(2)}) collective-permute-start(f32[16,1024]{1,0:T(8,128)} %join.1.refs_8_), channel_id=1, source_target_pairs={{0,8},{2,10},{4,12},{6,14},{8,0},{10,2},{12,4},{14,6},{1,9},{3,11}... | collective-permute-start | bytes 196616 | tf_op jit(solution)/shard_map/ppermute | solution.py:238
  41.6 6.8 %collective-permute-start.8 = (f32[16,1024]{1,0:T(8,128)}, f32[16,1024]{1,0:T(8,128)S(1)}, u32[]{:S(2)}, u32[]{:S(2)}) collective-permute-start(f32[16,1024]{1,0:T(8,128)} %join.1.refs_8_), channel_id=1, source_target_pairs={{0,4},{2,6},{4,0},{6,2},{8,12},{10,14},{12,8},{14,10},{1,5},{3,7},... | collective-permute-start | bytes 196616 | tf_op jit(solution)/shard_map/ppermute | solution.py:238
  47.7 0.7 %copy-start.3 = (f32[16,1024]{1,0:T(8,128)}, f32[16,1024]{1,0:T(8,128)S(1)}, u32[]{:S(2)}) copy-start(f32[16,1024]{1,0:T(8,128)S(1)} %collective-permute-done.6.refs_9_) | copy-start | bytes 196612
  47.7 0.7 %copy-start.4 = (f32[16,1024]{1,0:T(8,128)}, f32[16,1024]{1,0:T(8,128)S(1)}, u32[]{:S(2)}) copy-start(f32[16,1024]{1,0:T(8,128)S(1)} %collective-permute-done.7.refs_10_) | copy-start | bytes 196612
  48.4 0.6 %copy-start.5 = (f32[16,1024]{1,0:T(8,128)}, f32[16,1024]{1,0:T(8,128)S(1)}, u32[]{:S(2)}) copy-start(f32[16,1024]{1,0:T(8,128)S(1)} %collective-permute-done.8.refs_11_) | copy-start | bytes 196612

commit v2 on v1

--- a/solution.py
+++ b/solution.py
@@ -12,7 +12,6 @@
 HIGHEST = lax.Precision.HIGHEST
 LANES = 128
 VMEM = pl.BlockSpec(memory_space=pltpu.VMEM)
-SMEM = pl.BlockSpec(memory_space=pltpu.SMEM)
 F32 = jnp.float32
 BF16 = jnp.bfloat16
 
@@ -25,8 +24,10 @@
     return lax.dot_general(left, right, (((1,), (1,)), ((), ())), preferred_element_type=F32)
 
 
-def dot_tn(left, right):
-    return lax.dot_general(left, right, (((0,), (0,)), ((), ())), preferred_element_type=F32)
+def dot_tn(left, right, precision=None):
+    return lax.dot_general(
+        left, right, (((0,), (0,)), ((), ())), preferred_element_type=F32, precision=precision
+    )
 
 
 def iota(shape, axis):
@@ -40,7 +41,8 @@
 
 def pick_time(step_ref, table_ref):
     table = table_ref[...].astype(F32)
-    return jnp.sum(jnp.where(iota(table.shape, 0) == step_ref[0], table, 0.0), axis=0, keepdims=True)
+    picked = iota(table.shape, 0) == step_ref[...]
+    return jnp.sum(jnp.where(picked, table, 0.0), axis=0, keepdims=True)
 
 
 def normalized(features, gain):
@@ -56,25 +58,26 @@
     return jnp.sum(jnp.where(iota(square, 0) == iota(square, 1), row, 0), axis=1, keepdims=True)
 
 
+def rows_column(table):
+    return jnp.concatenate([column_of(table[i : i + 1]) for i in range(table.shape[0])], axis=0)
+
+
 def query_kernel(step, mask, single, table, gain, proj, part_out, norm_out):
     slabs, rows, width = single.shape
     count = slabs * rows
     features = single[...].astype(F32).reshape(count, width)
-    place = iota((count, 1), 0)
-    kept = jnp.zeros((count, 1), F32)
-    for index in range(count):
-        kept = jnp.where(place == index, mask[index // rows, index % rows].astype(F32), kept)
-    norm = normalized(features + kept * pick_time(step, table), gain[...])
+    kept = rows_column(mask[...].astype(F32))
+    norm = normalized(features + kept * pick_time(step, table), gain[...].reshape(1, width))
     norm_out[...] = norm
-    part_out[...] = dot(norm, proj[...]).astype(BF16)
+    part_out[...] = dot_nt(norm, proj[...]).astype(BF16)
 
 
 def key_kernel(step, mask, single, table, gain, proj, right_proj, half_out, right_out):
     kept = column_of(mask[...].astype(F32))
     features = single[...].astype(F32) + kept * pick_time(step, table)
-    norm = normalized(features, gain[...])
+    norm = normalized(features, gain[...].reshape(1, features.shape[1]))
     half_out[...] = dot(norm, proj[...]).astype(BF16)
-    right_out[...] = dot(norm, right_proj[...])
+    right_out[...] = dot_nt(norm, right_proj[...])
 
 
 def pair_kernel(
@@ -95,15 +98,15 @@
 ):
     step = pl.program_id(0)
     count = query_norm.shape[0]
-    rank = left_proj.shape[1]
-    channels, heads = bias_proj.shape
+    rank = left_proj.shape[0]
+    heads, channels = bias_proj.shape
     key_count = right.shape[0]
     lanes = heads * count
     block = pair.shape[1]
 
     @pl.when(step == 0)
     def _():
-        left = dot(query_norm[...], left_proj[...])
+        left = dot_nt(query_norm[...], left_proj[...])
         repeated = (iota((rank, rank * rank), 1) // rank == iota((rank, rank * rank), 0)).astype(F32)
         wide = dot(left, repeated, HIGHEST)
         tall = jnp.broadcast_to(wide[:, None, :], (count, rank, rank * rank))
@@ -120,17 +123,16 @@
             [high.astype(F32), low.astype(F32), high.astype(F32)], axis=1
         )
         expand = (iota((heads, lanes), 1) // count == iota((heads, lanes), 0)).astype(F32)
-        high, low = split(dot(bias_proj[...], expand, HIGHEST))
+        high, low = split(dot_tn(bias_proj[...], expand, HIGHEST))
         weight_scratch[0] = high
         weight_scratch[1] = low
-        lane = iota((1, lanes), 1)
-        weights = jnp.zeros((1, lanes), F32)
-        for head in range(heads):
-            weights = jnp.where(lane // count == head, chain_weight[head], weights)
-        chains = jnp.zeros((1, lanes), jnp.int32)
-        rows = query_chain.shape[1]
-        for index in range(count):
-            chains = jnp.where(lane % count == index, query_chain[index // rows, index % rows], chains)
+        spot = (heads, lanes)
+        weights = jnp.where(iota(spot, 1) // count == iota(spot, 0), column_of(chain_weight[...]), 0.0)
+        weights = jnp.sum(weights, axis=0, keepdims=True)
+        spot = (count, lanes)
+        chains = rows_column(query_chain[...])
+        chains = jnp.where(iota(spot, 1) % count == iota(spot, 0), chains, 0)
+        chains = jnp.sum(chains, axis=0, keepdims=True)
         own = column_of(key_chain[...])
         bias_out[...] = jnp.where(own != chains, weights, 0.0)
 
@@ -147,21 +149,32 @@
     bias_out[...] = total
 
 
-def attend_kernel(place, pieces, own, other, bias, part_out, heads, count, mask_count):
-    col, row = place[0], place[1]
+def listed(refs):
+    values = []
+    for ref in refs:
+        values += [ref[...]] if len(ref.shape) == 2 else [ref[i] for i in range(ref.shape[0])]
+    return values
+
+
+def gathered(pieces, col, start, stop):
+    values = listed(pieces)
+    if len(values) == 1:
+        return values[0][:, start:stop]
+    share = values[0].shape[1]
+    blocks = []
+    for target in range(start // share, stop // share):
+        chosen = values[0]
+        for index in range(1, len(values)):
+            chosen = jnp.where((col ^ target) == index, values[index], chosen)
+        blocks.append(chosen)
+    return jnp.concatenate(blocks, axis=1)
+
+
+def attend_kernel(place, pieces, own, other, bias, part_out, heads, count):
+    col, row = place[0:1, 0:1], place[0:1, 1:2]
     model = own.shape[1]
     head = model // heads
-    share = pieces[0].shape[1]
-    if len(pieces) > 1:
-        blocks = []
-        for target in range(model // share):
-            chosen = pieces[0][...]
-            for index in range(1, len(pieces)):
-                chosen = jnp.where((col ^ target) == index, pieces[index][...], chosen)
-            blocks.append(chosen)
-        query = jnp.concatenate(blocks, axis=1)
-    else:
-        query = pieces[0][:, :model]
+    query = gathered(pieces, col, 0, model)
     first, second = own[...], other[...]
     keys = jnp.where(row == 0, first, second)
     values = jnp.where(row == 0, second, first)
@@ -212,22 +225,10 @@
 
 
 def finish_kernel(place, pieces, parts, out_proj, update_out, heads):
-    col = place[0]
+    col = place[0:1, 0:1]
     model = out_proj.shape[0]
-    share = pieces[0].shape[1]
-    if len(pieces) > 1:
-        blocks = []
-        for target in range(model // share, 2 * model // share):
-            chosen = pieces[0][...]
-            for index in range(1, len(pieces)):
-                chosen = jnp.where((col ^ target) == index, pieces[index][...], chosen)
-            blocks.append(chosen)
-        gate = jnp.concatenate(blocks, axis=1)
-    else:
-        gate = pieces[0][:, model:]
-    values = []
-    for part in parts:
-        values += [part[...]] if len(part.shape) == 2 else [part[i] for i in range(part.shape[0])]
+    gate = gathered(pieces, col, model, 2 * model)
+    values = listed(parts)
     summed, _, _, total = merged(values, heads)
     attended = (summed / total * jax.nn.sigmoid(gate.astype(F32))).astype(BF16)
     update_out[...] = dot(attended, out_proj[...]).astype(BF16)
@@ -266,8 +267,9 @@
     rank = left_proj.shape[1]
     lanes = heads * count
     cols = lax.axis_size("col")
-    gain = norm_gain.reshape(1, model)
-    place = jnp.stack([lax.axis_index("col"), lax.axis_index("row")]).astype(jnp.int32)
+    step_index = timestep.reshape(1, 1)
+    place = jnp.stack([lax.axis_index("col"), lax.axis_index("row")]).astype(jnp.int32)[None]
+    grant = pltpu.CompilerParams(vmem_limit_bytes=16 << 20)
 
     query_part, query_norm = pl.pallas_call(
         query_kernel,
@@ -275,10 +277,11 @@
             jax.ShapeDtypeStruct((count, query_proj.shape[1]), BF16),
             jax.ShapeDtypeStruct((count, model), BF16),
         ),
-        in_specs=[SMEM, SMEM] + [VMEM] * 4,
+        in_specs=[VMEM] * 6,
         out_specs=(VMEM, VMEM),
+        compiler_params=grant,
         name="query",
-    )(timestep, query_mask, query_single, time_table, gain, query_proj)
+    )(step_index, query_mask, query_single, time_table, norm_gain, query_proj.T)
 
     half, right = pl.pallas_call(
         key_kernel,
@@ -286,17 +289,18 @@
             jax.ShapeDtypeStruct((key_count, kv_proj.shape[1]), BF16),
             jax.ShapeDtypeStruct((key_count, rank), F32),
         ),
-        in_specs=[SMEM] + [VMEM] * 6,
+        in_specs=[VMEM] * 7,
         out_specs=(VMEM, VMEM),
+        compiler_params=grant,
         name="keys",
     )(
-        timestep,
+        step_index,
         key_mask.reshape(1, key_count),
         key_single,
         time_table,
-        gain,
+        norm_gain,
         kv_proj,
-        right_proj,
+        right_proj.T,
     )
     other = exchanged(half, "row", 1)
 
@@ -306,8 +310,7 @@
         both = jnp.stack([query_part, near])
         pieces = [query_part, near]
         for flip in (2, 4, 6):
-            far = exchanged(both, "col", flip)
-            pieces += [far[0], far[1]]
+            pieces.append(exchanged(both, "col", flip))
     else:
         pieces = [lax.all_gather(query_part, "col", axis=1, tiled=True)]
 
@@ -326,12 +329,12 @@
             jax.ShapeDtypeStruct((key_count, lanes), F32),
         ),
         in_specs=[
-            SMEM,
-            SMEM,
+            whole(1, heads),
+            whole(slabs, rows),
             whole(count, model),
-            whole(model, rank),
+            whole(rank, model),
             whole(rank * rank, channels),
-            whole(channels, heads),
+            whole(heads, channels),
             whole(key_count, rank),
             whole(1, key_count),
             pair_spec,
@@ -342,14 +345,15 @@
             pltpu.VMEM((key_count, 3 * rank), F32),
             pltpu.VMEM((2, channels, lanes), BF16),
         ],
+        compiler_params=grant,
         name="pairs",
     )(
-        chain_weight,
+        chain_weight.reshape(1, heads),
         query_chain,
         query_norm,
-        left_proj,
+        left_proj.T,
         outer_proj,
-        bias_proj,
+        bias_proj.T,
         right,
         key_chain.reshape(1, key_count),
         pair_block,
@@ -359,13 +363,14 @@
 
     def attend_body(place, *refs):
         n = len(pieces)
-        attend_kernel(place, refs[:n], *refs[n:], heads, count, None)
+        attend_kernel(place, refs[:n], *refs[n:], heads, count)
 
     part = pl.pallas_call(
         attend_body,
         out_shape=part_shape,
-        in_specs=[SMEM] + [VMEM] * (len(pieces) + 3),
+        in_specs=[VMEM] * (len(pieces) + 4),
         out_specs=VMEM,
+        compiler_params=grant,
         name="attend",
     )(place, *pieces, half, other, bias)
 
@@ -375,6 +380,7 @@
             out_shape=part_shape,
             in_specs=[VMEM, VMEM],
             out_specs=VMEM,
+            compiler_params=grant,
             name="join",
         )(part, exchanged(part, "col", 1))
         parts = [part] + [exchanged(part, "col", flip) for flip in (6, 4, 2)]
@@ -388,8 +394,9 @@
     update = pl.pallas_call(
         finish_body,
         out_shape=jax.ShapeDtypeStruct((count, model), BF16),
-        in_specs=[SMEM] + [VMEM] * (len(pieces) + len(parts) + 1),
+        in_specs=[VMEM] * (len(pieces) + len(parts) + 2),
         out_specs=VMEM,
+        compiler_params=grant,
         name="finish",
     )(place, *pieces, *parts, out_proj)
     return (new_pair, update.reshape(slabs, rows, model))

time: 52.2 us -> 39.7 us (0.76)
  Pallas kernels: 17.5 us -> 7.33 us
  waiting for transfers between devices: 10.6 us -> 8.67 us
  other arithmetic: 0.62 us -> 0.08 us
    unnamed x24 -> x38, local copies, waits for them, and re-layouts: 6.18 us -> 9.14 us
    pallas_call x1, Pallas kernels: 2.82 us -> 0.68 us  [on_device(): pl.pallas_call(key_kernel, out_shape=(jax.ShapeDtypeStruct((key_count, kv...]
    ppermute x9, waiting for transfers between devices: 10.6 us -> 8.67 us  [exchanged(): lax.ppermute(value, axis, [(index, index ^ flip) for index in range(size)])]
    squeeze x3 -> x0, local copies, waits for them, and re-layouts: 1.81 us -> none  [on_device(): pieces += [far[0], far[1]]]
    pallas_call x1, Pallas kernels: 2.67 us -> 0.88 us  [on_device(): pl.pallas_call(attend_body, out_shape=part_shape, in_specs=[VMEM] * (len(...]
    pallas_call x1, Pallas kernels: 2.04 us -> 0.42 us  [on_device(): pl.pallas_call(query_kernel, out_shape=(jax.ShapeDtypeStruct((count, quer...]
    pallas_call x1, Pallas kernels: 5.38 us -> 3.82 us  [on_device(): pl.pallas_call(pair_kernel, grid=(steps,), out_shape=(jax.ShapeDtypeStruc...]
    pallas_call x1, Pallas kernels: 2.78 us -> 1.26 us  [on_device(): pl.pallas_call(finish_body, out_shape=jax.ShapeDtypeStruct((count, model)...]
  transfers between devices with their start and end apart: 9 -> 9, of which waited for: 5 -> 4; matrix products, arithmetic and copies ran while one was open for 9% -> 0% of each run, Pallas kernels for 16% -> 11%
where the time goes in v2:
time: 39.7 us; the launch traced here: 39.2 us
  starting transfers between devices  12.6 us (32%)
  local copies, waits for them, and re-layouts  9.14 us (23%)
  waiting for transfers between devices  8.67 us (22%)
  Pallas kernels  7.33 us (18%)
  between operations  1.44 us (4%)
    ppermute x9, starting transfers between devices, exchanged(): lax.ppermute(value, axis, [(index, index ^ flip) for index in range(size)])  12.6 us
    unnamed x38, local copies, waits for them, and re-layouts  9.14 us
    ppermute x9, waiting for transfers between devices, exchanged(): lax.ppermute(value, axis, [(index, index ^ flip) for index in range(size)])  8.67 us
    pallas_call x1, Pallas kernels, on_device(): pl.pallas_call(pair_kernel, grid=(steps,), out_shape=(jax.ShapeDtypeStruc...  3.82 us
    pallas_call x1, Pallas kernels, on_device(): pl.pallas_call(finish_body, out_shape=jax.ShapeDtypeStruct((count, model)...  1.26 us
    pallas_call x1, Pallas kernels, on_device(): pl.pallas_call(attend_body, out_shape=part_shape, in_specs=[VMEM] * (len(...  0.88 us
  transfers between devices with their start and end apart: 9, of which 4 were waited for; matrix products, arithmetic and copies ran while one was open for 0% of the time, Pallas kernels for 11%

profile of v2, /device:TPU:0, one launch (start us, length us, event | category | flops | bytes accessed | tf_op | source)
XLA Modules:
  0.0 39.2 jit_solution(17204780727592831573)
XLA Ops:
  1.3 0.9 %copy-done.3 = bf16[50,768]{1,0:T(8,128)(2,1)S(1)} copy-done((bf16[50,768]{1,0:T(8,128)(2,1)S(1)}, bf16[50,768]{1,0:T(8,128)(2,1)}, u32[]{:S(2)}) %copy-start.3) | copy-done | bytes 76824
  2.2 1.0 %copy-done.5 = bf16[768,192]{0,1:T(8,128)(2,1)S(1)} copy-done((bf16[768,192]{0,1:T(8,128)(2,1)S(1)}, bf16[768,192]{0,1:T(8,128)(2,1)}, u32[]{:S(2)}) %copy-start.5) | copy-done | bytes 294936
  3.2 0.7 %copy-done.7 = bf16[2,8,768]{2,1,0:T(8,128)(2,1)S(1)} copy-done((bf16[2,8,768]{2,1,0:T(8,128)(2,1)S(1)}, bf16[2,8,768]{2,1,0:T(8,128)(2,1)}, u32[]{:S(2)}) %copy-start.7) | copy-done | bytes 24600
  3.9 0.7 %copy-done.9 = f32[768]{0:T(1024)S(1)} copy-done((f32[768]{0:T(1024)S(1)}, f32[768]{0:T(1024)}, u32[]{:S(2)}) %copy-start.9) | copy-done | bytes 3096
  4.6 0.7 %copy-done.14 = s32[2,8]{1,0:T(2,128)S(1)} copy-done((s32[2,8]{1,0:T(2,128)S(1)}, s32[2,8]{1,0:T(2,128)}, u32[]{:S(2)}) %copy-start.14) | copy-done | bytes 88
  5.7 3.1 %collective-permute-start = (bf16[16,192]{1,0:T(8,128)(2,1)S(1)}, bf16[16,192]{1,0:T(8,128)(2,1)S(1)}, u32[]{:S(2)}, u32[]{:S(2)}) collective-permute-start(bf16[16,192]{1,0:T(8,128)(2,1)S(1)} %get-tuple-element.11.refs_0_), channel_id=1, source_target_pairs={{0,2},{2,0},{4,6},{6,4},{8,10},{10,8},{12,14},{14,12},{1,3},{3,1},... | collective-permute-start | bytes 18440 | tf_op jit(solution)/shard_map/ppermute | solution.py:239
  8.8 1.3 %copy-done = bf16[768,768]{1,0:T(8,128)(2,1)S(1)} copy-done((bf16[768,768]{1,0:T(8,128)(2,1)S(1)}, bf16[768,768]{1,0:T(8,128)(2,1)}, u32[]{:S(2)}) %copy-start) | copy-done | bytes 1179672
  10.0 0.9 %copy-done.4 = bf16[50,768]{1,0:T(8,128)(2,1)S(1)} copy-done((bf16[50,768]{1,0:T(8,128)(2,1)S(1)}, bf16[50,768]{1,0:T(8,128)(2,1)}, u32[]{:S(2)}) %copy-start.4) | copy-done | bytes 76824
  10.9 0.9 %copy-done.6 = bf16[144,768]{1,0:T(8,128)(2,1)S(1)} copy-done((bf16[144,768]{1,0:T(8,128)(2,1)S(1)}, bf16[144,768]{1,0:T(8,128)(2,1)}, u32[]{:S(2)}) %copy-start.6) | copy-done | bytes 221208
  11.9 0.7 %copy-done.10 = f32[768]{0:T(1024)S(1)} copy-done((f32[768]{0:T(1024)S(1)}, f32[768]{0:T(1024)}, u32[]{:S(2)}) %copy-start.10) | copy-done | bytes 3096
  12.6 0.7 %copy-done.11 = bf16[768,8]{0,1:T(8,128)(2,1)S(1)} copy-done((bf16[768,8]{0,1:T(8,128)(2,1)S(1)}, bf16[768,8]{0,1:T(8,128)(2,1)}, u32[]{:S(2)}) %copy-start.11) | copy-done | bytes 12312
  13.3 0.7 %copy-done.15 = s32[144]{0:T(256)S(1)} copy-done((s32[144]{0:T(256)S(1)}, s32[144]{0:T(256)}, u32[]{:S(2)}) %copy-start.15) | copy-done | bytes 600
  13.9 0.7 %keys.1 = (bf16[144,768]{1,0:T(8,128)(2,1)S(1)}, f32[144,8]{1,0:T(8,128)S(1)}) custom-call(s32[1,1]{1,0:T(1,128)} %bitcast.16.step, s32[1,144]{1,0:T(1,128)S(1)} %bitcast.23, bf16[144,768]{1,0:T(8,128)(2,1)S(1)} %copy-done.6, bf16[50,768]{1,0:T(8,128)(2,1)S(1)} %copy-done.4, f32[768]{0:T(1024)S(1)} %copy-done.10, bf16[768,768]{1,0:T(8,128)(2,1)S(1)} %copy-done, ...), custom_call_target="tpu_custom_call" | custom-call | tf_op jit(solution)/shard_map/keys/pallas_call | solution.py:286
  14.8 1.6 %collective-permute-start.1 = (bf16[2,16,192]{2,1,0:T(8,128)(2,1)S(1)}, bf16[2,16,192]{2,1,0:T(8,128)(2,1)S(1)}, u32[]{:S(2)}, u32[]{:S(2)}) collective-permute-start(bf16[2,16,192]{2,1,0:T(8,128)(2,1)S(1)} %pad_maximum_fusion), channel_id=1, source_target_pairs={{0,4},{2,6},{4,0},{6,2},{8,12},{10,14},{12,8},{14,10},{1,5},{3,7},... | collective-permute-start | bytes 36872 | tf_op jit(solution)/shard_map/ppermute | solution.py:239
  16.4 2.6 %collective-permute-start.2 = (bf16[2,16,192]{2,1,0:T(8,128)(2,1)S(1)}, bf16[2,16,192]{2,1,0:T(8,128)(2,1)S(1)}, u32[]{:S(2)}, u32[]{:S(2)}) collective-permute-start(bf16[2,16,192]{2,1,0:T(8,128)(2,1)S(1)} %pad_maximum_fusion), channel_id=1, source_target_pairs={{0,8},{2,10},{4,12},{6,14},{8,0},{10,2},{12,4},{14,6},{1,9},{3,11}... | collective-permute-start | bytes 36872 | tf_op jit(solution)/shard_map/ppermute | solution.py:239
  19.3 3.8 %pairs.1 = (f32[2,8,144,128]{3,2,1,0:T(8,128)}, f32[144,192]{1,0:T(8,128)S(1)}) custom-call(f32[1,12]{1,0:T(1,128)S(1)} %bitcast.25, s32[2,8]{1,0:T(2,128)S(1)} %copy-done.16, bf16[16,768]{1,0:T(8,128)(2,1)S(1)} %get-tuple-element.8.query_norm, bf16[8,768]{1,0:T(8,128)(2,1)S(1)} %bitcast.21, bf16[64,128]{1,0:T(8,128)(2,1)S(1)} %copy-done.8, ...), custom_call_target="tpu_custom_call" | custom-call | tf_op jit(solution)/shard_map/pairs/pallas_call | solution.py:324
  23.1 1.4 %collective-permute-done.3.refs_4_ = bf16[2,16,192]{2,1,0:T(8,128)(2,1)S(1)} collective-permute-done((bf16[2,16,192]{2,1,0:T(8,128)(2,1)S(1)}, bf16[2,16,192]{2,1,0:T(8,128)(2,1)S(1)}, u32[]{:S(2)}, u32[]{:S(2)}) %collective-permute-start.3) | collective-permute-done | bytes 12320 | tf_op jit(solution)/shard_map/ppermute | solution.py:239
  24.5 0.9 %attend.1.first = f32[16,1024]{1,0:T(8,128)S(1)} custom-call(s32[1,2]{1,0:T(1,128)S(1)} %add_bitcast_fusion.place, bf16[16,192]{1,0:T(8,128)(2,1)S(1)} %get-tuple-element.11.refs_0_, bf16[16,192]{1,0:T(8,128)(2,1)S(1)} %collective-permute-done.refs_1_, bf16[2,16,192]{2,1,0:T(8,128)(2,1)S(1)} %collective-permute-done.1.refs_2_, ...), custom_call_target="tpu_custom_call" | custom-call | tf_op jit(solution)/shard_map/attend/pallas_call | solution.py:368
  25.9 3.7 %collective-permute-done.5.second = f32[16,1024]{1,0:T(8,128)S(1)} collective-permute-done((f32[16,1024]{1,0:T(8,128)S(1)}, f32[16,1024]{1,0:T(8,128)S(1)}, u32[]{:S(2)}, u32[]{:S(2)}) %collective-permute-start.5) | collective-permute-done | bytes 65568 | tf_op jit(solution)/shard_map/ppermute | solution.py:239
  30.0 2.3 %collective-permute-start.6 = (f32[16,1024]{1,0:T(8,128)S(1)}, f32[16,1024]{1,0:T(8,128)S(1)}, u32[]{:S(2)}, u32[]{:S(2)}) collective-permute-start(f32[16,1024]{1,0:T(8,128)S(1)} %join.1.refs_5_), channel_id=1, source_target_pairs={{0,12},{2,14},{4,8},{6,10},{8,4},{10,6},{12,0},{14,2},{1,13},{3,15... | collective-permute-start | bytes 196616 | tf_op jit(solution)/shard_map/ppermute | solution.py:239
  32.3 2.1 %collective-permute-start.8 = (f32[16,1024]{1,0:T(8,128)S(1)}, f32[16,1024]{1,0:T(8,128)S(1)}, u32[]{:S(2)}, u32[]{:S(2)}) collective-permute-start(f32[16,1024]{1,0:T(8,128)S(1)} %join.1.refs_5_), channel_id=1, source_target_pairs={{0,4},{2,6},{4,0},{6,2},{8,12},{10,14},{12,8},{14,10},{1,5},{3,7},... | collective-permute-start | bytes 196616 | tf_op jit(solution)/shard_map/ppermute | solution.py:239
  34.4 2.2 %collective-permute-done.6.refs_6_ = f32[16,1024]{1,0:T(8,128)S(1)} collective-permute-done((f32[16,1024]{1,0:T(8,128)S(1)}, f32[16,1024]{1,0:T(8,128)S(1)}, u32[]{:S(2)}, u32[]{:S(2)}) %collective-permute-start.6) | collective-permute-done | bytes 65568 | tf_op jit(solution)/shard_map/ppermute | solution.py:239
  36.7 1.3 %collective-permute-done.7.refs_7_ = f32[16,1024]{1,0:T(8,128)S(1)} collective-permute-done((f32[16,1024]{1,0:T(8,128)S(1)}, f32[16,1024]{1,0:T(8,128)S(1)}, u32[]{:S(2)}, u32[]{:S(2)}) %collective-permute-start.7) | collective-permute-done | bytes 65568 | tf_op jit(solution)/shard_map/ppermute | solution.py:239
  38.0 1.3 %finish.1 = bf16[16,768]{1,0:T(8,128)(2,1)} custom-call(s32[1,2]{1,0:T(1,128)S(1)} %add_bitcast_fusion.place, bf16[16,192]{1,0:T(8,128)(2,1)S(1)} %get-tuple-element.11.refs_0_, bf16[16,192]{1,0:T(8,128)(2,1)S(1)} %collective-permute-done.refs_1_, bf16[2,16,192]{2,1,0:T(8,128)(2,1)S(1)} %collective-permute-done.1.refs_2_, ...), custom_call_target="tpu_custom_call" | custom-call | tf_op jit(solution)/shard_map/finish/pallas_call | solution.py:394
  (40 shorter events, 1.7 us)
Async XLA Ops:
  0.6 18.6 %copy-start.18 = (f32[12]{0:T(128)S(1)}, f32[12]{0:T(128)}, u32[]{:S(2)}) copy-start(f32[12]{0:T(128)} %param.32) | copy-start | bytes 148
  0.6 18.6 %copy-start.16 = (s32[2,8]{1,0:T(2,128)S(1)}, s32[2,8]{1,0:T(2,128)}, u32[]{:S(2)}) copy-start(s32[2,8]{1,0:T(2,128)} %query_chain.1) | copy-start | bytes 196
  0.7 18.6 %copy-start.17 = (s32[144]{0:T(256)S(1)}, s32[144]{0:T(256)}, u32[]{:S(2)}) copy-start(s32[144]{0:T(256)} %param.22) | copy-start | bytes 1732
  1.3 0.9 %copy-start.3 = (bf16[50,768]{1,0:T(8,128)(2,1)S(1)}, bf16[50,768]{1,0:T(8,128)(2,1)}, u32[]{:S(2)}) copy-start(bf16[50,768]{1,0:T(8,128)(2,1)} %table.3) | copy-start | bytes 230404
  2.2 1.0 %copy-start.5 = (bf16[768,192]{0,1:T(8,128)(2,1)S(1)}, bf16[768,192]{0,1:T(8,128)(2,1)}, u32[]{:S(2)}) copy-start(bf16[768,192]{0,1:T(8,128)(2,1)} %param.33) | copy-start | bytes 884740
  3.2 0.7 %copy-start.7 = (bf16[2,8,768]{2,1,0:T(8,128)(2,1)S(1)}, bf16[2,8,768]{2,1,0:T(8,128)(2,1)}, u32[]{:S(2)}) copy-start(bf16[2,8,768]{2,1,0:T(8,128)(2,1)} %single.2) | copy-start | bytes 73732
  5.3 14.0 %copy-start.8 = (bf16[64,128]{1,0:T(8,128)(2,1)S(1)}, bf16[64,128]{1,0:T(8,128)(2,1)}, u32[]{:S(2)}) copy-start(bf16[64,128]{1,0:T(8,128)(2,1)} %outer_proj.1) | copy-start | bytes 49156
  5.3 14.0 %copy-start.12 = (bf16[768,8]{0,1:T(8,128)(2,1)S(1)}, bf16[768,8]{0,1:T(8,128)(2,1)}, u32[]{:S(2)}) copy-start(bf16[768,8]{0,1:T(8,128)(2,1)} %param.28) | copy-start | bytes 36868
  5.3 14.0 %copy-start.13 = (f32[128,12]{0,1:T(8,128)S(1)}, f32[128,12]{0,1:T(8,128)}, u32[]{:S(2)}) copy-start(f32[128,12]{0,1:T(8,128)} %param.31) | copy-start | bytes 18436
  5.7 9.0 %collective-permute-start = (bf16[16,192]{1,0:T(8,128)(2,1)S(1)}, bf16[16,192]{1,0:T(8,128)(2,1)S(1)}, u32[]{:S(2)}, u32[]{:S(2)}) collective-permute-start(bf16[16,192]{1,0:T(8,128)(2,1)S(1)} %get-tuple-element.11.refs_0_), channel_id=1, source_target_pairs={{0,2},{2,0},{4,6},{6,4},{8,10},{10,8},{12,14},{14,12},{1,3},{3,1},... | collective-permute-start | bytes 18440 | tf_op jit(solution)/shard_map/ppermute | solution.py:239
  8.8 1.3 %copy-start = (bf16[768,768]{1,0:T(8,128)(2,1)S(1)}, bf16[768,768]{1,0:T(8,128)(2,1)}, u32[]{:S(2)}) copy-start(bf16[768,768]{1,0:T(8,128)(2,1)} %proj.1) | copy-start | bytes 3538948
  10.0 0.9 %copy-start.4 = (bf16[50,768]{1,0:T(8,128)(2,1)S(1)}, bf16[50,768]{1,0:T(8,128)(2,1)}, u32[]{:S(2)}) copy-start(bf16[50,768]{1,0:T(8,128)(2,1)} %table.3) | copy-start | bytes 230404
  10.9 0.9 %copy-start.6 = (bf16[144,768]{1,0:T(8,128)(2,1)S(1)}, bf16[144,768]{1,0:T(8,128)(2,1)}, u32[]{:S(2)}) copy-start(bf16[144,768]{1,0:T(8,128)(2,1)} %single.3) | copy-start | bytes 663556
  12.6 0.7 %copy-start.11 = (bf16[768,8]{0,1:T(8,128)(2,1)S(1)}, bf16[768,8]{0,1:T(8,128)(2,1)}, u32[]{:S(2)}) copy-start(bf16[768,8]{0,1:T(8,128)(2,1)} %param.29) | copy-start | bytes 36868
  13.9 5.4 %copy-start.1 = (f32[2,8,144,128]{3,2,1,0:T(8,128)S(1)}, f32[2,8,144,128]{3,2,1,0:T(8,128)}, u32[]{:S(2)}) copy-start(f32[2,8,144,128]{3,2,1,0:T(8,128)} %pair.1) | copy-start | bytes 3538948
  14.6 23.3 %copy-start.2 = (bf16[768,768]{1,0:T(8,128)(2,1)S(1)}, bf16[768,768]{1,0:T(8,128)(2,1)}, u32[]{:S(2)}) copy-start(bf16[768,768]{1,0:T(8,128)(2,1)} %refs_9_.1) | copy-start | bytes 3538948
  14.6 9.9 %collective-permute-start.4 = (bf16[144,768]{1,0:T(8,128)(2,1)S(1)}, bf16[144,768]{1,0:T(8,128)(2,1)S(1)}, u32[]{:S(2)}, u32[]{:S(2)}) collective-permute-start(bf16[144,768]{1,0:T(8,128)(2,1)S(1)} %get-tuple-element.12.refs_5_), channel_id=1, source_target_pairs={{0,1},{1,0},{2,3},{3,2},{4,5},{5,4},{6,7},{7,6},{8,9},{9,8},{10,11... | collective-permute-start | bytes 663560 | tf_op jit(solution)/shard_map/ppermute | solution.py:239
  14.8 8.4 %collective-permute-start.1 = (bf16[2,16,192]{2,1,0:T(8,128)(2,1)S(1)}, bf16[2,16,192]{2,1,0:T(8,128)(2,1)S(1)}, u32[]{:S(2)}, u32[]{:S(2)}) collective-permute-start(bf16[2,16,192]{2,1,0:T(8,128)(2,1)S(1)} %pad_maximum_fusion), channel_id=1, source_target_pairs={{0,4},{2,6},{4,0},{6,2},{8,12},{10,14},{12,8},{14,10},{1,5},{3,7},... | collective-permute-start | bytes 36872 | tf_op jit(solution)/shard_map/ppermute | solution.py:239
  16.4 6.7 %collective-permute-start.2 = (bf16[2,16,192]{2,1,0:T(8,128)(2,1)S(1)}, bf16[2,16,192]{2,1,0:T(8,128)(2,1)S(1)}, u32[]{:S(2)}, u32[]{:S(2)}) collective-permute-start(bf16[2,16,192]{2,1,0:T(8,128)(2,1)S(1)} %pad_maximum_fusion), channel_id=1, source_target_pairs={{0,8},{2,10},{4,12},{6,14},{8,0},{10,2},{12,4},{14,6},{1,9},{3,11}... | collective-permute-start | bytes 36872 | tf_op jit(solution)/shard_map/ppermute | solution.py:239
  19.0 5.5 %collective-permute-start.3 = (bf16[2,16,192]{2,1,0:T(8,128)(2,1)S(1)}, bf16[2,16,192]{2,1,0:T(8,128)(2,1)S(1)}, u32[]{:S(2)}, u32[]{:S(2)}) collective-permute-start(bf16[2,16,192]{2,1,0:T(8,128)(2,1)S(1)} %pad_maximum_fusion), channel_id=1, source_target_pairs={{0,12},{2,14},{4,8},{6,10},{8,4},{10,6},{12,0},{14,2},{1,13},{3,15... | collective-permute-start | bytes 36872 | tf_op jit(solution)/shard_map/ppermute | solution.py:239
  25.4 4.3 %collective-permute-start.5 = (f32[16,1024]{1,0:T(8,128)S(1)}, f32[16,1024]{1,0:T(8,128)S(1)}, u32[]{:S(2)}, u32[]{:S(2)}) collective-permute-start(f32[16,1024]{1,0:T(8,128)S(1)} %attend.1.first), channel_id=1, source_target_pairs={{0,2},{2,0},{4,6},{6,4},{8,10},{10,8},{12,14},{14,12},{1,3},{3,1},... | collective-permute-start | bytes 196616 | tf_op jit(solution)/shard_map/ppermute | solution.py:239
  30.0 6.7 %collective-permute-start.6 = (f32[16,1024]{1,0:T(8,128)S(1)}, f32[16,1024]{1,0:T(8,128)S(1)}, u32[]{:S(2)}, u32[]{:S(2)}) collective-permute-start(f32[16,1024]{1,0:T(8,128)S(1)} %join.1.refs_5_), channel_id=1, source_target_pairs={{0,12},{2,14},{4,8},{6,10},{8,4},{10,6},{12,0},{14,2},{1,13},{3,15... | collective-permute-start | bytes 196616 | tf_op jit(solution)/shard_map/ppermute | solution.py:239
  32.3 5.7 %collective-permute-start.7 = (f32[16,1024]{1,0:T(8,128)S(1)}, f32[16,1024]{1,0:T(8,128)S(1)}, u32[]{:S(2)}, u32[]{:S(2)}) collective-permute-start(f32[16,1024]{1,0:T(8,128)S(1)} %join.1.refs_5_), channel_id=1, source_target_pairs={{0,8},{2,10},{4,12},{6,14},{8,0},{10,2},{12,4},{14,6},{1,9},{3,11}... | collective-permute-start | bytes 196616 | tf_op jit(solution)/shard_map/ppermute | solution.py:239
  32.3 5.7 %collective-permute-start.8 = (f32[16,1024]{1,0:T(8,128)S(1)}, f32[16,1024]{1,0:T(8,128)S(1)}, u32[]{:S(2)}, u32[]{:S(2)}) collective-permute-start(f32[16,1024]{1,0:T(8,128)S(1)} %join.1.refs_5_), channel_id=1, source_target_pairs={{0,4},{2,6},{4,0},{6,2},{8,12},{10,14},{12,8},{14,10},{1,5},{3,7},... | collective-permute-start | bytes 196616 | tf_op jit(solution)/shard_map/ppermute | solution.py:239
  (4 other events, 2.7 us)

commit v3 on v2

v3 whole, which is shorter than its diff:
```python
import functools
import math

import jax
import jax.numpy as jnp
from jax import lax
from jax.experimental import pallas as pl
from jax.experimental.pallas import tpu as pltpu
from jax.sharding import PartitionSpec as P


EPSILON = 1e-05
HIGHEST = lax.Precision.HIGHEST
LANES = 128
TERM = LANES // 5
VMEM = pl.BlockSpec(memory_space=pltpu.VMEM)
HBM = pl.BlockSpec(memory_space=pltpu.HBM)
SMEM = pl.BlockSpec(memory_space=pltpu.SMEM)
F32 = jnp.float32
BF16 = jnp.bfloat16


def dot(left, right, precision=None):
    return jnp.dot(left, right, preferred_element_type=F32, precision=precision)


def dot_nt(left, right):
    return lax.dot_general(left, right, (((1,), (1,)), ((), ())), preferred_element_type=F32)


def dot_tn(left, right, precision=None):
    return lax.dot_general(
        left, right, (((0,), (0,)), ((), ())), preferred_element_type=F32, precision=precision
    )


def iota(shape, axis):
    return lax.broadcasted_iota(jnp.int32, shape, axis)


def split(value):
    high = value.astype(BF16)
    return high, (value - high.astype(F32)).astype(BF16)


def normalized(features, gain):
    average = jnp.mean(features, axis=-1, keepdims=True)
    centred = features - average
    spread = jnp.mean(centred * centred, axis=-1, keepdims=True)
    return (centred * lax.rsqrt(spread + EPSILON) * gain).astype(BF16)


def column_of(row):
    count = row.shape[1]
    square = (count, count)
    return jnp.sum(jnp.where(iota(square, 0) == iota(square, 1), row, 0), axis=1, keepdims=True)


def rows_column(table):
    return jnp.concatenate([column_of(table[i : i + 1]) for i in range(table.shape[0])], axis=0)


def query_kernel(*refs):
    step, mask, single, table, gain, proj = refs[:6]
    later = refs[6:10]
    part_out, norm_out, time_out, gain_out = refs[10:14]
    later_out = refs[14:18]
    mask_in, single_in, table_in, proj_in, sems = refs[18:]
    sources = (mask, single, table, gain, proj) + later
    targets = (mask_in, single_in, table_in, gain_out, proj_in) + later_out
    copies = [
        pltpu.make_async_copy(source, target, sems.at[index])
        for index, (source, target) in enumerate(zip(sources, targets))
    ]
    for copy in copies:
        copy.start()
    for copy in copies[:4]:
        copy.wait()
    slabs, rows, width = single.shape
    features = single_in[...].astype(F32).reshape(slabs * rows, width)
    kept = rows_column(mask_in[...].astype(F32))
    held = table_in[...].astype(F32)
    time_row = jnp.sum(jnp.where(iota(held.shape, 0) == step[0], held, 0.0), axis=0, keepdims=True)
    time_out[...] = time_row
    norm = normalized(features + kept * time_row, gain_out[...].reshape(1, width))
    norm_out[...] = norm
    copies[4].wait()
    part_out[...] = dot_nt(norm, proj_in[...]).astype(BF16)
    for copy in copies[5:]:
        copy.wait()


def key_kernel(time_row, gain, single, proj, mask, right_proj, half_out, right_out):
    kept = column_of(mask[...].astype(F32))
    features = single[...].astype(F32) + kept * time_row[...]
    norm = normalized(features, gain[...].reshape(1, features.shape[1]))
    half_out[...] = dot(norm, proj[...]).astype(BF16)
    right_out[...] = dot_nt(norm, right_proj[...])


def pair_kernel(
    chain_weight,
    query_chain,
    query_norm,
    left_proj,
    outer_proj,
    bias_proj,
    right,
    key_chain,
    pair,
    pair_out,
    bias_out,
    fresh_scratch,
    sems,
):
    slabs, rows = query_chain.shape
    count = slabs * rows
    rank = left_proj.shape[0]
    heads, channels = bias_proj.shape
    key_count = right.shape[0]
    lanes = heads * count
    left = dot_nt(query_norm[...], left_proj[...])
    spot = (rank, rank * rank)
    wide = dot(left, (iota(spot, 1) // rank == iota(spot, 0)).astype(F32), HIGHEST)
    tall = jnp.broadcast_to(wide[:, None, :], (count, rank, rank * rank))
    tall = tall.reshape(count * rank, rank * rank)
    spot = (count * rank, rank * rank)
    tall = jnp.where(iota(spot, 0) % rank == iota(spot, 1) % rank, tall, 0.0)
    mixer = dot(tall, outer_proj[...].astype(F32), HIGHEST).reshape(count, rank, channels)
    high, low = (part.astype(F32) for part in split(mixer))
    mixer = jnp.concatenate([high, high, low], axis=1).astype(BF16)
    high, low = (part.astype(F32) for part in split(right[...]))
    spread = jnp.concatenate([high, low, high], axis=1).astype(BF16)
    spot = (heads, lanes)
    expand = iota(spot, 1) // count == iota(spot, 0)
    high, low = split(dot_tn(bias_proj[...], expand.astype(F32), HIGHEST))
    weights = jnp.concatenate([high, high, low], axis=0)
    apart = jnp.sum(jnp.where(expand, column_of(chain_weight[...]), 0.0), axis=0, keepdims=True)
    spot = (count, lanes)
    chains = jnp.where(iota(spot, 1) % count == iota(spot, 0), rows_column(query_chain[...]), 0)
    chains = jnp.sum(chains, axis=0, keepdims=True)
    total = jnp.where(column_of(key_chain[...]) != chains, apart, 0.0)
    lane = iota((key_count, lanes), 1) % count
    bias = jnp.zeros((key_count, lanes), F32)
    copies = []
    for index in range(count):
        spot = (index // rows, index % rows)
        fresh = pair[spot] + dot(spread, mixer[index])
        fresh_scratch[index] = fresh
        copy = pltpu.make_async_copy(fresh_scratch.at[index], pair_out.at[spot], sems.at[index])
        copy.start()
        copies.append(copy)
        high, low = split(fresh)
        here = dot(jnp.concatenate([high, low, high], axis=1), weights)
        bias = jnp.where(lane == index, here, bias)
    bias_out[...] = bias + total
    for copy in copies:
        copy.wait()


def listed(refs):
    values = []
    for ref in refs:
        values += [ref[...]] if len(ref.shape) == 2 else [ref[i] for i in range(ref.shape[0])]
    return values


def gathered(pieces, col, start, stop):
    values = listed(pieces)
    if len(values) == 1:
        return values[0][:, start:stop]
    share = values[0].shape[1]
    blocks = []
    for target in range(start // share, stop // share):
        chosen = values[0]
        for index in range(1, len(values)):
            chosen = jnp.where((col ^ target) == index, values[index], chosen)
        blocks.append(chosen)
    return jnp.concatenate(blocks, axis=1)


def attend_kernel(pieces, halves, biases, part_out, heads, count):
    col, row = lax.axis_index("col"), lax.axis_index("row")
    model = halves[0].shape[1]
    head = model // heads
    lanes = heads * count
    query = gathered(pieces, col, 0, model)
    firsts = [ref[...] for ref in halves[::2]]
    seconds = [ref[...] for ref in halves[1::2]]
    keys = [jnp.where(row == 0, first, second) for first, second in zip(firsts, seconds)]
    values = [jnp.where(row == 0, second, first) for first, second in zip(firsts, seconds)]
    lane = iota((count, model), 1)
    spread = jnp.concatenate(
        [jnp.where(lane // head == index, query, jnp.zeros_like(query)) for index in range(heads)],
        axis=0,
    )
    scale = 1.0 / math.sqrt(head)
    scores = [dot_nt(key, spread) * scale + bias[...] for key, bias in zip(keys, biases)]
    peak = functools.reduce(jnp.maximum, [jnp.max(score, axis=0, keepdims=True) for score in scores])
    exponents = [jnp.exp(score - peak) for score in scores]
    total = sum(jnp.sum(exponent, axis=0, keepdims=True) for exponent in exponents)
    weights = jnp.concatenate([exponent.astype(BF16) for exponent in exponents], axis=0)
    summed = dot_tn(weights, jnp.concatenate(values, axis=0))
    taken = jnp.zeros((count, model), F32)
    for index in range(heads):
        taken = jnp.where(lane // head == index, summed[index * count : (index + 1) * count], taken)
    part_out[:, :model] = taken.astype(BF16)
    spot = (count, lanes)
    keep = iota(spot, 1) % count == iota(spot, 0)
    terms = terms_of(peak, 3) + terms_of(total, 2)
    rows = jnp.concatenate([jnp.where(keep, term, 0.0).astype(BF16) for term in terms], axis=1)
    spot = (len(terms) * lanes, LANES)
    source = iota(spot, 0)
    target = source // lanes * TERM + source % lanes // count
    part_out[:, model:] = dot(rows, (target == iota(spot, 1)).astype(BF16)).astype(BF16)


def terms_of(value, count):
    terms = []
    for _ in range(count):
        term = value.astype(BF16).astype(F32)
        terms.append(term)
        value = value - term
    return terms


def merged(parts, heads):
    model = parts[0].shape[1] - LANES
    count = parts[0].shape[0]
    spot = (LANES, model)
    term, place = iota(spot, 0), iota(spot, 1) // (model // heads)
    ours = term % TERM == place
    for_peak = (ours & (term // TERM < 3)).astype(BF16)
    for_total = (ours & (term // TERM >= 3) & (term // TERM < 5)).astype(BF16)
    stats = jnp.concatenate([part[:, model:] for part in parts], axis=0)
    peaks, totals = dot(stats, for_peak), dot(stats, for_total)
    cut = lambda array, index: array[index * count : (index + 1) * count]
    peak = functools.reduce(jnp.maximum, [cut(peaks, index) for index in range(len(parts))])
    scales = [jnp.exp(cut(peaks, index) - peak) for index in range(len(parts))]
    total = sum(scale * cut(totals, index) for index, scale in enumerate(scales))
    summed = sum(scale * part[:, :model].astype(F32) for scale, part in zip(scales, parts))
    return summed / total


def finish_kernel(pieces, parts, out_proj, update_out, heads):
    model = out_proj.shape[0]
    gate = gathered(pieces, lax.axis_index("col"), model, 2 * model)
    average = merged(listed(parts), heads)
    attended = (average * jax.nn.sigmoid(gate.astype(F32))).astype(BF16)
    update_out[...] = dot(attended, out_proj[...]).astype(BF16)


def exchanged(value, axis, flip):
    size = lax.axis_size(axis)
    return lax.ppermute(value, axis, [(index, index ^ flip) for index in range(size)])


def on_device(
    pair_block,
    query_single,
    key_single,
    query_chain,
    key_chain,
    query_mask,
    key_mask,
    timestep,
    time_table,
    norm_gain,
    left_proj,
    right_proj,
    outer_proj,
    bias_proj,
    chain_weight,
    query_proj,
    kv_proj,
    out_proj,
):
    slabs, rows, model = query_single.shape
    count = slabs * rows
    key_count = key_single.shape[0]
    heads = chain_weight.shape[0]
    channels = pair_block.shape[-1]
    rank = left_proj.shape[1]
    lanes = heads * count
    cols = lax.axis_size("col")
    direct = cols == 8
    grant = pltpu.CompilerParams(vmem_limit_bytes=16 << 20)
    now = (query_mask, query_single, time_table, norm_gain, query_proj.T)
    later = (key_single, kv_proj, key_mask.reshape(1, key_count), right_proj.T)
    shape_of = lambda array: jax.ShapeDtypeStruct(array.shape, array.dtype)
    scratch_of = lambda array: pltpu.VMEM(array.shape, array.dtype)

    query_part, query_norm, time_row, gain, *later = pl.pallas_call(
        query_kernel,
        out_shape=(
            jax.ShapeDtypeStruct((count, query_proj.shape[1]), BF16),
            jax.ShapeDtypeStruct((count, model), BF16),
            jax.ShapeDtypeStruct((1, model), F32),
            shape_of(norm_gain),
        )
        + tuple(shape_of(array) for array in later),
        in_specs=[SMEM] + [HBM] * 9,
        out_specs=[VMEM] * 8,
        scratch_shapes=[
            scratch_of(query_mask),
            scratch_of(query_single),
            scratch_of(time_table),
            scratch_of(query_proj.T),
            pltpu.SemaphoreType.DMA((9,)),
        ],
        compiler_params=grant,
        name="query",
    )(timestep, *[pltpu.with_memory_space_constraint(array, pltpu.HBM) for array in now + later])

    if direct:
        near = exchanged(query_part, "col", 1)

    half, right = pl.pallas_call(
        key_kernel,
        out_shape=(
            jax.ShapeDtypeStruct((key_count, kv_proj.shape[1]), BF16),
            jax.ShapeDtypeStruct((key_count, rank), F32),
        ),
        in_specs=[VMEM] * 6,
        out_specs=(VMEM, VMEM),
        compiler_params=grant,
        name="keys",
    )(time_row, gain, *later)
    halves = [half, exchanged(half, "row", 1)]
    if direct:
        far = exchanged(half, "col", 1)
        halves += [far, exchanged(far, "row", 1)]

    new_pair, bias = pl.pallas_call(
        pair_kernel,
        out_shape=(
            jax.ShapeDtypeStruct(pair_block.shape, F32),
            jax.ShapeDtypeStruct((key_count, lanes), F32),
        ),
        in_specs=[VMEM] * 9,
        out_specs=(HBM, VMEM),
        scratch_shapes=[
            pltpu.VMEM((count, key_count, channels), F32),
            pltpu.SemaphoreType.DMA((count,)),
        ],
        compiler_params=grant,
        name="pairs",
    )(
        chain_weight.reshape(1, heads),
        query_chain,
        query_norm,
        left_proj.T,
        outer_proj,
        bias_proj.T,
        right,
        key_chain.reshape(1, key_count),
        pair_block,
    )
    biases = [bias]

    if direct:
        both = jnp.stack([query_part, near])
        both, bias = lax.optimization_barrier((both, bias))
        biases = [bias, exchanged(bias, "col", 1)]
        pieces = [query_part, near] + [exchanged(both, "col", flip) for flip in (2, 4, 6)]
    else:
        pieces = [lax.all_gather(query_part, "col", axis=1, tiled=True)]

    def attend_body(*refs):
        n, k = len(pieces), len(halves)
        attend_kernel(refs[:n], refs[n : n + k], refs[n + k : -1], refs[-1], heads, count)

    part = pl.pallas_call(
        attend_body,
        out_shape=jax.ShapeDtypeStruct((count, model + LANES), BF16),
        in_specs=[VMEM] * (len(pieces) + len(halves) + len(biases)),
        out_specs=VMEM,
        compiler_params=grant,
        name="attend",
    )(*pieces, *halves, *biases)

    if direct:
        parts = [part] + [exchanged(part, "col", flip) for flip in (2, 4, 6)]
    else:
        parts = [lax.all_gather(part, "col")]

    def finish_body(*refs):
        n, k = len(pieces), len(parts)
        finish_kernel(refs[:n], refs[n : n + k], *refs[n + k :], heads)

    update = pl.pallas_call(
        finish_body,
        out_shape=jax.ShapeDtypeStruct((count, model), BF16),
        in_specs=[VMEM] * (len(pieces) + len(parts) + 1),
        out_specs=VMEM,
        compiler_params=grant,
        name="finish",
    )(*pieces, *parts, out_proj)
    return (new_pair, update.reshape(slabs, rows, model))


def solution(mesh):
    return jax.shard_map(
        on_device,
        mesh=mesh,
        in_specs=(
            P("grp", "row", "col", None),
            P("grp", "row", None),
            P(("grp", "col"), None),
            P("grp", "row"),
            P(("grp", "col")),
            P("grp", "row"),
            P(("grp", "col")),
            P("grp"),
            P(),
            P(),
            P(),
            P(),
            P(),
            P(),
            P(),
            P(None, "col"),
            P(None, "row"),
            P(),
        ),
        out_specs=(P("grp", "row", "col", None), P("grp", "row", None)),
        check_vma=False,
    )
```

time: 39.7 us -> 34.3 us (0.86)
  local copies, waits for them, and re-layouts: 9.14 us -> 0.05 us
  waiting for transfers between devices: 8.67 us -> 12.2 us
    unnamed x38 -> x16, local copies, waits for them, and re-layouts: 9.14 us -> 0.05 us
    ppermute x9 -> x11, waiting for transfers between devices: 8.67 us -> 12.2 us  [exchanged(): lax.ppermute(value, axis, [(index, index ^ flip) for index in range(size)])]
    pallas_call x1, Pallas kernels: 0.42 us -> 1.65 us  [on_device(): pl.pallas_call(query_kernel, out_shape=(jax.ShapeDtypeStruct((count, quer...]
    pallas_call x3 -> x2, Pallas kernels: 4.98 us -> 4.17 us  [the longest x1 2.91 us: on_device(): pl.pallas_call(pair_kernel, out_shape=(jax.ShapeDtypeStruct(pair_block.sh...]
    ppermute x9 -> x11, starting transfers between devices: 12.6 us -> 12.9 us  [exchanged(): lax.ppermute(value, axis, [(index, index ^ flip) for index in range(size)])]
  transfers between devices with their start and end apart: 9 -> 11, of which waited for: 4 -> 7; matrix products, arithmetic and copies ran while one was open for 0% -> 0% of each run, Pallas kernels for 11% -> 8%
where the time goes in v3:
time: 34.3 us; the launch traced here: 34.2 us
  starting transfers between devices  12.9 us (38%)
  waiting for transfers between devices  12.2 us (36%)
  Pallas kernels  7.59 us (22%)
  between operations  1.42 us (4%)
    ppermute x11, starting transfers between devices, exchanged(): lax.ppermute(value, axis, [(index, index ^ flip) for index in range(size)])  12.9 us
    ppermute x11, waiting for transfers between devices, exchanged(): lax.ppermute(value, axis, [(index, index ^ flip) for index in range(size)])  12.2 us
    pallas_call x1, Pallas kernels, on_device(): pl.pallas_call(pair_kernel, out_shape=(jax.ShapeDtypeStruct(pair_block.sh...  2.91 us
    pallas_call x1, Pallas kernels, on_device(): pl.pallas_call(query_kernel, out_shape=(jax.ShapeDtypeStruct((count, quer...  1.65 us
    pallas_call x1, Pallas kernels, on_device(): pl.pallas_call(attend_body, out_shape=jax.ShapeDtypeStruct((count, model...  1.26 us
    pallas_call x1, Pallas kernels, on_device(): pl.pallas_call(finish_body, out_shape=jax.ShapeDtypeStruct((count, model)...  1.12 us
  transfers between devices with their start and end apart: 11, of which 7 were waited for; matrix products, arithmetic and copies ran while one was open for 0% of the time, Pallas kernels for 8%

profile of v3, /device:TPU:0, one launch (start us, length us, event | category | flops | bytes accessed | tf_op | source)
XLA Modules:
  0.0 34.2 jit_solution(8615868045682727520)
XLA Ops:
  1.3 1.7 %query.1 = (bf16[16,192]{1,0:T(8,128)(2,1)S(1)}, bf16[16,768]{1,0:T(8,128)(2,1)S(1)}, f32[1,768]{1,0:T(1,128)S(1)}, f32[768]{0:T(1024)S(1)}, bf16[144,768]{1,0:T...) custom-call(s32[1]{0:T(128)S(6)} %copy.20.refs_0_, ...), custom_call_target="tpu_custom_call" | custom-call | tf_op jit(solution)/shard_map/query/pallas_call | solution.py:293
  2.9 0.0 copy-start
  3.0 0.0 copy-start.2
  3.0 0.0 copy-start.3
  3.0 0.0 copy-start.6
  3.0 0.0 copy-start.7
  3.0 0.7 %keys.1 = (bf16[144,768]{1,0:T(8,128)(2,1)S(1)}, f32[144,8]{1,0:T(8,128)S(1)}) custom-call(f32[1,768]{1,0:T(1,128)S(1)} %get-tuple-element.17.time_row, f32[768]{0:T(1024)S(1)} %get-tuple-element.18.gain, bf16[144,768]{1,0:T(8,128)(2,1)S(1)} %get-tuple-element.19.single, bf16[768,768]{1,0:T(8,128)(2,1)S(1)} %get-tuple-element.20.proj, ...), custom_call_target="tpu_custom_call" | custom-call | tf_op jit(solution)/shard_map/keys/pallas_call | solution.py:318
  3.7 3.0 %collective-permute-start.5 = (bf16[144,768]{1,0:T(8,128)(2,1)S(1)}, bf16[144,768]{1,0:T(8,128)(2,1)S(1)}, u32[]{:S(2)}, u32[]{:S(2)}) collective-permute-start(bf16[144,768]{1,0:T(8,128)(2,1)S(1)} %get-tuple-element.28.refs_5_), channel_id=1, source_target_pairs={{0,2},{2,0},{4,6},{6,4},{8,10},{10,8},{12,14},{14,12},{1,3},{3,1},... | collective-permute-start | bytes 663560 | tf_op jit(solution)/shard_map/ppermute | solution.py:255
  6.7 0.1 collective-permute-start
  6.9 0.0 copy-start.1
  6.9 2.9 %pairs.1 = (f32[2,8,144,128]{3,2,1,0:T(8,128)}, f32[144,192]{1,0:T(8,128)S(1)}) custom-call(f32[1,12]{1,0:T(1,128)S(1)} %bitcast.15, s32[2,8]{1,0:T(2,128)S(1)} %copy-done.5, bf16[16,768]{1,0:T(8,128)(2,1)S(1)} %get-tuple-element.16.query_norm, bf16[8,768]{1,0:T(8,128)(2,1)S(1)} %bitcast.12, bf16[64,128]{1,0:T(8,128)(2,1)S(1)} %copy-done.2, ...), custom_call_target="tpu_custom_call" | custom-call | tf_op jit(solution)/shard_map/pairs/pallas_call | solution.py:334
  9.8 2.4 %collective-permute-done.5.refs_7_ = bf16[144,768]{1,0:T(8,128)(2,1)S(1)} collective-permute-done((bf16[144,768]{1,0:T(8,128)(2,1)S(1)}, bf16[144,768]{1,0:T(8,128)(2,1)S(1)}, u32[]{:S(2)}, u32[]{:S(2)}) %collective-permute-start.5) | collective-permute-done | bytes 221216 | tf_op jit(solution)/shard_map/ppermute | solution.py:255
  12.2 0.1 collective-permute-done.refs_1_
  12.3 1.8 %collective-permute-start.7 = (f32[144,192]{1,0:T(8,128)S(1)}, f32[144,192]{1,0:T(8,128)S(1)}, u32[]{:S(2)}, u32[]{:S(2)}) collective-permute-start(f32[144,192]{1,0:T(8,128)S(1)} %get-tuple-element.29.refs_9_), channel_id=1, source_target_pairs={{0,2},{2,0},{4,6},{6,4},{8,10},{10,8},{12,14},{14,12},{1,3},{3,1},... | collective-permute-start | bytes 331784 | tf_op jit(solution)/shard_map/ppermute | solution.py:255
  14.1 3.6 %collective-permute-start.3 = (bf16[2,16,192]{2,1,0:T(8,128)(2,1)S(1)}, bf16[2,16,192]{2,1,0:T(8,128)(2,1)S(1)}, u32[]{:S(2)}, u32[]{:S(2)}) collective-permute-start(bf16[2,16,192]{2,1,0:T(8,128)(2,1)S(1)} %pad_maximum_fusion), channel_id=1, source_target_pairs={{0,12},{2,14},{4,8},{6,10},{8,4},{10,6},{12,0},{14,2},{1,13},{3,15... | collective-permute-start | bytes 36872 | tf_op jit(solution)/shard_map/ppermute | solution.py:255
  17.7 1.9 %collective-permute-done.3.refs_4_ = bf16[2,16,192]{2,1,0:T(8,128)(2,1)S(1)} collective-permute-done((bf16[2,16,192]{2,1,0:T(8,128)(2,1)S(1)}, bf16[2,16,192]{2,1,0:T(8,128)(2,1)S(1)}, u32[]{:S(2)}, u32[]{:S(2)}) %collective-permute-start.3) | collective-permute-done | bytes 12320 | tf_op jit(solution)/shard_map/ppermute | solution.py:255
  19.7 2.7 %collective-permute-done.2.refs_3_ = bf16[2,16,192]{2,1,0:T(8,128)(2,1)S(1)} collective-permute-done((bf16[2,16,192]{2,1,0:T(8,128)(2,1)S(1)}, bf16[2,16,192]{2,1,0:T(8,128)(2,1)S(1)}, u32[]{:S(2)}, u32[]{:S(2)}) %collective-permute-start.2) | collective-permute-done | bytes 12320 | tf_op jit(solution)/shard_map/ppermute | solution.py:255
  22.4 1.0 %collective-permute-done.1.refs_2_ = bf16[2,16,192]{2,1,0:T(8,128)(2,1)S(1)} collective-permute-done((bf16[2,16,192]{2,1,0:T(8,128)(2,1)S(1)}, bf16[2,16,192]{2,1,0:T(8,128)(2,1)S(1)}, u32[]{:S(2)}, u32[]{:S(2)}) %collective-permute-start.1) | collective-permute-done | bytes 12320 | tf_op jit(solution)/shard_map/ppermute | solution.py:255
  23.4 1.3 %attend.1.refs_5_ = bf16[16,896]{1,0:T(8,128)(2,1)S(1)} custom-call(bf16[16,192]{1,0:T(8,128)(2,1)S(1)} %get-tuple-element.25.refs_0_, bf16[16,192]{1,0:T(8,128)(2,1)S(1)} %collective-permute-done.refs_1_, bf16[2,16,192]{2,1,0:T(8,128)(2,1)S(1)} %collective-permute-done.1.refs_2_, bf16[2,16,192]{2,1,0:T(8,128)(2,1)S(1)} %collective-permute-done.2.refs_3_, ...), custom_call_target="tpu_custom_call" | custom-call | tf_op jit(solution)/shard_map/attend/pallas_call | solution.py:373
  24.7 3.6 %collective-permute-start.10 = (bf16[16,896]{1,0:T(8,128)(2,1)S(1)}, bf16[16,896]{1,0:T(8,128)(2,1)S(1)}, u32[]{:S(2)}, u32[]{:S(2)}) collective-permute-start(bf16[16,896]{1,0:T(8,128)(2,1)S(1)} %attend.1.refs_5_), channel_id=1, source_target_pairs={{0,12},{2,14},{4,8},{6,10},{8,4},{10,6},{12,0},{14,2},{1,13},{3,15... | collective-permute-start | bytes 86024 | tf_op jit(solution)/shard_map/ppermute | solution.py:255
  28.3 0.8 %collective-permute-start.8 = (bf16[16,896]{1,0:T(8,128)(2,1)S(1)}, bf16[16,896]{1,0:T(8,128)(2,1)S(1)}, u32[]{:S(2)}, u32[]{:S(2)}) collective-permute-start(bf16[16,896]{1,0:T(8,128)(2,1)S(1)} %attend.1.refs_5_), channel_id=1, source_target_pairs={{0,4},{2,6},{4,0},{6,2},{8,12},{10,14},{12,8},{14,10},{1,5},{3,7},... | collective-permute-start | bytes 86024 | tf_op jit(solution)/shard_map/ppermute | solution.py:255
  29.1 1.3 %collective-permute-done.10.refs_8_ = bf16[16,896]{1,0:T(8,128)(2,1)S(1)} collective-permute-done((bf16[16,896]{1,0:T(8,128)(2,1)S(1)}, bf16[16,896]{1,0:T(8,128)(2,1)S(1)}, u32[]{:S(2)}, u32[]{:S(2)}) %collective-permute-start.10) | collective-permute-done | bytes 28704 | tf_op jit(solution)/shard_map/ppermute | solution.py:255
  30.4 2.7 %collective-permute-done.9.refs_7_ = bf16[16,896]{1,0:T(8,128)(2,1)S(1)} collective-permute-done((bf16[16,896]{1,0:T(8,128)(2,1)S(1)}, bf16[16,896]{1,0:T(8,128)(2,1)S(1)}, u32[]{:S(2)}, u32[]{:S(2)}) %collective-permute-start.9) | collective-permute-done | bytes 28704 | tf_op jit(solution)/shard_map/ppermute | solution.py:255
  33.0 1.1 %finish.1 = bf16[16,768]{1,0:T(8,128)(2,1)} custom-call(bf16[16,192]{1,0:T(8,128)(2,1)S(1)} %get-tuple-element.25.refs_0_, bf16[16,192]{1,0:T(8,128)(2,1)S(1)} %collective-permute-done.refs_1_, bf16[2,16,192]{2,1,0:T(8,128)(2,1)S(1)} %collective-permute-done.1.refs_2_, bf16[2,16,192]{2,1,0:T(8,128)(2,1)S(1)} %collective-permute-done.2.refs_3_, ...), custom_call_target="tpu_custom_call" | custom-call | tf_op jit(solution)/shard_map/finish/pallas_call | solution.py:391
  (20 shorter events, 0.1 us)
Async XLA Ops:
  2.9 3.9 %copy-start = (f32[2,8,144,128]{3,2,1,0:T(8,128)S(1)}, f32[2,8,144,128]{3,2,1,0:T(8,128)}, u32[]{:S(2)}) copy-start(f32[2,8,144,128]{3,2,1,0:T(8,128)} %pair.1) | copy-start | bytes 3538948
  3.0 3.9 %copy-start.2 = (bf16[64,128]{1,0:T(8,128)(2,1)S(1)}, bf16[64,128]{1,0:T(8,128)(2,1)}, u32[]{:S(2)}) copy-start(bf16[64,128]{1,0:T(8,128)(2,1)} %outer_proj.1) | copy-start | bytes 49156
  3.0 3.8 %copy-start.3 = (bf16[768,8]{0,1:T(8,128)(2,1)S(1)}, bf16[768,8]{0,1:T(8,128)(2,1)}, u32[]{:S(2)}) copy-start(bf16[768,8]{0,1:T(8,128)(2,1)} %param.28) | copy-start | bytes 36868
  3.0 3.8 %copy-start.4 = (f32[128,12]{0,1:T(8,128)S(1)}, f32[128,12]{0,1:T(8,128)}, u32[]{:S(2)}) copy-start(f32[128,12]{0,1:T(8,128)} %param.31) | copy-start | bytes 18436
  3.0 3.8 %copy-start.5 = (s32[2,8]{1,0:T(2,128)S(1)}, s32[2,8]{1,0:T(2,128)}, u32[]{:S(2)}) copy-start(s32[2,8]{1,0:T(2,128)} %query_chain.1) | copy-start | bytes 196
  3.0 3.8 %copy-start.6 = (s32[144]{0:T(256)S(1)}, s32[144]{0:T(256)}, u32[]{:S(2)}) copy-start(s32[144]{0:T(256)} %param.22) | copy-start | bytes 1732
  3.0 3.8 %copy-start.7 = (f32[12]{0:T(128)S(1)}, f32[12]{0:T(128)}, u32[]{:S(2)}) copy-start(f32[12]{0:T(128)} %param.32) | copy-start | bytes 148
  3.7 8.6 %collective-permute-start.5 = (bf16[144,768]{1,0:T(8,128)(2,1)S(1)}, bf16[144,768]{1,0:T(8,128)(2,1)S(1)}, u32[]{:S(2)}, u32[]{:S(2)}) collective-permute-start(bf16[144,768]{1,0:T(8,128)(2,1)S(1)} %get-tuple-element.28.refs_5_), channel_id=1, source_target_pairs={{0,2},{2,0},{4,6},{6,4},{8,10},{10,8},{12,14},{14,12},{1,3},{3,1},... | collective-permute-start | bytes 663560 | tf_op jit(solution)/shard_map/ppermute | solution.py:255
  6.7 5.6 %collective-permute-start = (bf16[16,192]{1,0:T(8,128)(2,1)S(1)}, bf16[16,192]{1,0:T(8,128)(2,1)S(1)}, u32[]{:S(2)}, u32[]{:S(2)}) collective-permute-start(bf16[16,192]{1,0:T(8,128)(2,1)S(1)} %get-tuple-element.25.refs_0_), channel_id=1, source_target_pairs={{0,2},{2,0},{4,6},{6,4},{8,10},{10,8},{12,14},{14,12},{1,3},{3,1},... | collective-permute-start | bytes 18440 | tf_op jit(solution)/shard_map/ppermute | solution.py:255
  6.8 16.6 %collective-permute-start.4 = (bf16[144,768]{1,0:T(8,128)(2,1)S(1)}, bf16[144,768]{1,0:T(8,128)(2,1)S(1)}, u32[]{:S(2)}, u32[]{:S(2)}) collective-permute-start(bf16[144,768]{1,0:T(8,128)(2,1)S(1)} %get-tuple-element.28.refs_5_), channel_id=1, source_target_pairs={{0,1},{1,0},{2,3},{3,2},{4,5},{5,4},{6,7},{7,6},{8,9},{9,8},{10,11... | collective-permute-start | bytes 663560 | tf_op jit(solution)/shard_map/ppermute | solution.py:255
  6.9 26.2 %copy-start.1 = (bf16[768,768]{1,0:T(8,128)(2,1)S(1)}, bf16[768,768]{1,0:T(8,128)(2,1)}, u32[]{:S(2)}) copy-start(bf16[768,768]{1,0:T(8,128)(2,1)} %refs_9_.1) | copy-start | bytes 3538948
  12.2 11.2 %collective-permute-start.6 = (bf16[144,768]{1,0:T(8,128)(2,1)S(1)}, bf16[144,768]{1,0:T(8,128)(2,1)S(1)}, u32[]{:S(2)}, u32[]{:S(2)}) collective-permute-start(bf16[144,768]{1,0:T(8,128)(2,1)S(1)} %collective-permute-done.5.refs_7_), channel_id=1, source_target_pairs={{0,1},{1,0},{2,3},{3,2},{4,5},{5,4},{6,7},{7,6},{8,9},{9,8},{10,11... | collective-permute-start | bytes 663560 | tf_op jit(solution)/shard_map/ppermute | solution.py:255
  12.3 11.1 %collective-permute-start.7 = (f32[144,192]{1,0:T(8,128)S(1)}, f32[144,192]{1,0:T(8,128)S(1)}, u32[]{:S(2)}, u32[]{:S(2)}) collective-permute-start(f32[144,192]{1,0:T(8,128)S(1)} %get-tuple-element.29.refs_9_), channel_id=1, source_target_pairs={{0,2},{2,0},{4,6},{6,4},{8,10},{10,8},{12,14},{14,12},{1,3},{3,1},... | collective-permute-start | bytes 331784 | tf_op jit(solution)/shard_map/ppermute | solution.py:255
  14.1 5.5 %collective-permute-start.3 = (bf16[2,16,192]{2,1,0:T(8,128)(2,1)S(1)}, bf16[2,16,192]{2,1,0:T(8,128)(2,1)S(1)}, u32[]{:S(2)}, u32[]{:S(2)}) collective-permute-start(bf16[2,16,192]{2,1,0:T(8,128)(2,1)S(1)} %pad_maximum_fusion), channel_id=1, source_target_pairs={{0,12},{2,14},{4,8},{6,10},{8,4},{10,6},{12,0},{14,2},{1,13},{3,15... | collective-permute-start | bytes 36872 | tf_op jit(solution)/shard_map/ppermute | solution.py:255
  17.7 4.6 %collective-permute-start.2 = (bf16[2,16,192]{2,1,0:T(8,128)(2,1)S(1)}, bf16[2,16,192]{2,1,0:T(8,128)(2,1)S(1)}, u32[]{:S(2)}, u32[]{:S(2)}) collective-permute-start(bf16[2,16,192]{2,1,0:T(8,128)(2,1)S(1)} %pad_maximum_fusion), channel_id=1, source_target_pairs={{0,8},{2,10},{4,12},{6,14},{8,0},{10,2},{12,4},{14,6},{1,9},{3,11}... | collective-permute-start | bytes 36872 | tf_op jit(solution)/shard_map/ppermute | solution.py:255
  19.7 3.7 %collective-permute-start.1 = (bf16[2,16,192]{2,1,0:T(8,128)(2,1)S(1)}, bf16[2,16,192]{2,1,0:T(8,128)(2,1)S(1)}, u32[]{:S(2)}, u32[]{:S(2)}) collective-permute-start(bf16[2,16,192]{2,1,0:T(8,128)(2,1)S(1)} %pad_maximum_fusion), channel_id=1, source_target_pairs={{0,4},{2,6},{4,0},{6,2},{8,12},{10,14},{12,8},{14,10},{1,5},{3,7},... | collective-permute-start | bytes 36872 | tf_op jit(solution)/shard_map/ppermute | solution.py:255
  24.7 5.7 %collective-permute-start.10 = (bf16[16,896]{1,0:T(8,128)(2,1)S(1)}, bf16[16,896]{1,0:T(8,128)(2,1)S(1)}, u32[]{:S(2)}, u32[]{:S(2)}) collective-permute-start(bf16[16,896]{1,0:T(8,128)(2,1)S(1)} %attend.1.refs_5_), channel_id=1, source_target_pairs={{0,12},{2,14},{4,8},{6,10},{8,4},{10,6},{12,0},{14,2},{1,13},{3,15... | collective-permute-start | bytes 86024 | tf_op jit(solution)/shard_map/ppermute | solution.py:255
  28.3 4.8 %collective-permute-start.9 = (bf16[16,896]{1,0:T(8,128)(2,1)S(1)}, bf16[16,896]{1,0:T(8,128)(2,1)S(1)}, u32[]{:S(2)}, u32[]{:S(2)}) collective-permute-start(bf16[16,896]{1,0:T(8,128)(2,1)S(1)} %attend.1.refs_5_), channel_id=1, source_target_pairs={{0,8},{2,10},{4,12},{6,14},{8,0},{10,2},{12,4},{14,6},{1,9},{3,11}... | collective-permute-start | bytes 86024 | tf_op jit(solution)/shard_map/ppermute | solution.py:255
  28.3 4.8 %collective-permute-start.8 = (bf16[16,896]{1,0:T(8,128)(2,1)S(1)}, bf16[16,896]{1,0:T(8,128)(2,1)S(1)}, u32[]{:S(2)}, u32[]{:S(2)}) collective-permute-start(bf16[16,896]{1,0:T(8,128)(2,1)S(1)} %attend.1.refs_5_), channel_id=1, source_target_pairs={{0,4},{2,6},{4,0},{6,2},{8,12},{10,14},{12,8},{14,10},{1,5},{3,7},... | collective-permute-start | bytes 86024 | tf_op jit(solution)/shard_map/ppermute | solution.py:255

commit v4 on v3

--- a/solution.py
+++ b/solution.py
@@ -13,6 +13,7 @@
 HIGHEST = lax.Precision.HIGHEST
 LANES = 128
 TERM = LANES // 5
+GROUP = 4
 VMEM = pl.BlockSpec(memory_space=pltpu.VMEM)
 HBM = pl.BlockSpec(memory_space=pltpu.HBM)
 SMEM = pl.BlockSpec(memory_space=pltpu.SMEM)
@@ -110,6 +111,7 @@
     pair,
     pair_out,
     bias_out,
+    terms_out,
     fresh_scratch,
     sems,
 ):
@@ -128,32 +130,42 @@
     tall = jnp.where(iota(spot, 0) % rank == iota(spot, 1) % rank, tall, 0.0)
     mixer = dot(tall, outer_proj[...].astype(F32), HIGHEST).reshape(count, rank, channels)
     high, low = (part.astype(F32) for part in split(mixer))
-    mixer = jnp.concatenate([high, high, low], axis=1).astype(BF16)
+    mixer = jnp.concatenate([high, high, low, jnp.zeros_like(low)], axis=1).astype(BF16)
     high, low = (part.astype(F32) for part in split(right[...]))
-    spread = jnp.concatenate([high, low, high], axis=1).astype(BF16)
-    spot = (heads, lanes)
-    expand = iota(spot, 1) // count == iota(spot, 0)
+    spread = jnp.concatenate([high, low, high, jnp.zeros_like(low)], axis=1).astype(BF16)
+    head_of = iota((1, lanes), 1) // count
+    row_of = iota((1, lanes), 1) - head_of * count
+    expand = head_of == iota((heads, lanes), 0)
     high, low = split(dot_tn(bias_proj[...], expand.astype(F32), HIGHEST))
     weights = jnp.concatenate([high, high, low], axis=0)
     apart = jnp.sum(jnp.where(expand, column_of(chain_weight[...]), 0.0), axis=0, keepdims=True)
-    spot = (count, lanes)
-    chains = jnp.where(iota(spot, 1) % count == iota(spot, 0), rows_column(query_chain[...]), 0)
+    chains = jnp.where(row_of == iota((count, lanes), 0), rows_column(query_chain[...]), 0)
     chains = jnp.sum(chains, axis=0, keepdims=True)
-    total = jnp.where(column_of(key_chain[...]) != chains, apart, 0.0)
-    lane = iota((key_count, lanes), 1) % count
     bias = jnp.zeros((key_count, lanes), F32)
     copies = []
-    for index in range(count):
-        spot = (index // rows, index % rows)
-        fresh = pair[spot] + dot(spread, mixer[index])
-        fresh_scratch[index] = fresh
-        copy = pltpu.make_async_copy(fresh_scratch.at[index], pair_out.at[spot], sems.at[index])
-        copy.start()
-        copies.append(copy)
-        high, low = split(fresh)
-        here = dot(jnp.concatenate([high, low, high], axis=1), weights)
-        bias = jnp.where(lane == index, here, bias)
-    bias_out[...] = bias + total
+    for start in range(0, count, GROUP):
+        indices = range(start, start + GROUP)
+        updates = dot(spread, jnp.concatenate([mixer[index] for index in indices], axis=1))
+        terms = []
+        for index in indices:
+            spot = (index // rows, index % rows)
+            place = (index - start) * channels
+            fresh = pair[spot] + updates[:, place : place + channels]
+            fresh_scratch[index] = fresh
+            copy = pltpu.make_async_copy(fresh_scratch.at[index], pair_out.at[spot], sems.at[index])
+            copy.start()
+            copies.append(copy)
+            high, low = split(fresh)
+            terms.append(jnp.concatenate([high, low, high], axis=1))
+        here = dot(jnp.concatenate(terms, axis=0), weights)
+        for index in indices:
+            place = (index - start) * key_count
+            bias = jnp.where(row_of == index, here[place : place + key_count], bias)
+    bias = bias + jnp.where(column_of(key_chain[...]) != chains, apart, 0.0)
+    bias_out[...] = bias
+    high, low = split(bias)
+    terms_out[:key_count] = high
+    terms_out[key_count:] = low
     for copy in copies:
         copy.wait()
 
@@ -165,11 +177,17 @@
     return values
 
 
-def gathered(pieces, col, start, stop):
-    values = listed(pieces)
-    if len(values) == 1:
-        return values[0][:, start:stop]
-    share = values[0].shape[1]
+def gathered(pieces, start, stop):
+    if len(pieces) == 1:
+        return pieces[0][:, start:stop]
+    col = lax.axis_index("col")
+    ours = listed(pieces[:3])
+    count, share = ours[0].shape
+    message = pieces[3]
+    base = message.shape[0] - len(ours) * count
+    values = []
+    for index, value in enumerate(ours):
+        values += [value, message[base + index * count : base + (index + 1) * count]]
     blocks = []
     for target in range(start // share, stop // share):
         chosen = values[0]
@@ -179,40 +197,46 @@
     return jnp.concatenate(blocks, axis=1)
 
 
-def attend_kernel(pieces, halves, biases, part_out, heads, count):
-    col, row = lax.axis_index("col"), lax.axis_index("row")
-    model = halves[0].shape[1]
+def attend_kernel(pieces, halves, bias_ref, part_out, heads, count):
+    row = lax.axis_index("row")
+    key_count, model = halves[0].shape
     head = model // heads
     lanes = heads * count
-    query = gathered(pieces, col, 0, model)
+    query = gathered(pieces, 0, model)
+    biases = [bias_ref[...]]
+    if len(pieces) > 1:
+        message = pieces[3]
+        biases.append(
+            message[:key_count].astype(F32) + message[key_count : 2 * key_count].astype(F32)
+        )
     firsts = [ref[...] for ref in halves[::2]]
     seconds = [ref[...] for ref in halves[1::2]]
     keys = [jnp.where(row == 0, first, second) for first, second in zip(firsts, seconds)]
     values = [jnp.where(row == 0, second, first) for first, second in zip(firsts, seconds)]
-    lane = iota((count, model), 1)
+    head_of = iota((1, model), 1) // head
     spread = jnp.concatenate(
-        [jnp.where(lane // head == index, query, jnp.zeros_like(query)) for index in range(heads)],
+        [jnp.where(head_of == index, query, jnp.zeros_like(query)) for index in range(heads)],
         axis=0,
     )
     scale = 1.0 / math.sqrt(head)
-    scores = [dot_nt(key, spread) * scale + bias[...] for key, bias in zip(keys, biases)]
+    scores = [dot_nt(key, spread) * scale + bias for key, bias in zip(keys, biases)]
     peak = functools.reduce(jnp.maximum, [jnp.max(score, axis=0, keepdims=True) for score in scores])
     exponents = [jnp.exp(score - peak) for score in scores]
     total = sum(jnp.sum(exponent, axis=0, keepdims=True) for exponent in exponents)
     weights = jnp.concatenate([exponent.astype(BF16) for exponent in exponents], axis=0)
     summed = dot_tn(weights, jnp.concatenate(values, axis=0))
-    taken = jnp.zeros((count, model), F32)
-    for index in range(heads):
-        taken = jnp.where(lane // head == index, summed[index * count : (index + 1) * count], taken)
+    taken = summed[:count]
+    for index in range(1, heads):
+        taken = jnp.where(head_of == index, summed[index * count : (index + 1) * count], taken)
     part_out[:, :model] = taken.astype(BF16)
-    spot = (count, lanes)
-    keep = iota(spot, 1) % count == iota(spot, 0)
-    terms = terms_of(peak, 3) + terms_of(total, 2)
-    rows = jnp.concatenate([jnp.where(keep, term, 0.0).astype(BF16) for term in terms], axis=1)
-    spot = (len(terms) * lanes, LANES)
-    source = iota(spot, 0)
-    target = source // lanes * TERM + source % lanes // count
-    part_out[:, model:] = dot(rows, (target == iota(spot, 1)).astype(BF16)).astype(BF16)
+    row_of = iota((1, lanes), 1) % count
+    keep = row_of == iota((count, lanes), 0)
+    source = iota((lanes, 1), 0) // count
+    stats = jnp.zeros((count, LANES), F32)
+    for index, term in enumerate(terms_of(peak, 3) + terms_of(total, 2)):
+        target = (source + index * TERM == iota((lanes, LANES), 1)).astype(BF16)
+        stats = stats + dot(jnp.where(keep, term, 0.0).astype(BF16), target)
+    part_out[:, model:] = stats.astype(BF16)
 
 
 def terms_of(value, count):
@@ -227,26 +251,39 @@
 def merged(parts, heads):
     model = parts[0].shape[1] - LANES
     count = parts[0].shape[0]
-    spot = (LANES, model)
-    term, place = iota(spot, 0), iota(spot, 1) // (model // heads)
-    ours = term % TERM == place
-    for_peak = (ours & (term // TERM < 3)).astype(BF16)
-    for_total = (ours & (term // TERM >= 3) & (term // TERM < 5)).astype(BF16)
+    term = iota((LANES, 1), 0)
+    place = iota((1, model), 1) // (model // heads)
+    kind = term // TERM
+    wanted = term - kind * TERM
+    for_peak = (jnp.where(kind < 3, wanted, -1) == place).astype(BF16)
+    for_total = (jnp.where((kind >= 3) & (kind < 5), wanted, -1) == place).astype(BF16)
     stats = jnp.concatenate([part[:, model:] for part in parts], axis=0)
     peaks, totals = dot(stats, for_peak), dot(stats, for_total)
     cut = lambda array, index: array[index * count : (index + 1) * count]
-    peak = functools.reduce(jnp.maximum, [cut(peaks, index) for index in range(len(parts))])
+    peak = tree(jnp.maximum, [cut(peaks, index) for index in range(len(parts))])
     scales = [jnp.exp(cut(peaks, index) - peak) for index in range(len(parts))]
-    total = sum(scale * cut(totals, index) for index, scale in enumerate(scales))
-    summed = sum(scale * part[:, :model].astype(F32) for scale, part in zip(scales, parts))
+    total = tree(jnp.add, [scale * cut(totals, index) for index, scale in enumerate(scales)])
+    summed = tree(jnp.add, [scale * part[:, :model].astype(F32) for scale, part in zip(scales, parts)])
     return summed / total
 
 
-def finish_kernel(pieces, parts, out_proj, update_out, heads):
-    model = out_proj.shape[0]
-    gate = gathered(pieces, lax.axis_index("col"), model, 2 * model)
-    average = merged(listed(parts), heads)
-    attended = (average * jax.nn.sigmoid(gate.astype(F32))).astype(BF16)
+def tree(combine, values):
+    while len(values) > 1:
+        values = [
+            combine(*values[index : index + 2]) if index + 1 < len(values) else values[index]
+            for index in range(0, len(values), 2)
+        ]
+    return values[0]
+
+
+def gate_kernel(*refs):
+    pieces, gate_out = refs[:-1], refs[-1]
+    model = gate_out.shape[1]
+    gate_out[...] = jax.nn.sigmoid(gathered(pieces, model, 2 * model).astype(F32))
+
+
+def finish_kernel(gate, parts, out_proj, update_out, heads):
+    attended = (merged(listed(parts), heads) * gate[...]).astype(BF16)
     update_out[...] = dot(attended, out_proj[...]).astype(BF16)
 
 
@@ -313,7 +350,7 @@
     )(timestep, *[pltpu.with_memory_space_constraint(array, pltpu.HBM) for array in now + later])
 
     if direct:
-        near = exchanged(query_part, "col", 1)
+        beside = exchanged(query_part, "col", 2)
 
     half, right = pl.pallas_call(
         key_kernel,
@@ -331,14 +368,15 @@
         far = exchanged(half, "col", 1)
         halves += [far, exchanged(far, "row", 1)]
 
-    new_pair, bias = pl.pallas_call(
+    new_pair, bias, terms = pl.pallas_call(
         pair_kernel,
         out_shape=(
             jax.ShapeDtypeStruct(pair_block.shape, F32),
             jax.ShapeDtypeStruct((key_count, lanes), F32),
+            jax.ShapeDtypeStruct((2 * key_count, lanes), BF16),
         ),
         in_specs=[VMEM] * 9,
-        out_specs=(HBM, VMEM),
+        out_specs=(HBM, VMEM, VMEM),
         scratch_shapes=[
             pltpu.VMEM((count, key_count, channels), F32),
             pltpu.SemaphoreType.DMA((count,)),
@@ -356,46 +394,51 @@
         key_chain.reshape(1, key_count),
         pair_block,
     )
-    biases = [bias]
-
     if direct:
-        both = jnp.stack([query_part, near])
-        both, bias = lax.optimization_barrier((both, bias))
-        biases = [bias, exchanged(bias, "col", 1)]
-        pieces = [query_part, near] + [exchanged(both, "col", flip) for flip in (2, 4, 6)]
+        far = exchanged(jnp.stack([query_part, beside]), "col", 4)
+        message = jnp.concatenate([terms, query_part, beside, far[0], far[1]], axis=0)
+        pieces = [query_part, beside, far, exchanged(message, "col", 1)]
     else:
         pieces = [lax.all_gather(query_part, "col", axis=1, tiled=True)]
 
     def attend_body(*refs):
-        n, k = len(pieces), len(halves)
-        attend_kernel(refs[:n], refs[n : n + k], refs[n + k : -1], refs[-1], heads, count)
+        n = len(pieces)
+        attend_kernel(refs[:n], refs[n:-2], *refs[-2:], heads, count)
 
     part = pl.pallas_call(
         attend_body,
         out_shape=jax.ShapeDtypeStruct((count, model + LANES), BF16),
-        in_specs=[VMEM] * (len(pieces) + len(halves) + len(biases)),
+        in_specs=[VMEM] * (len(pieces) + len(halves) + 1),
         out_specs=VMEM,
         compiler_params=grant,
         name="attend",
-    )(*pieces, *halves, *biases)
+    )(*pieces, *halves, bias)
 
     if direct:
         parts = [part] + [exchanged(part, "col", flip) for flip in (2, 4, 6)]
     else:
         parts = [lax.all_gather(part, "col")]
 
-    def finish_body(*refs):
-        n, k = len(pieces), len(parts)
-        finish_kernel(refs[:n], refs[n : n + k], *refs[n + k :], heads)
+    gate = pl.pallas_call(
+        gate_kernel,
+        out_shape=jax.ShapeDtypeStruct((count, model), F32),
+        in_specs=[VMEM] * len(pieces),
+        out_specs=VMEM,
+        compiler_params=grant,
+        name="gate",
+    )(*pieces)
+
+    def finish_body(gate, *refs):
+        finish_kernel(gate, refs[:-2], *refs[-2:], heads)
 
     update = pl.pallas_call(
         finish_body,
         out_shape=jax.ShapeDtypeStruct((count, model), BF16),
-        in_specs=[VMEM] * (len(pieces) + len(parts) + 1),
+        in_specs=[VMEM] * (len(parts) + 2),
         out_specs=VMEM,
         compiler_params=grant,
         name="finish",
-    )(*pieces, *parts, out_proj)
+    )(gate, *parts, out_proj)
     return (new_pair, update.reshape(slabs, rows, model))
 
 

time: 34.3 us -> 34.1 us (level)
  waiting for transfers between devices: 12.2 us -> 13.3 us
  Pallas kernels: 7.59 us -> 6.76 us
  starting transfers between devices: 12.9 us -> 12.3 us
    ppermute x11 -> x9, waiting for transfers between devices: 12.2 us -> 13.3 us  [exchanged(): lax.ppermute(value, axis, [(index, index ^ flip) for index in range(size)])]
    ppermute x11 -> x9, starting transfers between devices: 12.9 us -> 12.3 us  [exchanged(): lax.ppermute(value, axis, [(index, index ^ flip) for index in range(size)])]
    pallas_call x1, Pallas kernels: 2.91 us -> 2.39 us  [on_device(): pl.pallas_call(pair_kernel, out_shape=(jax.ShapeDtypeStruct(pair_block.sh...]
    pallas_call x1, Pallas kernels: 1.26 us -> 0.88 us  [on_device(): pl.pallas_call(attend_body, out_shape=jax.ShapeDtypeStruct((count, model...]
  transfers between devices with their start and end apart: 11 -> 9, of which waited for: 7 -> 4; matrix products, arithmetic and copies ran while one was open for 0% -> 0% of each run, Pallas kernels for 8% -> 7%
where the time goes in v4:
time: 34.1 us; the launch traced here: 33.9 us
  waiting for transfers between devices  13.3 us (39%)
  starting transfers between devices  12.3 us (36%)
  Pallas kernels  6.76 us (20%)
  between operations  1.47 us (4%)
    ppermute x9, waiting for transfers between devices, exchanged(): lax.ppermute(value, axis, [(index, index ^ flip) for index in range(size)])  13.3 us
    ppermute x9, starting transfers between devices, exchanged(): lax.ppermute(value, axis, [(index, index ^ flip) for index in range(size)])  12.3 us
    pallas_call x1, Pallas kernels, on_device(): pl.pallas_call(pair_kernel, out_shape=(jax.ShapeDtypeStruct(pair_block.sh...  2.39 us
    pallas_call x1, Pallas kernels, on_device(): pl.pallas_call(query_kernel, out_shape=(jax.ShapeDtypeStruct((count, quer...  1.65 us
    pallas_call x1, Pallas kernels, on_device(): pl.pallas_call(finish_body, out_shape=jax.ShapeDtypeStruct((count, model)...  1.09 us
    pallas_call x1, Pallas kernels, on_device(): pl.pallas_call(attend_body, out_shape=jax.ShapeDtypeStruct((count, model...  0.88 us
  transfers between devices with their start and end apart: 9, of which 4 were waited for; matrix products, arithmetic and copies ran while one was open for 0% of the time, Pallas kernels for 7%

profile of v4, /device:TPU:0, one launch (start us, length us, event | category | flops | bytes accessed | tf_op | source)
XLA Modules:
  0.0 33.9 jit_solution(55714749028079736)
XLA Ops:
  1.3 1.7 %query.1 = (bf16[16,192]{1,0:T(8,128)(2,1)S(1)}, bf16[16,768]{1,0:T(8,128)(2,1)S(1)}, f32[1,768]{1,0:T(1,128)S(1)}, f32[768]{0:T(1024)S(1)}, bf16[144,768]{1,0:T...) custom-call(s32[1]{0:T(128)S(6)} %copy.24.refs_0_, ...), custom_call_target="tpu_custom_call" | custom-call | tf_op jit(solution)/shard_map/query/pallas_call | solution.py:330
  2.9 0.0 copy-start
  3.0 0.0 copy-start.2
  3.0 0.0 copy-start.3
  3.0 0.0 copy-start.4
  3.0 0.0 copy-start.6
  3.0 0.0 copy-start.7
  3.0 0.7 %keys.1 = (bf16[144,768]{1,0:T(8,128)(2,1)S(1)}, f32[144,8]{1,0:T(8,128)S(1)}) custom-call(f32[1,768]{1,0:T(1,128)S(1)} %get-tuple-element.16.time_row, f32[768]{0:T(1024)S(1)} %get-tuple-element.17.gain, bf16[144,768]{1,0:T(8,128)(2,1)S(1)} %get-tuple-element.18.single, bf16[768,768]{1,0:T(8,128)(2,1)S(1)} %get-tuple-element.19.proj, ...), custom_call_target="tpu_custom_call" | custom-call | tf_op jit(solution)/shard_map/keys/pallas_call | solution.py:355
  3.7 3.0 %collective-permute-start.4 = (bf16[144,768]{1,0:T(8,128)(2,1)S(1)}, bf16[144,768]{1,0:T(8,128)(2,1)S(1)}, u32[]{:S(2)}, u32[]{:S(2)}) collective-permute-start(bf16[144,768]{1,0:T(8,128)(2,1)S(1)} %get-tuple-element.26.refs_4_), channel_id=1, source_target_pairs={{0,2},{2,0},{4,6},{6,4},{8,10},{10,8},{12,14},{14,12},{1,3},{3,1},... | collective-permute-start | bytes 663560 | tf_op jit(solution)/shard_map/ppermute | solution.py:292
  6.7 1.6 %collective-permute-start = (bf16[16,192]{1,0:T(8,128)(2,1)S(1)}, bf16[16,192]{1,0:T(8,128)(2,1)S(1)}, u32[]{:S(2)}, u32[]{:S(2)}) collective-permute-start(bf16[16,192]{1,0:T(8,128)(2,1)S(1)} %get-tuple-element.24.refs_0_), channel_id=1, source_target_pairs={{0,4},{2,6},{4,0},{6,2},{8,12},{10,14},{12,8},{14,10},{1,5},{3,7},... | collective-permute-start | bytes 18440 | tf_op jit(solution)/shard_map/ppermute | solution.py:292
  8.3 2.4 %pairs.1 = (f32[2,8,144,128]{3,2,1,0:T(8,128)}, f32[144,192]{1,0:T(8,128)S(1)}, bf16[288,192]{1,0:T(8,128)(2,1)S(1)}) custom-call(f32[1,12]{1,0:T(1,128)S(1)} %bitcast.23, s32[2,8]{1,0:T(2,128)S(1)} %copy-done.5, bf16[16,768]{1,0:T(8,128)(2,1)S(1)} %get-tuple-element.15.query_norm, bf16[8,768]{1,0:T(8,128)(2,1)S(1)} %bitcast.20, ...), custom_call_target="tpu_custom_call" | custom-call | tf_op jit(solution)/shard_map/pairs/pallas_call | solution.py:371
  10.7 0.0 copy-start.1
  10.8 2.6 %collective-permute-start.1 = (bf16[2,16,192]{2,1,0:T(8,128)(2,1)S(1)}, bf16[2,16,192]{2,1,0:T(8,128)(2,1)S(1)}, u32[]{:S(2)}, u32[]{:S(2)}) collective-permute-start(bf16[2,16,192]{2,1,0:T(8,128)(2,1)S(1)} %pad_maximum_fusion), channel_id=1, source_target_pairs={{0,8},{2,10},{4,12},{6,14},{8,0},{10,2},{12,4},{14,6},{1,9},{3,11}... | collective-permute-start | bytes 36872 | tf_op jit(solution)/shard_map/ppermute | solution.py:292
  13.5 2.1 %collective-permute-done.1.refs_2_ = bf16[2,16,192]{2,1,0:T(8,128)(2,1)S(1)} collective-permute-done((bf16[2,16,192]{2,1,0:T(8,128)(2,1)S(1)}, bf16[2,16,192]{2,1,0:T(8,128)(2,1)S(1)}, u32[]{:S(2)}, u32[]{:S(2)}) %collective-permute-start.1) | collective-permute-done | bytes 12320 | tf_op jit(solution)/shard_map/ppermute | solution.py:292
  15.5 0.6 %collective-permute-start.2 = (bf16[352,192]{1,0:T(8,128)(2,1)S(1)}, bf16[352,192]{1,0:T(8,128)(2,1)S(1)}, u32[]{:S(2)}, u32[]{:S(2)}) collective-permute-start(bf16[352,192]{1,0:T(8,128)(2,1)S(1)} %constant_dynamic-update-slice_fusion), channel_id=1, source_target_pairs={{0,2},{2,0},{4,6},{6,4},{8,10},{10,8},{12,14},{14,12},{1,3},{3,1},... | collective-permute-start | bytes 405512 | tf_op jit(solution)/shard_map/ppermute | solution.py:292
  16.1 6.4 %collective-permute-done.2.refs_3_ = bf16[352,192]{1,0:T(8,128)(2,1)S(1)} collective-permute-done((bf16[352,192]{1,0:T(8,128)(2,1)S(1)}, bf16[352,192]{1,0:T(8,128)(2,1)S(1)}, u32[]{:S(2)}, u32[]{:S(2)}) %collective-permute-start.2) | collective-permute-done | bytes 135200 | tf_op jit(solution)/shard_map/ppermute | solution.py:292
  22.5 0.9 %attend.1.refs_0_ = bf16[16,896]{1,0:T(8,128)(2,1)S(1)} custom-call(bf16[16,192]{1,0:T(8,128)(2,1)S(1)} %get-tuple-element.24.refs_0_, bf16[16,192]{1,0:T(8,128)(2,1)S(1)} %collective-permute-done.refs_1_, bf16[2,16,192]{2,1,0:T(8,128)(2,1)S(1)} %collective-permute-done.1.refs_2_, bf16[352,192]{1,0:T(8,128)(2,1)S(1)} %collective-permute-done.2.refs_3_, ...), custom_call_target="tpu_custom_call" | custom-call | tf_op jit(solution)/shard_map/attend/pallas_call | solution.py:408
  23.4 1.2 %collective-permute-start.6 = (bf16[16,896]{1,0:T(8,128)(2,1)S(1)}, bf16[16,896]{1,0:T(8,128)(2,1)S(1)}, u32[]{:S(2)}, u32[]{:S(2)}) collective-permute-start(bf16[16,896]{1,0:T(8,128)(2,1)S(1)} %attend.1.refs_0_), channel_id=1, source_target_pairs={{0,4},{2,6},{4,0},{6,2},{8,12},{10,14},{12,8},{14,10},{1,5},{3,7},... | collective-permute-start | bytes 86024 | tf_op jit(solution)/shard_map/ppermute | solution.py:292
  24.6 2.6 %collective-permute-start.7 = (bf16[16,896]{1,0:T(8,128)(2,1)S(1)}, bf16[16,896]{1,0:T(8,128)(2,1)S(1)}, u32[]{:S(2)}, u32[]{:S(2)}) collective-permute-start(bf16[16,896]{1,0:T(8,128)(2,1)S(1)} %attend.1.refs_0_), channel_id=1, source_target_pairs={{0,8},{2,10},{4,12},{6,14},{8,0},{10,2},{12,4},{14,6},{1,9},{3,11}... | collective-permute-start | bytes 86024 | tf_op jit(solution)/shard_map/ppermute | solution.py:292
  27.2 0.7 %collective-permute-start.8 = (bf16[16,896]{1,0:T(8,128)(2,1)S(1)}, bf16[16,896]{1,0:T(8,128)(2,1)S(1)}, u32[]{:S(2)}, u32[]{:S(2)}) collective-permute-start(bf16[16,896]{1,0:T(8,128)(2,1)S(1)} %attend.1.refs_0_), channel_id=1, source_target_pairs={{0,12},{2,14},{4,8},{6,10},{8,4},{10,6},{12,0},{14,2},{1,13},{3,15... | collective-permute-start | bytes 86024 | tf_op jit(solution)/shard_map/ppermute | solution.py:292
  27.8 0.1 gate.1
  27.9 2.0 %collective-permute-done.7.refs_2_ = bf16[16,896]{1,0:T(8,128)(2,1)S(1)} collective-permute-done((bf16[16,896]{1,0:T(8,128)(2,1)S(1)}, bf16[16,896]{1,0:T(8,128)(2,1)S(1)}, u32[]{:S(2)}, u32[]{:S(2)}) %collective-permute-start.7) | collective-permute-done | bytes 28704 | tf_op jit(solution)/shard_map/ppermute | solution.py:292
  29.9 2.9 %collective-permute-done.8.refs_3_ = bf16[16,896]{1,0:T(8,128)(2,1)S(1)} collective-permute-done((bf16[16,896]{1,0:T(8,128)(2,1)S(1)}, bf16[16,896]{1,0:T(8,128)(2,1)S(1)}, u32[]{:S(2)}, u32[]{:S(2)}) %collective-permute-start.8) | collective-permute-done | bytes 28704 | tf_op jit(solution)/shard_map/ppermute | solution.py:292
  32.8 1.1 %finish.1 = bf16[16,768]{1,0:T(8,128)(2,1)} custom-call(f32[16,768]{1,0:T(8,128)S(1)} %gate.1, bf16[16,896]{1,0:T(8,128)(2,1)S(1)} %attend.1.refs_0_, bf16[16,896]{1,0:T(8,128)(2,1)S(1)} %collective-permute-done.6.refs_1_, bf16[16,896]{1,0:T(8,128)(2,1)S(1)} %collective-permute-done.7.refs_2_, bf16[16,896]{1,0:T(8,128)(2,1)S(1)} %collective-permute-done.8.refs_3_, ...), custom_call_target="tpu_custom_call" | custom-call | tf_op jit(solution)/shard_map/finish/pallas_call | solution.py:434
  (22 shorter events, 0.1 us)
Async XLA Ops:
  2.9 5.4 %copy-start = (f32[2,8,144,128]{3,2,1,0:T(8,128)S(1)}, f32[2,8,144,128]{3,2,1,0:T(8,128)}, u32[]{:S(2)}) copy-start(f32[2,8,144,128]{3,2,1,0:T(8,128)} %pair.1) | copy-start | bytes 3538948
  3.0 5.4 %copy-start.2 = (bf16[64,128]{1,0:T(8,128)(2,1)S(1)}, bf16[64,128]{1,0:T(8,128)(2,1)}, u32[]{:S(2)}) copy-start(bf16[64,128]{1,0:T(8,128)(2,1)} %outer_proj.1) | copy-start | bytes 49156
  3.0 5.3 %copy-start.3 = (bf16[768,8]{0,1:T(8,128)(2,1)S(1)}, bf16[768,8]{0,1:T(8,128)(2,1)}, u32[]{:S(2)}) copy-start(bf16[768,8]{0,1:T(8,128)(2,1)} %param.28) | copy-start | bytes 36868
  3.0 5.3 %copy-start.4 = (f32[128,12]{0,1:T(8,128)S(1)}, f32[128,12]{0,1:T(8,128)}, u32[]{:S(2)}) copy-start(f32[128,12]{0,1:T(8,128)} %param.31) | copy-start | bytes 18436
  3.0 5.3 %copy-start.5 = (s32[2,8]{1,0:T(2,128)S(1)}, s32[2,8]{1,0:T(2,128)}, u32[]{:S(2)}) copy-start(s32[2,8]{1,0:T(2,128)} %query_chain.1) | copy-start | bytes 196
  3.0 5.3 %copy-start.6 = (s32[144]{0:T(256)S(1)}, s32[144]{0:T(256)}, u32[]{:S(2)}) copy-start(s32[144]{0:T(256)} %param.22) | copy-start | bytes 1732
  3.0 5.3 %copy-start.7 = (f32[12]{0:T(128)S(1)}, f32[12]{0:T(128)}, u32[]{:S(2)}) copy-start(f32[12]{0:T(128)} %param.32) | copy-start | bytes 148
  3.7 11.8 %collective-permute-start.4 = (bf16[144,768]{1,0:T(8,128)(2,1)S(1)}, bf16[144,768]{1,0:T(8,128)(2,1)S(1)}, u32[]{:S(2)}, u32[]{:S(2)}) collective-permute-start(bf16[144,768]{1,0:T(8,128)(2,1)S(1)} %get-tuple-element.26.refs_4_), channel_id=1, source_target_pairs={{0,2},{2,0},{4,6},{6,4},{8,10},{10,8},{12,14},{14,12},{1,3},{3,1},... | collective-permute-start | bytes 663560 | tf_op jit(solution)/shard_map/ppermute | solution.py:292
  6.7 15.8 %collective-permute-start.3 = (bf16[144,768]{1,0:T(8,128)(2,1)S(1)}, bf16[144,768]{1,0:T(8,128)(2,1)S(1)}, u32[]{:S(2)}, u32[]{:S(2)}) collective-permute-start(bf16[144,768]{1,0:T(8,128)(2,1)S(1)} %get-tuple-element.26.refs_4_), channel_id=1, source_target_pairs={{0,1},{1,0},{2,3},{3,2},{4,5},{5,4},{6,7},{7,6},{8,9},{9,8},{10,11... | collective-permute-start | bytes 663560 | tf_op jit(solution)/shard_map/ppermute | solution.py:292
  6.7 4.1 %collective-permute-start = (bf16[16,192]{1,0:T(8,128)(2,1)S(1)}, bf16[16,192]{1,0:T(8,128)(2,1)S(1)}, u32[]{:S(2)}, u32[]{:S(2)}) collective-permute-start(bf16[16,192]{1,0:T(8,128)(2,1)S(1)} %get-tuple-element.24.refs_0_), channel_id=1, source_target_pairs={{0,4},{2,6},{4,0},{6,2},{8,12},{10,14},{12,8},{14,10},{1,5},{3,7},... | collective-permute-start | bytes 18440 | tf_op jit(solution)/shard_map/ppermute | solution.py:292
  10.7 22.1 %copy-start.1 = (bf16[768,768]{1,0:T(8,128)(2,1)S(1)}, bf16[768,768]{1,0:T(8,128)(2,1)}, u32[]{:S(2)}) copy-start(bf16[768,768]{1,0:T(8,128)(2,1)} %refs_4_.3) | copy-start | bytes 3538948
  10.8 4.7 %collective-permute-start.1 = (bf16[2,16,192]{2,1,0:T(8,128)(2,1)S(1)}, bf16[2,16,192]{2,1,0:T(8,128)(2,1)S(1)}, u32[]{:S(2)}, u32[]{:S(2)}) collective-permute-start(bf16[2,16,192]{2,1,0:T(8,128)(2,1)S(1)} %pad_maximum_fusion), channel_id=1, source_target_pairs={{0,8},{2,10},{4,12},{6,14},{8,0},{10,2},{12,4},{14,6},{1,9},{3,11}... | collective-permute-start | bytes 36872 | tf_op jit(solution)/shard_map/ppermute | solution.py:292
  15.5 7.0 %collective-permute-start.5 = (bf16[144,768]{1,0:T(8,128)(2,1)S(1)}, bf16[144,768]{1,0:T(8,128)(2,1)S(1)}, u32[]{:S(2)}, u32[]{:S(2)}) collective-permute-start(bf16[144,768]{1,0:T(8,128)(2,1)S(1)} %collective-permute-done.4.refs_6_), channel_id=1, source_target_pairs={{0,1},{1,0},{2,3},{3,2},{4,5},{5,4},{6,7},{7,6},{8,9},{9,8},{10,11... | collective-permute-start | bytes 663560 | tf_op jit(solution)/shard_map/ppermute | solution.py:292
  15.5 7.0 %collective-permute-start.2 = (bf16[352,192]{1,0:T(8,128)(2,1)S(1)}, bf16[352,192]{1,0:T(8,128)(2,1)S(1)}, u32[]{:S(2)}, u32[]{:S(2)}) collective-permute-start(bf16[352,192]{1,0:T(8,128)(2,1)S(1)} %constant_dynamic-update-slice_fusion), channel_id=1, source_target_pairs={{0,2},{2,0},{4,6},{6,4},{8,10},{10,8},{12,14},{14,12},{1,3},{3,1},... | collective-permute-start | bytes 405512 | tf_op jit(solution)/shard_map/ppermute | solution.py:292
  23.4 4.6 %collective-permute-start.6 = (bf16[16,896]{1,0:T(8,128)(2,1)S(1)}, bf16[16,896]{1,0:T(8,128)(2,1)S(1)}, u32[]{:S(2)}, u32[]{:S(2)}) collective-permute-start(bf16[16,896]{1,0:T(8,128)(2,1)S(1)} %attend.1.refs_0_), channel_id=1, source_target_pairs={{0,4},{2,6},{4,0},{6,2},{8,12},{10,14},{12,8},{14,10},{1,5},{3,7},... | collective-permute-start | bytes 86024 | tf_op jit(solution)/shard_map/ppermute | solution.py:292
  24.6 5.3 %collective-permute-start.7 = (bf16[16,896]{1,0:T(8,128)(2,1)S(1)}, bf16[16,896]{1,0:T(8,128)(2,1)S(1)}, u32[]{:S(2)}, u32[]{:S(2)}) collective-permute-start(bf16[16,896]{1,0:T(8,128)(2,1)S(1)} %attend.1.refs_0_), channel_id=1, source_target_pairs={{0,8},{2,10},{4,12},{6,14},{8,0},{10,2},{12,4},{14,6},{1,9},{3,11}... | collective-permute-start | bytes 86024 | tf_op jit(solution)/shard_map/ppermute | solution.py:292
  27.2 5.7 %collective-permute-start.8 = (bf16[16,896]{1,0:T(8,128)(2,1)S(1)}, bf16[16,896]{1,0:T(8,128)(2,1)S(1)}, u32[]{:S(2)}, u32[]{:S(2)}) collective-permute-start(bf16[16,896]{1,0:T(8,128)(2,1)S(1)} %attend.1.refs_0_), channel_id=1, source_target_pairs={{0,12},{2,14},{4,8},{6,10},{8,4},{10,6},{12,0},{14,2},{1,13},{3,15... | collective-permute-start | bytes 86024 | tf_op jit(solution)/shard_map/ppermute | solution.py:292

commit v5 on v4

--- a/solution.py
+++ b/solution.py
@@ -110,7 +110,6 @@
     key_chain,
     pair,
     pair_out,
-    bias_out,
     terms_out,
     fresh_scratch,
     sems,
@@ -162,10 +161,8 @@
             place = (index - start) * key_count
             bias = jnp.where(row_of == index, here[place : place + key_count], bias)
     bias = bias + jnp.where(column_of(key_chain[...]) != chains, apart, 0.0)
-    bias_out[...] = bias
     high, low = split(bias)
-    terms_out[:key_count] = high
-    terms_out[key_count:] = low
+    terms_out[...] = jnp.concatenate([high, low], axis=1)
     for copy in copies:
         copy.wait()
 
@@ -182,12 +179,8 @@
         return pieces[0][:, start:stop]
     col = lax.axis_index("col")
     ours = listed(pieces[:3])
-    count, share = ours[0].shape
-    message = pieces[3]
-    base = message.shape[0] - len(ours) * count
-    values = []
-    for index, value in enumerate(ours):
-        values += [value, message[base + index * count : base + (index + 1) * count]]
+    share = ours[0].shape[1]
+    values = [value for both in zip(ours, listed(pieces[3:])) for value in both]
     blocks = []
     for target in range(start // share, stop // share):
         chosen = values[0]
@@ -197,18 +190,13 @@
     return jnp.concatenate(blocks, axis=1)
 
 
-def attend_kernel(pieces, halves, bias_ref, part_out, heads, count):
+def attend_kernel(pieces, halves, biases, part_out, heads, count):
     row = lax.axis_index("row")
-    key_count, model = halves[0].shape
+    _, model = halves[0].shape
     head = model // heads
     lanes = heads * count
     query = gathered(pieces, 0, model)
-    biases = [bias_ref[...]]
-    if len(pieces) > 1:
-        message = pieces[3]
-        biases.append(
-            message[:key_count].astype(F32) + message[key_count : 2 * key_count].astype(F32)
-        )
+    biases = [bias[:, :lanes].astype(F32) + bias[:, lanes:].astype(F32) for bias in biases]
     firsts = [ref[...] for ref in halves[::2]]
     seconds = [ref[...] for ref in halves[1::2]]
     keys = [jnp.where(row == 0, first, second) for first, second in zip(firsts, seconds)]
@@ -368,15 +356,14 @@
         far = exchanged(half, "col", 1)
         halves += [far, exchanged(far, "row", 1)]
 
-    new_pair, bias, terms = pl.pallas_call(
+    new_pair, bias = pl.pallas_call(
         pair_kernel,
         out_shape=(
             jax.ShapeDtypeStruct(pair_block.shape, F32),
-            jax.ShapeDtypeStruct((key_count, lanes), F32),
-            jax.ShapeDtypeStruct((2 * key_count, lanes), BF16),
+            jax.ShapeDtypeStruct((key_count, 2 * lanes), BF16),
         ),
         in_specs=[VMEM] * 9,
-        out_specs=(HBM, VMEM, VMEM),
+        out_specs=(HBM, VMEM),
         scratch_shapes=[
             pltpu.VMEM((count, key_count, channels), F32),
             pltpu.SemaphoreType.DMA((count,)),
@@ -395,24 +382,26 @@
         pair_block,
     )
     if direct:
-        far = exchanged(jnp.stack([query_part, beside]), "col", 4)
-        message = jnp.concatenate([terms, query_part, beside, far[0], far[1]], axis=0)
-        pieces = [query_part, beside, far, exchanged(message, "col", 1)]
+        biases = [bias, exchanged(bias, "col", 1)]
+        across = exchanged(jnp.stack([query_part, beside]), "col", 4)
+        ours = jnp.stack([query_part, beside, across[0], across[1]])
+        pieces = [query_part, beside, across, exchanged(ours, "col", 1)]
     else:
+        biases = [bias]
         pieces = [lax.all_gather(query_part, "col", axis=1, tiled=True)]
 
     def attend_body(*refs):
-        n = len(pieces)
-        attend_kernel(refs[:n], refs[n:-2], *refs[-2:], heads, count)
+        n, k = len(pieces), len(pieces) + len(halves)
+        attend_kernel(refs[:n], refs[n:k], refs[k:-1], refs[-1], heads, count)
 
     part = pl.pallas_call(
         attend_body,
         out_shape=jax.ShapeDtypeStruct((count, model + LANES), BF16),
-        in_specs=[VMEM] * (len(pieces) + len(halves) + 1),
+        in_specs=[VMEM] * (len(pieces) + len(halves) + len(biases)),
         out_specs=VMEM,
         compiler_params=grant,
         name="attend",
-    )(*pieces, *halves, bias)
+    )(*pieces, *halves, *biases)
 
     if direct:
         parts = [part] + [exchanged(part, "col", flip) for flip in (2, 4, 6)]

time: 34.1 us -> 33.3 us (0.977)
  waiting for transfers between devices: 13.3 us -> 10.7 us
  starting transfers between devices: 12.3 us -> 14.1 us
    ppermute x9 -> x10, waiting for transfers between devices: 13.3 us -> 10.7 us  [exchanged(): lax.ppermute(value, axis, [(index, index ^ flip) for index in range(size)])]
    ppermute x9 -> x10, starting transfers between devices: 12.3 us -> 14.1 us  [exchanged(): lax.ppermute(value, axis, [(index, index ^ flip) for index in range(size)])]
  transfers between devices with their start and end apart: 9 -> 10, of which waited for: 4 -> 4; matrix products, arithmetic and copies ran while one was open for 0% -> 0% of each run, Pallas kernels for 7% -> 7%
where the time goes in v5:
time: 33.3 us; the launch traced here: 33.1 us
  starting transfers between devices  14.1 us (42%)
  waiting for transfers between devices  10.7 us (32%)
  Pallas kernels  6.77 us (20%)
  between operations  1.43 us (4%)
    ppermute x10, starting transfers between devices, exchanged(): lax.ppermute(value, axis, [(index, index ^ flip) for index in range(size)])  14.1 us
    ppermute x10, waiting for transfers between devices, exchanged(): lax.ppermute(value, axis, [(index, index ^ flip) for index in range(size)])  10.7 us
    pallas_call x1, Pallas kernels, on_device(): pl.pallas_call(pair_kernel, out_shape=(jax.ShapeDtypeStruct(pair_block.sh...  2.39 us
    pallas_call x1, Pallas kernels, on_device(): pl.pallas_call(query_kernel, out_shape=(jax.ShapeDtypeStruct((count, quer...  1.65 us
    pallas_call x1, Pallas kernels, on_device(): pl.pallas_call(finish_body, out_shape=jax.ShapeDtypeStruct((count, model)...  1.09 us
    pallas_call x1, Pallas kernels, on_device(): pl.pallas_call(attend_body, out_shape=jax.ShapeDtypeStruct((count, model...  0.89 us
  transfers between devices with their start and end apart: 10, of which 4 were waited for; matrix products, arithmetic and copies ran while one was open for 0% of the time, Pallas kernels for 7%

profile of v5, /device:TPU:0, one launch (start us, length us, event | category | flops | bytes accessed | tf_op | source)
XLA Modules:
  0.0 33.1 jit_solution(16688196047928915776)
XLA Ops:
  1.3 1.7 %query.1 = (bf16[16,192]{1,0:T(8,128)(2,1)S(1)}, bf16[16,768]{1,0:T(8,128)(2,1)S(1)}, f32[1,768]{1,0:T(1,128)S(1)}, f32[768]{0:T(1024)S(1)}, bf16[144,768]{1,0:T...) custom-call(s32[1]{0:T(128)S(6)} %copy.20.refs_0_, ...), custom_call_target="tpu_custom_call" | custom-call | tf_op jit(solution)/shard_map/query/pallas_call | solution.py:318
  2.9 0.0 copy-start
  3.0 0.0 copy-start.2
  3.0 0.0 copy-start.3
  3.0 0.0 copy-start.6
  3.0 0.0 copy-start.7
  3.0 0.7 %keys.1 = (bf16[144,768]{1,0:T(8,128)(2,1)S(1)}, f32[144,8]{1,0:T(8,128)S(1)}) custom-call(f32[1,768]{1,0:T(1,128)S(1)} %get-tuple-element.15.time_row, f32[768]{0:T(1024)S(1)} %get-tuple-element.16.gain, bf16[144,768]{1,0:T(8,128)(2,1)S(1)} %get-tuple-element.17.single, bf16[768,768]{1,0:T(8,128)(2,1)S(1)} %get-tuple-element.18.proj, ...), custom_call_target="tpu_custom_call" | custom-call | tf_op jit(solution)/shard_map/keys/pallas_call | solution.py:343
  3.7 3.0 %collective-permute-start.4 = (bf16[144,768]{1,0:T(8,128)(2,1)S(1)}, bf16[144,768]{1,0:T(8,128)(2,1)S(1)}, u32[]{:S(2)}, u32[]{:S(2)}) collective-permute-start(bf16[144,768]{1,0:T(8,128)(2,1)S(1)} %get-tuple-element.24.refs_4_), channel_id=1, source_target_pairs={{0,2},{2,0},{4,6},{6,4},{8,10},{10,8},{12,14},{14,12},{1,3},{3,1},... | collective-permute-start | bytes 663560 | tf_op jit(solution)/shard_map/ppermute | solution.py:280
  6.7 1.6 %collective-permute-start = (bf16[16,192]{1,0:T(8,128)(2,1)S(1)}, bf16[16,192]{1,0:T(8,128)(2,1)S(1)}, u32[]{:S(2)}, u32[]{:S(2)}) collective-permute-start(bf16[16,192]{1,0:T(8,128)(2,1)S(1)} %get-tuple-element.23.refs_0_), channel_id=1, source_target_pairs={{0,4},{2,6},{4,0},{6,2},{8,12},{10,14},{12,8},{14,10},{1,5},{3,7},... | collective-permute-start | bytes 18440 | tf_op jit(solution)/shard_map/ppermute | solution.py:280
  8.3 3.8 %collective-permute-done.4.refs_6_ = bf16[144,768]{1,0:T(8,128)(2,1)S(1)} collective-permute-done((bf16[144,768]{1,0:T(8,128)(2,1)S(1)}, bf16[144,768]{1,0:T(8,128)(2,1)S(1)}, u32[]{:S(2)}, u32[]{:S(2)}) %collective-permute-start.4) | collective-permute-done | bytes 221216 | tf_op jit(solution)/shard_map/ppermute | solution.py:280
  12.2 2.9 %collective-permute-start.1 = (bf16[2,16,192]{2,1,0:T(8,128)(2,1)S(1)}, bf16[2,16,192]{2,1,0:T(8,128)(2,1)S(1)}, u32[]{:S(2)}, u32[]{:S(2)}) collective-permute-start(bf16[2,16,192]{2,1,0:T(8,128)(2,1)S(1)} %pad_maximum_fusion.1), channel_id=1, source_target_pairs={{0,8},{2,10},{4,12},{6,14},{8,0},{10,2},{12,4},{14,6},{1,9},{3,11}... | collective-permute-start | bytes 36872 | tf_op jit(solution)/shard_map/ppermute | solution.py:280
  15.1 0.0 copy-start.1
  15.1 2.4 %pairs.1 = (f32[2,8,144,128]{3,2,1,0:T(8,128)}, bf16[144,384]{1,0:T(8,128)(2,1)S(1)}) custom-call(f32[1,12]{1,0:T(1,128)S(1)} %bitcast.17, s32[2,8]{1,0:T(2,128)S(1)} %copy-done.5, bf16[16,768]{1,0:T(8,128)(2,1)S(1)} %get-tuple-element.14.query_norm, bf16[8,768]{1,0:T(8,128)(2,1)S(1)} %bitcast.14, bf16[64,128]{1,0:T(8,128)(2,1)S(1)} %copy-done.2, ...), custom_call_target="tpu_custom_call" | custom-call | tf_op jit(solution)/shard_map/pairs/pallas_call | solution.py:359
  17.5 1.6 %collective-permute-start.6 = (bf16[144,384]{1,0:T(8,128)(2,1)S(1)}, bf16[144,384]{1,0:T(8,128)(2,1)S(1)}, u32[]{:S(2)}, u32[]{:S(2)}) collective-permute-start(bf16[144,384]{1,0:T(8,128)(2,1)S(1)} %get-tuple-element.25.refs_8_), channel_id=1, source_target_pairs={{0,2},{2,0},{4,6},{6,4},{8,10},{10,8},{12,14},{14,12},{1,3},{3,1},... | collective-permute-start | bytes 331784 | tf_op jit(solution)/shard_map/ppermute | solution.py:280
  19.1 0.6 %collective-permute-start.2 = (bf16[4,16,192]{2,1,0:T(8,128)(2,1)S(1)}, bf16[4,16,192]{2,1,0:T(8,128)(2,1)S(1)}, u32[]{:S(2)}, u32[]{:S(2)}) collective-permute-start(bf16[4,16,192]{2,1,0:T(8,128)(2,1)S(1)} %pad_maximum_fusion), channel_id=1, source_target_pairs={{0,2},{2,0},{4,6},{6,4},{8,10},{10,8},{12,14},{14,12},{1,3},{3,1},... | collective-permute-start | bytes 73736 | tf_op jit(solution)/shard_map/ppermute | solution.py:280
  19.7 3.8 %collective-permute-done.2.refs_3_ = bf16[4,16,192]{2,1,0:T(8,128)(2,1)S(1)} collective-permute-done((bf16[4,16,192]{2,1,0:T(8,128)(2,1)S(1)}, bf16[4,16,192]{2,1,0:T(8,128)(2,1)S(1)}, u32[]{:S(2)}, u32[]{:S(2)}) %collective-permute-start.2) | collective-permute-done | bytes 24608 | tf_op jit(solution)/shard_map/ppermute | solution.py:280
  23.5 0.9 %attend.1.refs_0_ = bf16[16,896]{1,0:T(8,128)(2,1)S(1)} custom-call(bf16[16,192]{1,0:T(8,128)(2,1)S(1)} %get-tuple-element.23.refs_0_, bf16[16,192]{1,0:T(8,128)(2,1)S(1)} %collective-permute-done.refs_1_, bf16[2,16,192]{2,1,0:T(8,128)(2,1)S(1)} %collective-permute-done.1.refs_2_, bf16[4,16,192]{2,1,0:T(8,128)(2,1)S(1)} %collective-permute-done.2.refs_3_, ...), custom_call_target="tpu_custom_call" | custom-call | tf_op jit(solution)/shard_map/attend/pallas_call | solution.py:397
  24.4 1.7 %collective-permute-start.7 = (bf16[16,896]{1,0:T(8,128)(2,1)S(1)}, bf16[16,896]{1,0:T(8,128)(2,1)S(1)}, u32[]{:S(2)}, u32[]{:S(2)}) collective-permute-start(bf16[16,896]{1,0:T(8,128)(2,1)S(1)} %attend.1.refs_0_), channel_id=1, source_target_pairs={{0,4},{2,6},{4,0},{6,2},{8,12},{10,14},{12,8},{14,10},{1,5},{3,7},... | collective-permute-start | bytes 86024 | tf_op jit(solution)/shard_map/ppermute | solution.py:280
  26.0 0.3 collective-permute-start.8
  26.4 2.5 %collective-permute-start.9 = (bf16[16,896]{1,0:T(8,128)(2,1)S(1)}, bf16[16,896]{1,0:T(8,128)(2,1)S(1)}, u32[]{:S(2)}, u32[]{:S(2)}) collective-permute-start(bf16[16,896]{1,0:T(8,128)(2,1)S(1)} %attend.1.refs_0_), channel_id=1, source_target_pairs={{0,12},{2,14},{4,8},{6,10},{8,4},{10,6},{12,0},{14,2},{1,13},{3,15... | collective-permute-start | bytes 86024 | tf_op jit(solution)/shard_map/ppermute | solution.py:280
  28.8 0.1 gate.1
  28.9 2.0 %collective-permute-done.8.refs_2_ = bf16[16,896]{1,0:T(8,128)(2,1)S(1)} collective-permute-done((bf16[16,896]{1,0:T(8,128)(2,1)S(1)}, bf16[16,896]{1,0:T(8,128)(2,1)S(1)}, u32[]{:S(2)}, u32[]{:S(2)}) %collective-permute-start.8) | collective-permute-done | bytes 28704 | tf_op jit(solution)/shard_map/ppermute | solution.py:280
  31.0 1.0 %collective-permute-done.9.refs_3_ = bf16[16,896]{1,0:T(8,128)(2,1)S(1)} collective-permute-done((bf16[16,896]{1,0:T(8,128)(2,1)S(1)}, bf16[16,896]{1,0:T(8,128)(2,1)S(1)}, u32[]{:S(2)}, u32[]{:S(2)}) %collective-permute-start.9) | collective-permute-done | bytes 28704 | tf_op jit(solution)/shard_map/ppermute | solution.py:280
  32.0 1.1 %finish.1 = bf16[16,768]{1,0:T(8,128)(2,1)} custom-call(f32[16,768]{1,0:T(8,128)S(1)} %gate.1, bf16[16,896]{1,0:T(8,128)(2,1)S(1)} %attend.1.refs_0_, bf16[16,896]{1,0:T(8,128)(2,1)S(1)} %collective-permute-done.7.refs_1_, bf16[16,896]{1,0:T(8,128)(2,1)S(1)} %collective-permute-done.8.refs_2_, bf16[16,896]{1,0:T(8,128)(2,1)S(1)} %collective-permute-done.9.refs_3_, ...), custom_call_target="tpu_custom_call" | custom-call | tf_op jit(solution)/shard_map/finish/pallas_call | solution.py:423
  (20 shorter events, 0.1 us)
Async XLA Ops:
  2.9 12.1 %copy-start = (f32[2,8,144,128]{3,2,1,0:T(8,128)S(1)}, f32[2,8,144,128]{3,2,1,0:T(8,128)}, u32[]{:S(2)}) copy-start(f32[2,8,144,128]{3,2,1,0:T(8,128)} %pair.1) | copy-start | bytes 3538948
  3.0 12.1 %copy-start.2 = (bf16[64,128]{1,0:T(8,128)(2,1)S(1)}, bf16[64,128]{1,0:T(8,128)(2,1)}, u32[]{:S(2)}) copy-start(bf16[64,128]{1,0:T(8,128)(2,1)} %outer_proj.1) | copy-start | bytes 49156
  3.0 12.1 %copy-start.3 = (bf16[768,8]{0,1:T(8,128)(2,1)S(1)}, bf16[768,8]{0,1:T(8,128)(2,1)}, u32[]{:S(2)}) copy-start(bf16[768,8]{0,1:T(8,128)(2,1)} %param.28) | copy-start | bytes 36868
  3.0 12.1 %copy-start.4 = (f32[128,12]{0,1:T(8,128)S(1)}, f32[128,12]{0,1:T(8,128)}, u32[]{:S(2)}) copy-start(f32[128,12]{0,1:T(8,128)} %param.31) | copy-start | bytes 18436
  3.0 12.1 %copy-start.5 = (s32[2,8]{1,0:T(2,128)S(1)}, s32[2,8]{1,0:T(2,128)}, u32[]{:S(2)}) copy-start(s32[2,8]{1,0:T(2,128)} %query_chain.1) | copy-start | bytes 196
  3.0 12.1 %copy-start.6 = (s32[144]{0:T(256)S(1)}, s32[144]{0:T(256)}, u32[]{:S(2)}) copy-start(s32[144]{0:T(256)} %param.22) | copy-start | bytes 1732
  3.0 12.1 %copy-start.7 = (f32[12]{0:T(128)S(1)}, f32[12]{0:T(128)}, u32[]{:S(2)}) copy-start(f32[12]{0:T(128)} %param.32) | copy-start | bytes 148
  3.7 8.5 %collective-permute-start.4 = (bf16[144,768]{1,0:T(8,128)(2,1)S(1)}, bf16[144,768]{1,0:T(8,128)(2,1)S(1)}, u32[]{:S(2)}, u32[]{:S(2)}) collective-permute-start(bf16[144,768]{1,0:T(8,128)(2,1)S(1)} %get-tuple-element.24.refs_4_), channel_id=1, source_target_pairs={{0,2},{2,0},{4,6},{6,4},{8,10},{10,8},{12,14},{14,12},{1,3},{3,1},... | collective-permute-start | bytes 663560 | tf_op jit(solution)/shard_map/ppermute | solution.py:280
  6.7 5.4 %collective-permute-start = (bf16[16,192]{1,0:T(8,128)(2,1)S(1)}, bf16[16,192]{1,0:T(8,128)(2,1)S(1)}, u32[]{:S(2)}, u32[]{:S(2)}) collective-permute-start(bf16[16,192]{1,0:T(8,128)(2,1)S(1)} %get-tuple-element.23.refs_0_), channel_id=1, source_target_pairs={{0,4},{2,6},{4,0},{6,2},{8,12},{10,14},{12,8},{14,10},{1,5},{3,7},... | collective-permute-start | bytes 18440 | tf_op jit(solution)/shard_map/ppermute | solution.py:280
  8.3 15.2 %collective-permute-start.3 = (bf16[144,768]{1,0:T(8,128)(2,1)S(1)}, bf16[144,768]{1,0:T(8,128)(2,1)S(1)}, u32[]{:S(2)}, u32[]{:S(2)}) collective-permute-start(bf16[144,768]{1,0:T(8,128)(2,1)S(1)} %get-tuple-element.24.refs_4_), channel_id=1, source_target_pairs={{0,1},{1,0},{2,3},{3,2},{4,5},{5,4},{6,7},{7,6},{8,9},{9,8},{10,11... | collective-permute-start | bytes 663560 | tf_op jit(solution)/shard_map/ppermute | solution.py:280
  12.1 11.3 %collective-permute-start.5 = (bf16[144,768]{1,0:T(8,128)(2,1)S(1)}, bf16[144,768]{1,0:T(8,128)(2,1)S(1)}, u32[]{:S(2)}, u32[]{:S(2)}) collective-permute-start(bf16[144,768]{1,0:T(8,128)(2,1)S(1)} %collective-permute-done.4.refs_6_), channel_id=1, source_target_pairs={{0,1},{1,0},{2,3},{3,2},{4,5},{5,4},{6,7},{7,6},{8,9},{9,8},{10,11... | collective-permute-start | bytes 663560 | tf_op jit(solution)/shard_map/ppermute | solution.py:280
  12.2 6.9 %collective-permute-start.1 = (bf16[2,16,192]{2,1,0:T(8,128)(2,1)S(1)}, bf16[2,16,192]{2,1,0:T(8,128)(2,1)S(1)}, u32[]{:S(2)}, u32[]{:S(2)}) collective-permute-start(bf16[2,16,192]{2,1,0:T(8,128)(2,1)S(1)} %pad_maximum_fusion.1), channel_id=1, source_target_pairs={{0,8},{2,10},{4,12},{6,14},{8,0},{10,2},{12,4},{14,6},{1,9},{3,11}... | collective-permute-start | bytes 36872 | tf_op jit(solution)/shard_map/ppermute | solution.py:280
  15.1 16.9 %copy-start.1 = (bf16[768,768]{1,0:T(8,128)(2,1)S(1)}, bf16[768,768]{1,0:T(8,128)(2,1)}, u32[]{:S(2)}) copy-start(bf16[768,768]{1,0:T(8,128)(2,1)} %refs_4_.3) | copy-start | bytes 3538948
  17.5 6.0 %collective-permute-start.6 = (bf16[144,384]{1,0:T(8,128)(2,1)S(1)}, bf16[144,384]{1,0:T(8,128)(2,1)S(1)}, u32[]{:S(2)}, u32[]{:S(2)}) collective-permute-start(bf16[144,384]{1,0:T(8,128)(2,1)S(1)} %get-tuple-element.25.refs_8_), channel_id=1, source_target_pairs={{0,2},{2,0},{4,6},{6,4},{8,10},{10,8},{12,14},{14,12},{1,3},{3,1},... | collective-permute-start | bytes 331784 | tf_op jit(solution)/shard_map/ppermute | solution.py:280
  19.1 4.4 %collective-permute-start.2 = (bf16[4,16,192]{2,1,0:T(8,128)(2,1)S(1)}, bf16[4,16,192]{2,1,0:T(8,128)(2,1)S(1)}, u32[]{:S(2)}, u32[]{:S(2)}) collective-permute-start(bf16[4,16,192]{2,1,0:T(8,128)(2,1)S(1)} %pad_maximum_fusion), channel_id=1, source_target_pairs={{0,2},{2,0},{4,6},{6,4},{8,10},{10,8},{12,14},{14,12},{1,3},{3,1},... | collective-permute-start | bytes 73736 | tf_op jit(solution)/shard_map/ppermute | solution.py:280
  24.4 4.6 %collective-permute-start.7 = (bf16[16,896]{1,0:T(8,128)(2,1)S(1)}, bf16[16,896]{1,0:T(8,128)(2,1)S(1)}, u32[]{:S(2)}, u32[]{:S(2)}) collective-permute-start(bf16[16,896]{1,0:T(8,128)(2,1)S(1)} %attend.1.refs_0_), channel_id=1, source_target_pairs={{0,4},{2,6},{4,0},{6,2},{8,12},{10,14},{12,8},{14,10},{1,5},{3,7},... | collective-permute-start | bytes 86024 | tf_op jit(solution)/shard_map/ppermute | solution.py:280
  26.0 5.0 %collective-permute-start.8 = (bf16[16,896]{1,0:T(8,128)(2,1)S(1)}, bf16[16,896]{1,0:T(8,128)(2,1)S(1)}, u32[]{:S(2)}, u32[]{:S(2)}) collective-permute-start(bf16[16,896]{1,0:T(8,128)(2,1)S(1)} %attend.1.refs_0_), channel_id=1, source_target_pairs={{0,8},{2,10},{4,12},{6,14},{8,0},{10,2},{12,4},{14,6},{1,9},{3,11}... | collective-permute-start | bytes 86024 | tf_op jit(solution)/shard_map/ppermute | solution.py:280
  26.4 5.7 %collective-permute-start.9 = (bf16[16,896]{1,0:T(8,128)(2,1)S(1)}, bf16[16,896]{1,0:T(8,128)(2,1)S(1)}, u32[]{:S(2)}, u32[]{:S(2)}) collective-permute-start(bf16[16,896]{1,0:T(8,128)(2,1)S(1)} %attend.1.refs_0_), channel_id=1, source_target_pairs={{0,12},{2,14},{4,8},{6,10},{8,4},{10,6},{12,0},{14,2},{1,13},{3,15... | collective-permute-start | bytes 86024 | tf_op jit(solution)/shard_map/ppermute | solution.py:280

commit v6 on v5

--- a/solution.py
+++ b/solution.py
@@ -10,7 +10,6 @@
 
 
 EPSILON = 1e-05
-HIGHEST = lax.Precision.HIGHEST
 LANES = 128
 TERM = LANES // 5
 GROUP = 4
@@ -111,8 +110,7 @@
     pair,
     pair_out,
     terms_out,
-    fresh_scratch,
-    sems,
+    bias_scratch,
 ):
     slabs, rows = query_chain.shape
     count = slabs * rows
@@ -122,26 +120,27 @@
     lanes = heads * count
     left = dot_nt(query_norm[...], left_proj[...])
     spot = (rank, rank * rank)
-    wide = dot(left, (iota(spot, 1) // rank == iota(spot, 0)).astype(F32), HIGHEST)
-    tall = jnp.broadcast_to(wide[:, None, :], (count, rank, rank * rank))
-    tall = tall.reshape(count * rank, rank * rank)
+    repeat = (iota(spot, 1) // rank == iota(spot, 0)).astype(BF16)
     spot = (count * rank, rank * rank)
-    tall = jnp.where(iota(spot, 0) % rank == iota(spot, 1) % rank, tall, 0.0)
-    mixer = dot(tall, outer_proj[...].astype(F32), HIGHEST).reshape(count, rank, channels)
-    high, low = (part.astype(F32) for part in split(mixer))
+    diagonal = iota(spot, 0) % rank == iota(spot, 1) % rank
+    tall = []
+    for term in split(left):
+        wide = jnp.broadcast_to(dot(term, repeat)[:, None, :], (count, rank, rank * rank))
+        tall.append(jnp.where(diagonal, wide.reshape(spot), 0.0).astype(BF16))
+    outer = outer_proj[...]
+    mixer = dot(jnp.concatenate(tall, axis=1), jnp.concatenate([outer, outer], axis=0))
+    high, low = (part.astype(F32) for part in split(mixer.reshape(count, rank, channels)))
     mixer = jnp.concatenate([high, high, low, jnp.zeros_like(low)], axis=1).astype(BF16)
     high, low = (part.astype(F32) for part in split(right[...]))
     spread = jnp.concatenate([high, low, high, jnp.zeros_like(low)], axis=1).astype(BF16)
     head_of = iota((1, lanes), 1) // count
     row_of = iota((1, lanes), 1) - head_of * count
     expand = head_of == iota((heads, lanes), 0)
-    high, low = split(dot_tn(bias_proj[...], expand.astype(F32), HIGHEST))
+    high, low = (dot_tn(term, expand.astype(BF16)).astype(BF16) for term in split(bias_proj[...]))
     weights = jnp.concatenate([high, high, low], axis=0)
     apart = jnp.sum(jnp.where(expand, column_of(chain_weight[...]), 0.0), axis=0, keepdims=True)
     chains = jnp.where(row_of == iota((count, lanes), 0), rows_column(query_chain[...]), 0)
     chains = jnp.sum(chains, axis=0, keepdims=True)
-    bias = jnp.zeros((key_count, lanes), F32)
-    copies = []
     for start in range(0, count, GROUP):
         indices = range(start, start + GROUP)
         updates = dot(spread, jnp.concatenate([mixer[index] for index in indices], axis=1))
@@ -150,21 +149,16 @@
             spot = (index // rows, index % rows)
             place = (index - start) * channels
             fresh = pair[spot] + updates[:, place : place + channels]
-            fresh_scratch[index] = fresh
-            copy = pltpu.make_async_copy(fresh_scratch.at[index], pair_out.at[spot], sems.at[index])
-            copy.start()
-            copies.append(copy)
+            pair_out[spot] = fresh
             high, low = split(fresh)
             terms.append(jnp.concatenate([high, low, high], axis=1))
         here = dot(jnp.concatenate(terms, axis=0), weights)
         for index in indices:
             place = (index - start) * key_count
-            bias = jnp.where(row_of == index, here[place : place + key_count], bias)
-    bias = bias + jnp.where(column_of(key_chain[...]) != chains, apart, 0.0)
-    high, low = split(bias)
-    terms_out[...] = jnp.concatenate([high, low], axis=1)
-    for copy in copies:
-        copy.wait()
+            wanted = jnp.broadcast_to(row_of == index, (key_count, lanes))
+            pltpu.store(bias_scratch, here[place : place + key_count], mask=wanted)
+    bias = bias_scratch[...] + jnp.where(column_of(key_chain[...]) != chains, apart, 0.0)
+    terms_out[...] = jnp.concatenate(split(bias), axis=1)
 
 
 def listed(refs):
@@ -174,49 +168,60 @@
     return values
 
 
-def gathered(pieces, start, stop):
-    if len(pieces) == 1:
-        return pieces[0][:, start:stop]
+def gathered(pieces, flips, start, stop):
+    values = listed(pieces)
+    if len(values) == 1:
+        return values[0][:, start:stop]
     col = lax.axis_index("col")
-    ours = listed(pieces[:3])
-    share = ours[0].shape[1]
-    values = [value for both in zip(ours, listed(pieces[3:])) for value in both]
+    share = values[0].shape[1]
     blocks = []
     for target in range(start // share, stop // share):
         chosen = values[0]
-        for index in range(1, len(values)):
-            chosen = jnp.where((col ^ target) == index, values[index], chosen)
+        for flip, value in zip(flips[1:], values[1:]):
+            chosen = jnp.where((col ^ target) == flip, value, chosen)
         blocks.append(chosen)
     return jnp.concatenate(blocks, axis=1)
 
 
-def attend_kernel(pieces, halves, biases, part_out, heads, count):
+def attend_kernel(pieces, flips, halves, biases, part_out, heads, count):
     row = lax.axis_index("row")
-    _, model = halves[0].shape
+    query = gathered(pieces, flips, 0, halves[0].shape[1])
+
+    @pl.when(row == 0)
+    def _():
+        attend(query, halves[::2], halves[1::2], biases, part_out, heads, count)
+
+    @pl.when(row != 0)
+    def _():
+        attend(query, halves[1::2], halves[::2], biases, part_out, heads, count)
+
+
+def attend(query, keys, values, biases, part_out, heads, count):
+    model = query.shape[1]
     head = model // heads
     lanes = heads * count
-    query = gathered(pieces, 0, model)
     biases = [bias[:, :lanes].astype(F32) + bias[:, lanes:].astype(F32) for bias in biases]
-    firsts = [ref[...] for ref in halves[::2]]
-    seconds = [ref[...] for ref in halves[1::2]]
-    keys = [jnp.where(row == 0, first, second) for first, second in zip(firsts, seconds)]
-    values = [jnp.where(row == 0, second, first) for first, second in zip(firsts, seconds)]
     head_of = iota((1, model), 1) // head
     spread = jnp.concatenate(
         [jnp.where(head_of == index, query, jnp.zeros_like(query)) for index in range(heads)],
         axis=0,
     )
     scale = 1.0 / math.sqrt(head)
-    scores = [dot_nt(key, spread) * scale + bias for key, bias in zip(keys, biases)]
+    scores = [dot_nt(key[...], spread) * scale + bias for key, bias in zip(keys, biases)]
     peak = functools.reduce(jnp.maximum, [jnp.max(score, axis=0, keepdims=True) for score in scores])
     exponents = [jnp.exp(score - peak) for score in scores]
     total = sum(jnp.sum(exponent, axis=0, keepdims=True) for exponent in exponents)
-    weights = jnp.concatenate([exponent.astype(BF16) for exponent in exponents], axis=0)
-    summed = dot_tn(weights, jnp.concatenate(values, axis=0))
-    taken = summed[:count]
-    for index in range(1, heads):
-        taken = jnp.where(head_of == index, summed[index * count : (index + 1) * count], taken)
-    part_out[:, :model] = taken.astype(BF16)
+    weights = jnp.concatenate(exponents, axis=0).T.astype(BF16)
+    value = jnp.concatenate([value[...] for value in values], axis=0)
+    group = LANES // head
+    within = iota((1, LANES), 1) // head
+    for first in range(0, heads, group):
+        place = slice(first * head, first * head + LANES)
+        summed = dot(weights[first * count : (first + group) * count], value[:, place])
+        taken = summed[:count]
+        for index in range(1, group):
+            taken = jnp.where(within == index, summed[index * count : (index + 1) * count], taken)
+        part_out[:, place] = taken.astype(BF16)
     row_of = iota((1, lanes), 1) % count
     keep = row_of == iota((count, lanes), 0)
     source = iota((lanes, 1), 0) // count
@@ -236,17 +241,21 @@
     return terms
 
 
-def merged(parts, heads):
-    model = parts[0].shape[1] - LANES
-    count = parts[0].shape[0]
+def spreaders(model, heads):
     term = iota((LANES, 1), 0)
     place = iota((1, model), 1) // (model // heads)
     kind = term // TERM
     wanted = term - kind * TERM
-    for_peak = (jnp.where(kind < 3, wanted, -1) == place).astype(BF16)
-    for_total = (jnp.where((kind >= 3) & (kind < 5), wanted, -1) == place).astype(BF16)
+    for_peak = jnp.where(kind < 3, wanted, -1) == place
+    for_total = jnp.where((kind >= 3) & (kind < 5), wanted, -1) == place
+    return for_peak.astype(BF16), for_total.astype(BF16)
+
+
+def merged(parts, spreads):
+    model = parts[0].shape[1] - LANES
+    count = parts[0].shape[0]
     stats = jnp.concatenate([part[:, model:] for part in parts], axis=0)
-    peaks, totals = dot(stats, for_peak), dot(stats, for_total)
+    peaks, totals = dot(stats, spreads[0]), dot(stats, spreads[1])
     cut = lambda array, index: array[index * count : (index + 1) * count]
     peak = tree(jnp.maximum, [cut(peaks, index) for index in range(len(parts))])
     scales = [jnp.exp(cut(peaks, index) - peak) for index in range(len(parts))]
@@ -264,20 +273,38 @@
     return values[0]
 
 
-def gate_kernel(*refs):
-    pieces, gate_out = refs[:-1], refs[-1]
+def gate_kernel(fresh, *refs, flips, heads):
+    pieces, gate_out, spread_out, pair_out, sem = refs[:-4], *refs[-4:]
+    copy = pltpu.make_async_copy(fresh, pair_out, sem)
+    copy.start()
     model = gate_out.shape[1]
-    gate_out[...] = jax.nn.sigmoid(gathered(pieces, model, 2 * model).astype(F32))
-
-
-def finish_kernel(gate, parts, out_proj, update_out, heads):
-    attended = (merged(listed(parts), heads) * gate[...]).astype(BF16)
+    spread_out[0], spread_out[1] = spreaders(model, heads)
+    gate_out[...] = jax.nn.sigmoid(gathered(pieces, flips, model, 2 * model).astype(F32))
+    copy.wait()
+
+
+def finish_kernel(gate, spreads, *refs):
+    parts, out_proj, update_out = refs[:-2], *refs[-2:]
+    attended = (merged(listed(parts), spreads) * gate[...]).astype(BF16)
     update_out[...] = dot(attended, out_proj[...]).astype(BF16)
 
 
 def exchanged(value, axis, flip):
     size = lax.axis_size(axis)
     return lax.ppermute(value, axis, [(index, index ^ flip) for index in range(size)])
+
+
+def spread_over(part):
+    held, pieces, flips = [part], [part], [0]
+    for group in PLAN:
+        count = len(held)
+        sent = held[0] if count == 1 else jnp.stack(held)
+        for flip in group:
+            piece = exchanged(sent, "col", flip)
+            pieces.append(piece)
+            flips = flips + [flip ^ other for other in flips[:count]]
+            held = held + ([piece] if count == 1 else [piece[i] for i in range(count)])
+    return pieces, flips
 
 
 def on_device(
@@ -304,7 +331,6 @@
     count = slabs * rows
     key_count = key_single.shape[0]
     heads = chain_weight.shape[0]
-    channels = pair_block.shape[-1]
     rank = left_proj.shape[1]
     lanes = heads * count
     cols = lax.axis_size("col")
@@ -337,8 +363,11 @@
         name="query",
     )(timestep, *[pltpu.with_memory_space_constraint(array, pltpu.HBM) for array in now + later])
 
+    flips = [0]
     if direct:
-        beside = exchanged(query_part, "col", 2)
+        pieces, flips = spread_over(query_part)
+    else:
+        pieces = [lax.all_gather(query_part, "col", axis=1, tiled=True)]
 
     half, right = pl.pallas_call(
         key_kernel,
@@ -356,18 +385,15 @@
         far = exchanged(half, "col", 1)
         halves += [far, exchanged(far, "row", 1)]
 
-    new_pair, bias = pl.pallas_call(
+    fresh_pair, bias = pl.pallas_call(
         pair_kernel,
         out_shape=(
             jax.ShapeDtypeStruct(pair_block.shape, F32),
             jax.ShapeDtypeStruct((key_count, 2 * lanes), BF16),
         ),
         in_specs=[VMEM] * 9,
-        out_specs=(HBM, VMEM),
-        scratch_shapes=[
-            pltpu.VMEM((count, key_count, channels), F32),
-            pltpu.SemaphoreType.DMA((count,)),
-        ],
+        out_specs=(VMEM, VMEM),
+        scratch_shapes=[pltpu.VMEM((key_count, lanes), F32)],
         compiler_params=grant,
         name="pairs",
     )(
@@ -381,18 +407,13 @@
         key_chain.reshape(1, key_count),
         pair_block,
     )
+    biases = [bias]
     if direct:
-        biases = [bias, exchanged(bias, "col", 1)]
-        across = exchanged(jnp.stack([query_part, beside]), "col", 4)
-        ours = jnp.stack([query_part, beside, across[0], across[1]])
-        pieces = [query_part, beside, across, exchanged(ours, "col", 1)]
-    else:
-        biases = [bias]
-        pieces = [lax.all_gather(query_part, "col", axis=1, tiled=True)]
+        biases.append(exchanged(bias, "col", 1))
 
     def attend_body(*refs):
         n, k = len(pieces), len(pieces) + len(halves)
-        attend_kernel(refs[:n], refs[n:k], refs[k:-1], refs[-1], heads, count)
+        attend_kernel(refs[:n], flips, refs[n:k], refs[k:-1], refs[-1], heads, count)
 
     part = pl.pallas_call(
         attend_body,
@@ -408,27 +429,32 @@
     else:
         parts = [lax.all_gather(part, "col")]
 
-    gate = pl.pallas_call(
-        gate_kernel,
-        out_shape=jax.ShapeDtypeStruct((count, model), F32),
-        in_specs=[VMEM] * len(pieces),
+    gate, spreads, new_pair = pl.pallas_call(
+        functools.partial(gate_kernel, flips=flips, heads=heads),
+        out_shape=(
+            jax.ShapeDtypeStruct((count, model), F32),
+            jax.ShapeDtypeStruct((2, LANES, model), BF16),
+            jax.ShapeDtypeStruct(pair_block.shape, F32),
+        ),
+        in_specs=[VMEM] * (1 + len(pieces)),
+        out_specs=(VMEM, VMEM, HBM),
+        scratch_shapes=[pltpu.SemaphoreType.DMA],
+        compiler_params=grant,
+        name="gate",
+    )(fresh_pair, *pieces)
+
+    update = pl.pallas_call(
+        finish_kernel,
+        out_shape=jax.ShapeDtypeStruct((count, model), BF16),
+        in_specs=[VMEM] * (len(parts) + 3),
         out_specs=VMEM,
         compiler_params=grant,
-        name="gate",
-    )(*pieces)
-
-    def finish_body(gate, *refs):
-        finish_kernel(gate, refs[:-2], *refs[-2:], heads)
-
-    update = pl.pallas_call(
-        finish_body,
-        out_shape=jax.ShapeDtypeStruct((count, model), BF16),
-        in_specs=[VMEM] * (len(parts) + 2),
-        out_specs=VMEM,
-        compiler_params=grant,
         name="finish",
-    )(gate, *parts, out_proj)
+    )(gate, spreads, *parts, out_proj)
     return (new_pair, update.reshape(slabs, rows, model))
+
+
+PLAN = ((1,), (6, 4, 2))
 
 
 def solution(mesh):

time: 33.3 us -> 36.3 us (1.090)
  starting transfers between devices: 14.1 us -> 17.4 us
  waiting for transfers between devices: 10.7 us -> 10.3 us
    ppermute x10 -> x11, starting transfers between devices: 14.1 us -> 17.4 us  [exchanged(): lax.ppermute(value, axis, [(index, index ^ flip) for index in range(size)])]
    pallas_call x2, Pallas kernels: 1.19 us -> 2.11 us  [the longest x1 1.08 us: on_device(): pl.pallas_call(finish_kernel, out_shape=jax.ShapeDtypeStruct((count, mode...]
    pallas_call x1, Pallas kernels: 2.39 us -> 1.66 us  [on_device(): pl.pallas_call(pair_kernel, out_shape=(jax.ShapeDtypeStruct(pair_block.sh...]
    ppermute x10 -> x11, waiting for transfers between devices: 10.7 us -> 10.3 us  [exchanged(): lax.ppermute(value, axis, [(index, index ^ flip) for index in range(size)])]
  transfers between devices with their start and end apart: 10 -> 11, of which waited for: 4 -> 4; matrix products, arithmetic and copies ran while one was open for 0% -> 0% of each run, Pallas kernels for 7% -> 7%
where the time goes in v6:
time: 36.3 us; the launch traced here: 36.1 us
  starting transfers between devices  17.4 us (48%)
  waiting for transfers between devices  10.3 us (28%)
  Pallas kernels  6.99 us (19%)
  between operations  1.41 us (4%)
    ppermute x11, starting transfers between devices, exchanged(): lax.ppermute(value, axis, [(index, index ^ flip) for index in range(size)])  17.4 us
    ppermute x11, waiting for transfers between devices, exchanged(): lax.ppermute(value, axis, [(index, index ^ flip) for index in range(size)])  10.3 us
    pallas_call x1, Pallas kernels, on_device(): pl.pallas_call(pair_kernel, out_shape=(jax.ShapeDtypeStruct(pair_block.sh...  1.66 us
    pallas_call x1, Pallas kernels, on_device(): pl.pallas_call(query_kernel, out_shape=(jax.ShapeDtypeStruct((count, quer...  1.65 us
    pallas_call x1, Pallas kernels, on_device(): pl.pallas_call(finish_kernel, out_shape=jax.ShapeDtypeStruct((count, mode...  1.08 us
    pallas_call x1, Pallas kernels, on_device(): pl.pallas_call(functools.partial(gate_kernel, flips=flips, heads=heads),...  1.03 us
    pallas_call x1, Pallas kernels, on_device(): pl.pallas_call(attend_body, out_shape=jax.ShapeDtypeStruct((count, model...  0.9 us
  transfers between devices with their start and end apart: 11, of which 4 were waited for; matrix products, arithmetic and copies ran while one was open for 0% of the time, Pallas kernels for 7%

profile of v6, /device:TPU:0, one launch (start us, length us, event | category | flops | bytes accessed | tf_op | source)
XLA Modules:
  0.0 36.1 jit_solution(8103715415564643013)
XLA Ops:
  1.3 1.7 %query.1 = (bf16[16,192]{1,0:T(8,128)(2,1)S(1)}, bf16[16,768]{1,0:T(8,128)(2,1)S(1)}, f32[1,768]{1,0:T(1,128)S(1)}, f32[768]{0:T(1024)S(1)}, bf16[144,768]{1,0:T...) custom-call(s32[1]{0:T(128)S(6)} %copy.20.refs_0_, ...), custom_call_target="tpu_custom_call" | custom-call | tf_op jit(solution)/shard_map/query/pallas_call | solution.py:344
  2.9 0.0 copy-start
  3.0 0.0 copy-start.2
  3.0 0.0 copy-start.3
  3.0 0.0 copy-start.4
  3.0 0.0 copy-start.6
  3.0 0.0 copy-start.7
  3.0 0.7 %keys.1 = (bf16[144,768]{1,0:T(8,128)(2,1)S(1)}, f32[144,8]{1,0:T(8,128)S(1)}) custom-call(f32[1,768]{1,0:T(1,128)S(1)} %get-tuple-element.18.time_row, f32[768]{0:T(1024)S(1)} %get-tuple-element.19.gain, bf16[144,768]{1,0:T(8,128)(2,1)S(1)} %get-tuple-element.20.single, bf16[768,768]{1,0:T(8,128)(2,1)S(1)} %get-tuple-element.21.proj, ...), custom_call_target="tpu_custom_call" | custom-call | tf_op jit(solution)/shard_map/keys/pallas_call | solution.py:372
  3.7 3.0 %collective-permute-start.5 = (bf16[144,768]{1,0:T(8,128)(2,1)S(1)}, bf16[144,768]{1,0:T(8,128)(2,1)S(1)}, u32[]{:S(2)}, u32[]{:S(2)}) collective-permute-start(bf16[144,768]{1,0:T(8,128)(2,1)S(1)} %get-tuple-element.30.refs_5_), channel_id=1, source_target_pairs={{0,2},{2,0},{4,6},{6,4},{8,10},{10,8},{12,14},{14,12},{1,3},{3,1},... | collective-permute-start | bytes 663560 | tf_op jit(solution)/shard_map/ppermute | solution.py:294
  6.7 5.4 %collective-permute-done.5.refs_7_ = bf16[144,768]{1,0:T(8,128)(2,1)S(1)} collective-permute-done((bf16[144,768]{1,0:T(8,128)(2,1)S(1)}, bf16[144,768]{1,0:T(8,128)(2,1)S(1)}, u32[]{:S(2)}, u32[]{:S(2)}) %collective-permute-start.5) | collective-permute-done | bytes 221216 | tf_op jit(solution)/shard_map/ppermute | solution.py:294
  12.2 1.7 %collective-permute-start = (bf16[16,192]{1,0:T(8,128)(2,1)S(1)}, bf16[16,192]{1,0:T(8,128)(2,1)S(1)}, u32[]{:S(2)}, u32[]{:S(2)}) collective-permute-start(bf16[16,192]{1,0:T(8,128)(2,1)S(1)} %get-tuple-element.26.refs_0_), channel_id=1, source_target_pairs={{0,2},{2,0},{4,6},{6,4},{8,10},{10,8},{12,14},{14,12},{1,3},{3,1},... | collective-permute-start | bytes 18440 | tf_op jit(solution)/shard_map/ppermute | solution.py:294
  13.9 1.7 %pairs.1 = (f32[2,8,144,128]{3,2,1,0:T(8,128)S(1)}, bf16[144,384]{1,0:T(8,128)(2,1)S(1)}) custom-call(f32[1,12]{1,0:T(1,128)S(1)} %bitcast.15, s32[2,8]{1,0:T(2,128)S(1)} %copy-done.5, bf16[16,768]{1,0:T(8,128)(2,1)S(1)} %get-tuple-element.17.query_norm, bf16[8,768]{1,0:T(8,128)(2,1)S(1)} %bitcast.12, bf16[64,128]{1,0:T(8,128)(2,1)S(1)} %copy-done.2, ...), custom_call_target="tpu_custom_call" | custom-call | tf_op jit(solution)/shard_map/pairs/pallas_call | solution.py:388
  15.6 0.3 collective-permute-start.7
  16.0 1.9 %collective-permute-start.3 = (bf16[2,16,192]{2,1,0:T(8,128)(2,1)S(1)}, bf16[2,16,192]{2,1,0:T(8,128)(2,1)S(1)}, u32[]{:S(2)}, u32[]{:S(2)}) collective-permute-start(bf16[2,16,192]{2,1,0:T(8,128)(2,1)S(1)} %pad_maximum_fusion), channel_id=1, source_target_pairs={{0,4},{2,6},{4,0},{6,2},{8,12},{10,14},{12,8},{14,10},{1,5},{3,7},... | collective-permute-start | bytes 36872 | tf_op jit(solution)/shard_map/ppermute | solution.py:294
  17.9 2.6 %collective-permute-start.2 = (bf16[2,16,192]{2,1,0:T(8,128)(2,1)S(1)}, bf16[2,16,192]{2,1,0:T(8,128)(2,1)S(1)}, u32[]{:S(2)}, u32[]{:S(2)}) collective-permute-start(bf16[2,16,192]{2,1,0:T(8,128)(2,1)S(1)} %pad_maximum_fusion), channel_id=1, source_target_pairs={{0,8},{2,10},{4,12},{6,14},{8,0},{10,2},{12,4},{14,6},{1,9},{3,11}... | collective-permute-start | bytes 36872 | tf_op jit(solution)/shard_map/ppermute | solution.py:294
  20.5 3.3 %collective-permute-start.1 = (bf16[2,16,192]{2,1,0:T(8,128)(2,1)S(1)}, bf16[2,16,192]{2,1,0:T(8,128)(2,1)S(1)}, u32[]{:S(2)}, u32[]{:S(2)}) collective-permute-start(bf16[2,16,192]{2,1,0:T(8,128)(2,1)S(1)} %pad_maximum_fusion), channel_id=1, source_target_pairs={{0,12},{2,14},{4,8},{6,10},{8,4},{10,6},{12,0},{14,2},{1,13},{3,15... | collective-permute-start | bytes 36872 | tf_op jit(solution)/shard_map/ppermute | solution.py:294
  23.8 2.2 %collective-permute-done.1.refs_2_ = bf16[2,16,192]{2,1,0:T(8,128)(2,1)S(1)} collective-permute-done((bf16[2,16,192]{2,1,0:T(8,128)(2,1)S(1)}, bf16[2,16,192]{2,1,0:T(8,128)(2,1)S(1)}, u32[]{:S(2)}, u32[]{:S(2)}) %collective-permute-start.1) | collective-permute-done | bytes 12320 | tf_op jit(solution)/shard_map/ppermute | solution.py:294
  26.0 0.9 %attend.1.refs_0_ = bf16[16,896]{1,0:T(8,128)(2,1)S(1)} custom-call(bf16[16,192]{1,0:T(8,128)(2,1)S(1)} %get-tuple-element.26.refs_0_, bf16[16,192]{1,0:T(8,128)(2,1)S(1)} %collective-permute-done.refs_1_, bf16[2,16,192]{2,1,0:T(8,128)(2,1)S(1)} %collective-permute-done.1.refs_2_, bf16[2,16,192]{2,1,0:T(8,128)(2,1)S(1)} %collective-permute-done.2.refs_3_, ...), custom_call_target="tpu_custom_call" | custom-call | tf_op jit(solution)/shard_map/attend/pallas_call | solution.py:418
  26.9 3.4 %collective-permute-start.10 = (bf16[16,896]{1,0:T(8,128)(2,1)S(1)}, bf16[16,896]{1,0:T(8,128)(2,1)S(1)}, u32[]{:S(2)}, u32[]{:S(2)}) collective-permute-start(bf16[16,896]{1,0:T(8,128)(2,1)S(1)} %attend.1.refs_0_), channel_id=1, source_target_pairs={{0,12},{2,14},{4,8},{6,10},{8,4},{10,6},{12,0},{14,2},{1,13},{3,15... | collective-permute-start | bytes 86024 | tf_op jit(solution)/shard_map/ppermute | solution.py:294
  30.3 1.0 %collective-permute-start.8 = (bf16[16,896]{1,0:T(8,128)(2,1)S(1)}, bf16[16,896]{1,0:T(8,128)(2,1)S(1)}, u32[]{:S(2)}, u32[]{:S(2)}) collective-permute-start(bf16[16,896]{1,0:T(8,128)(2,1)S(1)} %attend.1.refs_0_), channel_id=1, source_target_pairs={{0,4},{2,6},{4,0},{6,2},{8,12},{10,14},{12,8},{14,10},{1,5},{3,7},... | collective-permute-start | bytes 86024 | tf_op jit(solution)/shard_map/ppermute | solution.py:294
  31.3 1.0 %gate.1 = (f32[16,768]{1,0:T(8,128)S(1)}, bf16[2,128,768]{2,1,0:T(8,128)(2,1)S(1)}, f32[2,8,144,128]{3,2,1,0:T(8,128)}) custom-call(f32[2,8,144,128]{3,2,1,0:T(8,128)S(1)} %get-tuple-element.25.fresh, bf16[16,192]{1,0:T(8,128)(2,1)S(1)} %get-tuple-element.26.refs_0_, bf16[16,192]{1,0:T(8,128)(2,1)S(1)} %collective-permute-done.refs_1_, ...), custom_call_target="tpu_custom_call" | custom-call | tf_op jit(solution)/shard_map/gate/pallas_call | solution.py:432
  32.4 0.4 %collective-permute-done.10.refs_3_ = bf16[16,896]{1,0:T(8,128)(2,1)S(1)} collective-permute-done((bf16[16,896]{1,0:T(8,128)(2,1)S(1)}, bf16[16,896]{1,0:T(8,128)(2,1)S(1)}, u32[]{:S(2)}, u32[]{:S(2)}) %collective-permute-start.10) | collective-permute-done | bytes 28704 | tf_op jit(solution)/shard_map/ppermute | solution.py:294
  32.8 2.3 %collective-permute-done.9.refs_2_ = bf16[16,896]{1,0:T(8,128)(2,1)S(1)} collective-permute-done((bf16[16,896]{1,0:T(8,128)(2,1)S(1)}, bf16[16,896]{1,0:T(8,128)(2,1)S(1)}, u32[]{:S(2)}, u32[]{:S(2)}) %collective-permute-start.9) | collective-permute-done | bytes 28704 | tf_op jit(solution)/shard_map/ppermute | solution.py:294
  35.1 1.1 %finish.1 = bf16[16,768]{1,0:T(8,128)(2,1)} custom-call(f32[16,768]{1,0:T(8,128)S(1)} %get-tuple-element.28.gate, bf16[2,128,768]{2,1,0:T(8,128)(2,1)S(1)} %get-tuple-element.29.spreads, bf16[16,896]{1,0:T(8,128)(2,1)S(1)} %attend.1.refs_0_, bf16[16,896]{1,0:T(8,128)(2,1)S(1)} %collective-permute-done.8.refs_1_, ...), custom_call_target="tpu_custom_call" | custom-call | tf_op jit(solution)/shard_map/finish/pallas_call | solution.py:446
  (21 shorter events, 0.1 us)
Async XLA Ops:
  2.9 11.0 %copy-start = (f32[2,8,144,128]{3,2,1,0:T(8,128)S(1)}, f32[2,8,144,128]{3,2,1,0:T(8,128)}, u32[]{:S(2)}) copy-start(f32[2,8,144,128]{3,2,1,0:T(8,128)} %pair.1) | copy-start | bytes 3538948
  3.0 10.9 %copy-start.2 = (bf16[64,128]{1,0:T(8,128)(2,1)S(1)}, bf16[64,128]{1,0:T(8,128)(2,1)}, u32[]{:S(2)}) copy-start(bf16[64,128]{1,0:T(8,128)(2,1)} %outer_proj.1) | copy-start | bytes 49156
  3.0 10.9 %copy-start.3 = (bf16[768,8]{0,1:T(8,128)(2,1)S(1)}, bf16[768,8]{0,1:T(8,128)(2,1)}, u32[]{:S(2)}) copy-start(bf16[768,8]{0,1:T(8,128)(2,1)} %param.28) | copy-start | bytes 36868
  3.0 10.9 %copy-start.4 = (f32[128,12]{0,1:T(8,128)S(1)}, f32[128,12]{0,1:T(8,128)}, u32[]{:S(2)}) copy-start(f32[128,12]{0,1:T(8,128)} %param.31) | copy-start | bytes 18436
  3.0 10.9 %copy-start.5 = (s32[2,8]{1,0:T(2,128)S(1)}, s32[2,8]{1,0:T(2,128)}, u32[]{:S(2)}) copy-start(s32[2,8]{1,0:T(2,128)} %query_chain.1) | copy-start | bytes 196
  3.0 10.9 %copy-start.6 = (s32[144]{0:T(256)S(1)}, s32[144]{0:T(256)}, u32[]{:S(2)}) copy-start(s32[144]{0:T(256)} %param.22) | copy-start | bytes 1732
  3.0 10.9 %copy-start.7 = (f32[12]{0:T(128)S(1)}, f32[12]{0:T(128)}, u32[]{:S(2)}) copy-start(f32[12]{0:T(128)} %param.32) | copy-start | bytes 148
  3.7 8.5 %collective-permute-start.5 = (bf16[144,768]{1,0:T(8,128)(2,1)S(1)}, bf16[144,768]{1,0:T(8,128)(2,1)S(1)}, u32[]{:S(2)}, u32[]{:S(2)}) collective-permute-start(bf16[144,768]{1,0:T(8,128)(2,1)S(1)} %get-tuple-element.30.refs_5_), channel_id=1, source_target_pairs={{0,2},{2,0},{4,6},{6,4},{8,10},{10,8},{12,14},{14,12},{1,3},{3,1},... | collective-permute-start | bytes 663560 | tf_op jit(solution)/shard_map/ppermute | solution.py:294
  6.7 19.3 %collective-permute-start.4 = (bf16[144,768]{1,0:T(8,128)(2,1)S(1)}, bf16[144,768]{1,0:T(8,128)(2,1)S(1)}, u32[]{:S(2)}, u32[]{:S(2)}) collective-permute-start(bf16[144,768]{1,0:T(8,128)(2,1)S(1)} %get-tuple-element.30.refs_5_), channel_id=1, source_target_pairs={{0,1},{1,0},{2,3},{3,2},{4,5},{5,4},{6,7},{7,6},{8,9},{9,8},{10,11... | collective-permute-start | bytes 663560 | tf_op jit(solution)/shard_map/ppermute | solution.py:294
  12.1 13.9 %collective-permute-start.6 = (bf16[144,768]{1,0:T(8,128)(2,1)S(1)}, bf16[144,768]{1,0:T(8,128)(2,1)S(1)}, u32[]{:S(2)}, u32[]{:S(2)}) collective-permute-start(bf16[144,768]{1,0:T(8,128)(2,1)S(1)} %collective-permute-done.5.refs_7_), channel_id=1, source_target_pairs={{0,1},{1,0},{2,3},{3,2},{4,5},{5,4},{6,7},{7,6},{8,9},{9,8},{10,11... | collective-permute-start | bytes 663560 | tf_op jit(solution)/shard_map/ppermute | solution.py:294
  12.2 3.8 %collective-permute-start = (bf16[16,192]{1,0:T(8,128)(2,1)S(1)}, bf16[16,192]{1,0:T(8,128)(2,1)S(1)}, u32[]{:S(2)}, u32[]{:S(2)}) collective-permute-start(bf16[16,192]{1,0:T(8,128)(2,1)S(1)} %get-tuple-element.26.refs_0_), channel_id=1, source_target_pairs={{0,2},{2,0},{4,6},{6,4},{8,10},{10,8},{12,14},{14,12},{1,3},{3,1},... | collective-permute-start | bytes 18440 | tf_op jit(solution)/shard_map/ppermute | solution.py:294
  15.6 10.4 %collective-permute-start.7 = (bf16[144,384]{1,0:T(8,128)(2,1)S(1)}, bf16[144,384]{1,0:T(8,128)(2,1)S(1)}, u32[]{:S(2)}, u32[]{:S(2)}) collective-permute-start(bf16[144,384]{1,0:T(8,128)(2,1)S(1)} %get-tuple-element.31.refs_9_), channel_id=1, source_target_pairs={{0,2},{2,0},{4,6},{6,4},{8,10},{10,8},{12,14},{14,12},{1,3},{3,1},... | collective-permute-start | bytes 331784 | tf_op jit(solution)/shard_map/ppermute | solution.py:294
  16.0 19.1 %copy-start.1 = (bf16[768,768]{1,0:T(8,128)(2,1)S(1)}, bf16[768,768]{1,0:T(8,128)(2,1)}, u32[]{:S(2)}) copy-start(bf16[768,768]{1,0:T(8,128)(2,1)} %refs_4_.3) | copy-start | bytes 3538948
  16.0 4.5 %collective-permute-start.3 = (bf16[2,16,192]{2,1,0:T(8,128)(2,1)S(1)}, bf16[2,16,192]{2,1,0:T(8,128)(2,1)S(1)}, u32[]{:S(2)}, u32[]{:S(2)}) collective-permute-start(bf16[2,16,192]{2,1,0:T(8,128)(2,1)S(1)} %pad_maximum_fusion), channel_id=1, source_target_pairs={{0,4},{2,6},{4,0},{6,2},{8,12},{10,14},{12,8},{14,10},{1,5},{3,7},... | collective-permute-start | bytes 36872 | tf_op jit(solution)/shard_map/ppermute | solution.py:294
  17.9 5.9 %collective-permute-start.2 = (bf16[2,16,192]{2,1,0:T(8,128)(2,1)S(1)}, bf16[2,16,192]{2,1,0:T(8,128)(2,1)S(1)}, u32[]{:S(2)}, u32[]{:S(2)}) collective-permute-start(bf16[2,16,192]{2,1,0:T(8,128)(2,1)S(1)} %pad_maximum_fusion), channel_id=1, source_target_pairs={{0,8},{2,10},{4,12},{6,14},{8,0},{10,2},{12,4},{14,6},{1,9},{3,11}... | collective-permute-start | bytes 36872 | tf_op jit(solution)/shard_map/ppermute | solution.py:294
  20.5 5.5 %collective-permute-start.1 = (bf16[2,16,192]{2,1,0:T(8,128)(2,1)S(1)}, bf16[2,16,192]{2,1,0:T(8,128)(2,1)S(1)}, u32[]{:S(2)}, u32[]{:S(2)}) collective-permute-start(bf16[2,16,192]{2,1,0:T(8,128)(2,1)S(1)} %pad_maximum_fusion), channel_id=1, source_target_pairs={{0,12},{2,14},{4,8},{6,10},{8,4},{10,6},{12,0},{14,2},{1,13},{3,15... | collective-permute-start | bytes 36872 | tf_op jit(solution)/shard_map/ppermute | solution.py:294
  26.9 5.8 %collective-permute-start.10 = (bf16[16,896]{1,0:T(8,128)(2,1)S(1)}, bf16[16,896]{1,0:T(8,128)(2,1)S(1)}, u32[]{:S(2)}, u32[]{:S(2)}) collective-permute-start(bf16[16,896]{1,0:T(8,128)(2,1)S(1)} %attend.1.refs_0_), channel_id=1, source_target_pairs={{0,12},{2,14},{4,8},{6,10},{8,4},{10,6},{12,0},{14,2},{1,13},{3,15... | collective-permute-start | bytes 86024 | tf_op jit(solution)/shard_map/ppermute | solution.py:294
  30.3 4.8 %collective-permute-start.9 = (bf16[16,896]{1,0:T(8,128)(2,1)S(1)}, bf16[16,896]{1,0:T(8,128)(2,1)S(1)}, u32[]{:S(2)}, u32[]{:S(2)}) collective-permute-start(bf16[16,896]{1,0:T(8,128)(2,1)S(1)} %attend.1.refs_0_), channel_id=1, source_target_pairs={{0,8},{2,10},{4,12},{6,14},{8,0},{10,2},{12,4},{14,6},{1,9},{3,11}... | collective-permute-start | bytes 86024 | tf_op jit(solution)/shard_map/ppermute | solution.py:294
  30.3 4.8 %collective-permute-start.8 = (bf16[16,896]{1,0:T(8,128)(2,1)S(1)}, bf16[16,896]{1,0:T(8,128)(2,1)S(1)}, u32[]{:S(2)}, u32[]{:S(2)}) collective-permute-start(bf16[16,896]{1,0:T(8,128)(2,1)S(1)} %attend.1.refs_0_), channel_id=1, source_target_pairs={{0,4},{2,6},{4,0},{6,2},{8,12},{10,14},{12,8},{14,10},{1,5},{3,7},... | collective-permute-start | bytes 86024 | tf_op jit(solution)/shard_map/ppermute | solution.py:294

commit v7 on v6

--- a/solution.py
+++ b/solution.py
@@ -13,6 +13,7 @@
 LANES = 128
 TERM = LANES // 5
 GROUP = 4
+STACK = 2
 VMEM = pl.BlockSpec(memory_space=pltpu.VMEM)
 HBM = pl.BlockSpec(memory_space=pltpu.HBM)
 SMEM = pl.BlockSpec(memory_space=pltpu.SMEM)
@@ -98,7 +99,7 @@
     right_out[...] = dot_nt(norm, right_proj[...])
 
 
-def pair_kernel(
+def bias_kernel(
     chain_weight,
     query_chain,
     query_norm,
@@ -108,7 +109,8 @@
     right,
     key_chain,
     pair,
-    pair_out,
+    mixer_out,
+    spread_out,
     terms_out,
     bias_scratch,
 ):
@@ -129,35 +131,42 @@
         tall.append(jnp.where(diagonal, wide.reshape(spot), 0.0).astype(BF16))
     outer = outer_proj[...]
     mixer = dot(jnp.concatenate(tall, axis=1), jnp.concatenate([outer, outer], axis=0))
-    high, low = (part.astype(F32) for part in split(mixer.reshape(count, rank, channels)))
-    mixer = jnp.concatenate([high, high, low, jnp.zeros_like(low)], axis=1).astype(BF16)
-    high, low = (part.astype(F32) for part in split(right[...]))
-    spread = jnp.concatenate([high, low, high, jnp.zeros_like(low)], axis=1).astype(BF16)
     head_of = iota((1, lanes), 1) // count
     row_of = iota((1, lanes), 1) - head_of * count
     expand = head_of == iota((heads, lanes), 0)
     high, low = (dot_tn(term, expand.astype(BF16)).astype(BF16) for term in split(bias_proj[...]))
     weights = jnp.concatenate([high, high, low], axis=0)
+    masked = lambda term: [jnp.where(row_of % GROUP == r, term, 0.0).astype(BF16) for r in range(GROUP)]
+    wide = masked(high.astype(F32))
+    wide = jnp.concatenate(wide + wide + masked(low.astype(F32)), axis=0)
+    for start in range(0, count, GROUP * STACK):
+        terms = []
+        for first in range(start, start + GROUP * STACK, GROUP):
+            both = [split(pair[index // rows, index % rows]) for index in range(first, first + GROUP)]
+            highs, lows = [high for high, _ in both], [low for _, low in both]
+            terms.append(jnp.concatenate(highs + lows + highs, axis=1))
+        here = dot(jnp.concatenate(terms, axis=0), wide)
+        for step in range(STACK):
+            wanted = jnp.broadcast_to(row_of // GROUP == start // GROUP + step, (key_count, lanes))
+            place = step * key_count
+            pltpu.store(bias_scratch, here[place : place + key_count], mask=wanted)
+    high, low = split(mixer)
+    folded = dot(jnp.concatenate([high, low, high], axis=1), weights).reshape(count, rank, lanes)
+    folded = sum(jnp.where(row_of == index, folded[index], 0.0) for index in range(count))
+    stacked = lambda first, second, third, axis: jnp.concatenate(
+        [term.astype(F32) for term in (first, second, third)] + [jnp.zeros(first.shape, F32)], axis=axis
+    ).astype(BF16)
+    high, low = split(right[...])
+    spread = stacked(high, low, high, 1)
+    spread_out[...] = spread
+    high, low = split(mixer.reshape(count, rank, channels))
+    mixer_out[...] = stacked(high, high, low, 1)
+    high, low = split(folded)
+    bias = bias_scratch[...] + dot(spread, stacked(high, high, low, 0))
     apart = jnp.sum(jnp.where(expand, column_of(chain_weight[...]), 0.0), axis=0, keepdims=True)
     chains = jnp.where(row_of == iota((count, lanes), 0), rows_column(query_chain[...]), 0)
     chains = jnp.sum(chains, axis=0, keepdims=True)
-    for start in range(0, count, GROUP):
-        indices = range(start, start + GROUP)
-        updates = dot(spread, jnp.concatenate([mixer[index] for index in indices], axis=1))
-        terms = []
-        for index in indices:
-            spot = (index // rows, index % rows)
-            place = (index - start) * channels
-            fresh = pair[spot] + updates[:, place : place + channels]
-            pair_out[spot] = fresh
-            high, low = split(fresh)
-            terms.append(jnp.concatenate([high, low, high], axis=1))
-        here = dot(jnp.concatenate(terms, axis=0), weights)
-        for index in indices:
-            place = (index - start) * key_count
-            wanted = jnp.broadcast_to(row_of == index, (key_count, lanes))
-            pltpu.store(bias_scratch, here[place : place + key_count], mask=wanted)
-    bias = bias_scratch[...] + jnp.where(column_of(key_chain[...]) != chains, apart, 0.0)
+    bias = bias + jnp.where(column_of(key_chain[...]) != chains, apart, 0.0)
     terms_out[...] = jnp.concatenate(split(bias), axis=1)
 
 
@@ -273,14 +282,26 @@
     return values[0]
 
 
-def gate_kernel(fresh, *refs, flips, heads):
-    pieces, gate_out, spread_out, pair_out, sem = refs[:-4], *refs[-4:]
-    copy = pltpu.make_async_copy(fresh, pair_out, sem)
-    copy.start()
+def gate_kernel(pair, mixer, spread, *refs, flips, heads):
+    pieces, gate_out, spread_out, pair_out, fresh, sems = refs[:-5], *refs[-5:]
+    slabs, rows, _, channels = pair.shape
+    keys = spread[...]
+    copies = []
+    for start in range(0, slabs * rows, 2):
+        both = dot(keys, jnp.concatenate([mixer[start], mixer[start + 1]], axis=1))
+        for index in (start, start + 1):
+            spot = (index // rows, index % rows)
+            place = (index - start) * channels
+            fresh[spot] = pair[spot] + both[:, place : place + channels]
+        if (start + 2) % rows == 0:
+            slab = start // rows
+            copies.append(pltpu.make_async_copy(fresh.at[slab], pair_out.at[slab], sems.at[slab]))
+            copies[-1].start()
     model = gate_out.shape[1]
     spread_out[0], spread_out[1] = spreaders(model, heads)
     gate_out[...] = jax.nn.sigmoid(gathered(pieces, flips, model, 2 * model).astype(F32))
-    copy.wait()
+    for copy in copies:
+        copy.wait()
 
 
 def finish_kernel(gate, spreads, *refs):
@@ -331,6 +352,7 @@
     count = slabs * rows
     key_count = key_single.shape[0]
     heads = chain_weight.shape[0]
+    channels = pair_block.shape[-1]
     rank = left_proj.shape[1]
     lanes = heads * count
     cols = lax.axis_size("col")
@@ -385,17 +407,18 @@
         far = exchanged(half, "col", 1)
         halves += [far, exchanged(far, "row", 1)]
 
-    fresh_pair, bias = pl.pallas_call(
-        pair_kernel,
+    mixer, spread, bias = pl.pallas_call(
+        bias_kernel,
         out_shape=(
-            jax.ShapeDtypeStruct(pair_block.shape, F32),
+            jax.ShapeDtypeStruct((count, 4 * rank, channels), BF16),
+            jax.ShapeDtypeStruct((key_count, 4 * rank), BF16),
             jax.ShapeDtypeStruct((key_count, 2 * lanes), BF16),
         ),
         in_specs=[VMEM] * 9,
-        out_specs=(VMEM, VMEM),
+        out_specs=(VMEM, VMEM, VMEM),
         scratch_shapes=[pltpu.VMEM((key_count, lanes), F32)],
         compiler_params=grant,
-        name="pairs",
+        name="biases",
     )(
         chain_weight.reshape(1, heads),
         query_chain,
@@ -436,12 +459,12 @@
             jax.ShapeDtypeStruct((2, LANES, model), BF16),
             jax.ShapeDtypeStruct(pair_block.shape, F32),
         ),
-        in_specs=[VMEM] * (1 + len(pieces)),
+        in_specs=[VMEM] * (3 + len(pieces)),
         out_specs=(VMEM, VMEM, HBM),
-        scratch_shapes=[pltpu.SemaphoreType.DMA],
+        scratch_shapes=[pltpu.VMEM(pair_block.shape, F32), pltpu.SemaphoreType.DMA((slabs,))],
         compiler_params=grant,
         name="gate",
-    )(fresh_pair, *pieces)
+    )(pair_block, mixer, spread, *pieces)
 
     update = pl.pallas_call(
         finish_kernel,

time: 36.3 us -> 36 us (level)
    pallas_call x1, Pallas kernels: 1.66 us -> 1.14 us  [on_device(): pl.pallas_call(bias_kernel, out_shape=(jax.ShapeDtypeStruct((count, 4 * r...]
where the time goes in v7:
time: 36 us; the launch traced here: 35.8 us
  starting transfers between devices  17.2 us (48%)
  waiting for transfers between devices  10.5 us (29%)
  Pallas kernels  6.69 us (19%)
  between operations  1.41 us (4%)
    ppermute x11, starting transfers between devices, exchanged(): lax.ppermute(value, axis, [(index, index ^ flip) for index in range(size)])  17.2 us
    ppermute x11, waiting for transfers between devices, exchanged(): lax.ppermute(value, axis, [(index, index ^ flip) for index in range(size)])  10.5 us
    pallas_call x1, Pallas kernels, on_device(): pl.pallas_call(query_kernel, out_shape=(jax.ShapeDtypeStruct((count, quer...  1.65 us
    pallas_call x1, Pallas kernels, on_device(): pl.pallas_call(functools.partial(gate_kernel, flips=flips, heads=heads),...  1.23 us
    pallas_call x1, Pallas kernels, on_device(): pl.pallas_call(bias_kernel, out_shape=(jax.ShapeDtypeStruct((count, 4 * r...  1.14 us
    pallas_call x1, Pallas kernels, on_device(): pl.pallas_call(finish_kernel, out_shape=jax.ShapeDtypeStruct((count, mode...  1.08 us
    pallas_call x1, Pallas kernels, on_device(): pl.pallas_call(attend_body, out_shape=jax.ShapeDtypeStruct((count, model...  0.91 us
  transfers between devices with their start and end apart: 11, of which 4 were waited for; matrix products, arithmetic and copies ran while one was open for 0% of the time, Pallas kernels for 7%

profile of v7, /device:TPU:0, one launch (start us, length us, event | category | flops | bytes accessed | tf_op | source)
XLA Modules:
  0.0 35.8 jit_solution(1269802367493364990)
XLA Ops:
  1.3 1.7 %query.1 = (bf16[16,192]{1,0:T(8,128)(2,1)S(1)}, bf16[16,768]{1,0:T(8,128)(2,1)S(1)}, f32[1,768]{1,0:T(1,128)S(1)}, f32[768]{0:T(1024)S(1)}, bf16[144,768]{1,0:T...) custom-call(s32[1]{0:T(128)S(6)} %copy.20.refs_0_, ...), custom_call_target="tpu_custom_call" | custom-call | tf_op jit(solution)/shard_map/query/pallas_call | solution.py:366
  2.9 0.0 copy-start
  3.0 0.0 copy-start.2
  3.0 0.0 copy-start.3
  3.0 0.0 copy-start.6
  3.0 0.0 copy-start.7
  3.0 0.7 %keys.1 = (bf16[144,768]{1,0:T(8,128)(2,1)S(1)}, f32[144,8]{1,0:T(8,128)S(1)}) custom-call(f32[1,768]{1,0:T(1,128)S(1)} %get-tuple-element.19.time_row, f32[768]{0:T(1024)S(1)} %get-tuple-element.20.gain, bf16[144,768]{1,0:T(8,128)(2,1)S(1)} %get-tuple-element.21.single, bf16[768,768]{1,0:T(8,128)(2,1)S(1)} %get-tuple-element.22.proj, ...), custom_call_target="tpu_custom_call" | custom-call | tf_op jit(solution)/shard_map/keys/pallas_call | solution.py:394
  3.7 3.0 %collective-permute-start.5 = (bf16[144,768]{1,0:T(8,128)(2,1)S(1)}, bf16[144,768]{1,0:T(8,128)(2,1)S(1)}, u32[]{:S(2)}, u32[]{:S(2)}) collective-permute-start(bf16[144,768]{1,0:T(8,128)(2,1)S(1)} %get-tuple-element.32.refs_5_), channel_id=1, source_target_pairs={{0,2},{2,0},{4,6},{6,4},{8,10},{10,8},{12,14},{14,12},{1,3},{3,1},... | collective-permute-start | bytes 663560 | tf_op jit(solution)/shard_map/ppermute | solution.py:315
  6.7 5.4 %collective-permute-done.5.refs_7_ = bf16[144,768]{1,0:T(8,128)(2,1)S(1)} collective-permute-done((bf16[144,768]{1,0:T(8,128)(2,1)S(1)}, bf16[144,768]{1,0:T(8,128)(2,1)S(1)}, u32[]{:S(2)}, u32[]{:S(2)}) %collective-permute-start.5) | collective-permute-done | bytes 221216 | tf_op jit(solution)/shard_map/ppermute | solution.py:315
  12.2 1.7 %collective-permute-start = (bf16[16,192]{1,0:T(8,128)(2,1)S(1)}, bf16[16,192]{1,0:T(8,128)(2,1)S(1)}, u32[]{:S(2)}, u32[]{:S(2)}) collective-permute-start(bf16[16,192]{1,0:T(8,128)(2,1)S(1)} %get-tuple-element.28.refs_0_), channel_id=1, source_target_pairs={{0,2},{2,0},{4,6},{6,4},{8,10},{10,8},{12,14},{14,12},{1,3},{3,1},... | collective-permute-start | bytes 18440 | tf_op jit(solution)/shard_map/ppermute | solution.py:315
  13.9 1.1 %biases.1 = (bf16[16,32,128]{2,1,0:T(8,128)(2,1)S(1)}, bf16[144,32]{1,0:T(8,128)(2,1)S(1)}, bf16[144,384]{1,0:T(8,128)(2,1)S(1)}) custom-call(f32[1,12]{1,0:T(1,128)S(1)} %bitcast.15, s32[2,8]{1,0:T(2,128)S(1)} %copy-done.5, bf16[16,768]{1,0:T(8,128)(2,1)S(1)} %get-tuple-element.18.query_norm, bf16[8,768]{1,0:T(8,128)(2,1)S(1)} %bitcast.12, ...), custom_call_target="tpu_custom_call" | custom-call | tf_op jit(solution)/shard_map/biases/pallas_call | solution.py:410
  15.1 0.4 collective-permute-start.7
  15.4 0.4 %collective-permute-done.refs_1_ = bf16[16,192]{1,0:T(8,128)(2,1)S(1)} collective-permute-done((bf16[16,192]{1,0:T(8,128)(2,1)S(1)}, bf16[16,192]{1,0:T(8,128)(2,1)S(1)}, u32[]{:S(2)}, u32[]{:S(2)}) %collective-permute-start) | collective-permute-done | bytes 6176 | tf_op jit(solution)/shard_map/ppermute | solution.py:315
  15.8 1.9 %collective-permute-start.3 = (bf16[2,16,192]{2,1,0:T(8,128)(2,1)S(1)}, bf16[2,16,192]{2,1,0:T(8,128)(2,1)S(1)}, u32[]{:S(2)}, u32[]{:S(2)}) collective-permute-start(bf16[2,16,192]{2,1,0:T(8,128)(2,1)S(1)} %pad_maximum_fusion), channel_id=1, source_target_pairs={{0,4},{2,6},{4,0},{6,2},{8,12},{10,14},{12,8},{14,10},{1,5},{3,7},... | collective-permute-start | bytes 36872 | tf_op jit(solution)/shard_map/ppermute | solution.py:315
  17.7 2.6 %collective-permute-start.2 = (bf16[2,16,192]{2,1,0:T(8,128)(2,1)S(1)}, bf16[2,16,192]{2,1,0:T(8,128)(2,1)S(1)}, u32[]{:S(2)}, u32[]{:S(2)}) collective-permute-start(bf16[2,16,192]{2,1,0:T(8,128)(2,1)S(1)} %pad_maximum_fusion), channel_id=1, source_target_pairs={{0,8},{2,10},{4,12},{6,14},{8,0},{10,2},{12,4},{14,6},{1,9},{3,11}... | collective-permute-start | bytes 36872 | tf_op jit(solution)/shard_map/ppermute | solution.py:315
  20.3 3.2 %collective-permute-start.1 = (bf16[2,16,192]{2,1,0:T(8,128)(2,1)S(1)}, bf16[2,16,192]{2,1,0:T(8,128)(2,1)S(1)}, u32[]{:S(2)}, u32[]{:S(2)}) collective-permute-start(bf16[2,16,192]{2,1,0:T(8,128)(2,1)S(1)} %pad_maximum_fusion), channel_id=1, source_target_pairs={{0,12},{2,14},{4,8},{6,10},{8,4},{10,6},{12,0},{14,2},{1,13},{3,15... | collective-permute-start | bytes 36872 | tf_op jit(solution)/shard_map/ppermute | solution.py:315
  23.5 2.4 %collective-permute-done.1.refs_2_ = bf16[2,16,192]{2,1,0:T(8,128)(2,1)S(1)} collective-permute-done((bf16[2,16,192]{2,1,0:T(8,128)(2,1)S(1)}, bf16[2,16,192]{2,1,0:T(8,128)(2,1)S(1)}, u32[]{:S(2)}, u32[]{:S(2)}) %collective-permute-start.1) | collective-permute-done | bytes 12320 | tf_op jit(solution)/shard_map/ppermute | solution.py:315
  25.9 0.9 %attend.1.refs_0_ = bf16[16,896]{1,0:T(8,128)(2,1)S(1)} custom-call(bf16[16,192]{1,0:T(8,128)(2,1)S(1)} %get-tuple-element.28.refs_0_, bf16[16,192]{1,0:T(8,128)(2,1)S(1)} %collective-permute-done.refs_1_, bf16[2,16,192]{2,1,0:T(8,128)(2,1)S(1)} %collective-permute-done.1.refs_2_, bf16[2,16,192]{2,1,0:T(8,128)(2,1)S(1)} %collective-permute-done.2.refs_3_, ...), custom_call_target="tpu_custom_call" | custom-call | tf_op jit(solution)/shard_map/attend/pallas_call | solution.py:441
  26.8 3.2 %collective-permute-start.10 = (bf16[16,896]{1,0:T(8,128)(2,1)S(1)}, bf16[16,896]{1,0:T(8,128)(2,1)S(1)}, u32[]{:S(2)}, u32[]{:S(2)}) collective-permute-start(bf16[16,896]{1,0:T(8,128)(2,1)S(1)} %attend.1.refs_0_), channel_id=1, source_target_pairs={{0,12},{2,14},{4,8},{6,10},{8,4},{10,6},{12,0},{14,2},{1,13},{3,15... | collective-permute-start | bytes 86024 | tf_op jit(solution)/shard_map/ppermute | solution.py:315
  30.0 1.2 %collective-permute-start.8 = (bf16[16,896]{1,0:T(8,128)(2,1)S(1)}, bf16[16,896]{1,0:T(8,128)(2,1)S(1)}, u32[]{:S(2)}, u32[]{:S(2)}) collective-permute-start(bf16[16,896]{1,0:T(8,128)(2,1)S(1)} %attend.1.refs_0_), channel_id=1, source_target_pairs={{0,4},{2,6},{4,0},{6,2},{8,12},{10,14},{12,8},{14,10},{1,5},{3,7},... | collective-permute-start | bytes 86024 | tf_op jit(solution)/shard_map/ppermute | solution.py:315
  31.2 1.2 %gate.1 = (f32[16,768]{1,0:T(8,128)S(1)}, bf16[2,128,768]{2,1,0:T(8,128)(2,1)S(1)}, f32[2,8,144,128]{3,2,1,0:T(8,128)}) custom-call(f32[2,8,144,128]{3,2,1,0:T(8,128)S(1)} %copy-done, bf16[16,32,128]{2,1,0:T(8,128)(2,1)S(1)} %get-tuple-element.26.mixer, bf16[144,32]{1,0:T(8,128)(2,1)S(1)} %get-tuple-element.27.spread, ...), custom_call_target="tpu_custom_call" | custom-call | tf_op jit(solution)/shard_map/gate/pallas_call | solution.py:455
  32.4 0.0 collective-permute-done.10.refs_3_
  32.5 2.3 %collective-permute-done.9.refs_2_ = bf16[16,896]{1,0:T(8,128)(2,1)S(1)} collective-permute-done((bf16[16,896]{1,0:T(8,128)(2,1)S(1)}, bf16[16,896]{1,0:T(8,128)(2,1)S(1)}, u32[]{:S(2)}, u32[]{:S(2)}) %collective-permute-start.9) | collective-permute-done | bytes 28704 | tf_op jit(solution)/shard_map/ppermute | solution.py:315
  34.7 1.1 %finish.1 = bf16[16,768]{1,0:T(8,128)(2,1)} custom-call(f32[16,768]{1,0:T(8,128)S(1)} %get-tuple-element.30.gate, bf16[2,128,768]{2,1,0:T(8,128)(2,1)S(1)} %get-tuple-element.31.spreads, bf16[16,896]{1,0:T(8,128)(2,1)S(1)} %attend.1.refs_0_, bf16[16,896]{1,0:T(8,128)(2,1)S(1)} %collective-permute-done.8.refs_1_, ...), custom_call_target="tpu_custom_call" | custom-call | tf_op jit(solution)/shard_map/finish/pallas_call | solution.py:469
  (21 shorter events, 0.1 us)
Async XLA Ops:
  2.9 11.0 %copy-start = (f32[2,8,144,128]{3,2,1,0:T(8,128)S(1)}, f32[2,8,144,128]{3,2,1,0:T(8,128)}, u32[]{:S(2)}) copy-start(f32[2,8,144,128]{3,2,1,0:T(8,128)} %pair.3) | copy-start | bytes 3538948
  3.0 11.0 %copy-start.2 = (bf16[64,128]{1,0:T(8,128)(2,1)S(1)}, bf16[64,128]{1,0:T(8,128)(2,1)}, u32[]{:S(2)}) copy-start(bf16[64,128]{1,0:T(8,128)(2,1)} %outer_proj.1) | copy-start | bytes 49156
  3.0 10.9 %copy-start.3 = (bf16[768,8]{0,1:T(8,128)(2,1)S(1)}, bf16[768,8]{0,1:T(8,128)(2,1)}, u32[]{:S(2)}) copy-start(bf16[768,8]{0,1:T(8,128)(2,1)} %param.28) | copy-start | bytes 36868
  3.0 10.9 %copy-start.4 = (f32[128,12]{0,1:T(8,128)S(1)}, f32[128,12]{0,1:T(8,128)}, u32[]{:S(2)}) copy-start(f32[128,12]{0,1:T(8,128)} %param.31) | copy-start | bytes 18436
  3.0 10.9 %copy-start.5 = (s32[2,8]{1,0:T(2,128)S(1)}, s32[2,8]{1,0:T(2,128)}, u32[]{:S(2)}) copy-start(s32[2,8]{1,0:T(2,128)} %query_chain.1) | copy-start | bytes 196
  3.0 10.9 %copy-start.6 = (s32[144]{0:T(256)S(1)}, s32[144]{0:T(256)}, u32[]{:S(2)}) copy-start(s32[144]{0:T(256)} %param.22) | copy-start | bytes 1732
  3.0 10.9 %copy-start.7 = (f32[12]{0:T(128)S(1)}, f32[12]{0:T(128)}, u32[]{:S(2)}) copy-start(f32[12]{0:T(128)} %param.32) | copy-start | bytes 148
  3.7 8.5 %collective-permute-start.5 = (bf16[144,768]{1,0:T(8,128)(2,1)S(1)}, bf16[144,768]{1,0:T(8,128)(2,1)S(1)}, u32[]{:S(2)}, u32[]{:S(2)}) collective-permute-start(bf16[144,768]{1,0:T(8,128)(2,1)S(1)} %get-tuple-element.32.refs_5_), channel_id=1, source_target_pairs={{0,2},{2,0},{4,6},{6,4},{8,10},{10,8},{12,14},{14,12},{1,3},{3,1},... | collective-permute-start | bytes 663560 | tf_op jit(solution)/shard_map/ppermute | solution.py:315
  6.7 19.1 %collective-permute-start.4 = (bf16[144,768]{1,0:T(8,128)(2,1)S(1)}, bf16[144,768]{1,0:T(8,128)(2,1)S(1)}, u32[]{:S(2)}, u32[]{:S(2)}) collective-permute-start(bf16[144,768]{1,0:T(8,128)(2,1)S(1)} %get-tuple-element.32.refs_5_), channel_id=1, source_target_pairs={{0,1},{1,0},{2,3},{3,2},{4,5},{5,4},{6,7},{7,6},{8,9},{9,8},{10,11... | collective-permute-start | bytes 663560 | tf_op jit(solution)/shard_map/ppermute | solution.py:315
  12.2 13.7 %collective-permute-start.6 = (bf16[144,768]{1,0:T(8,128)(2,1)S(1)}, bf16[144,768]{1,0:T(8,128)(2,1)S(1)}, u32[]{:S(2)}, u32[]{:S(2)}) collective-permute-start(bf16[144,768]{1,0:T(8,128)(2,1)S(1)} %collective-permute-done.5.refs_7_), channel_id=1, source_target_pairs={{0,1},{1,0},{2,3},{3,2},{4,5},{5,4},{6,7},{7,6},{8,9},{9,8},{10,11... | collective-permute-start | bytes 663560 | tf_op jit(solution)/shard_map/ppermute | solution.py:315
  12.2 3.7 %collective-permute-start = (bf16[16,192]{1,0:T(8,128)(2,1)S(1)}, bf16[16,192]{1,0:T(8,128)(2,1)S(1)}, u32[]{:S(2)}, u32[]{:S(2)}) collective-permute-start(bf16[16,192]{1,0:T(8,128)(2,1)S(1)} %get-tuple-element.28.refs_0_), channel_id=1, source_target_pairs={{0,2},{2,0},{4,6},{6,4},{8,10},{10,8},{12,14},{14,12},{1,3},{3,1},... | collective-permute-start | bytes 18440 | tf_op jit(solution)/shard_map/ppermute | solution.py:315
  15.1 10.8 %collective-permute-start.7 = (bf16[144,384]{1,0:T(8,128)(2,1)S(1)}, bf16[144,384]{1,0:T(8,128)(2,1)S(1)}, u32[]{:S(2)}, u32[]{:S(2)}) collective-permute-start(bf16[144,384]{1,0:T(8,128)(2,1)S(1)} %get-tuple-element.33.refs_9_), channel_id=1, source_target_pairs={{0,2},{2,0},{4,6},{6,4},{8,10},{10,8},{12,14},{14,12},{1,3},{3,1},... | collective-permute-start | bytes 331784 | tf_op jit(solution)/shard_map/ppermute | solution.py:315
  15.8 18.9 %copy-start.1 = (bf16[768,768]{1,0:T(8,128)(2,1)S(1)}, bf16[768,768]{1,0:T(8,128)(2,1)}, u32[]{:S(2)}) copy-start(bf16[768,768]{1,0:T(8,128)(2,1)} %refs_4_.3) | copy-start | bytes 3538948
  15.8 4.5 %collective-permute-start.3 = (bf16[2,16,192]{2,1,0:T(8,128)(2,1)S(1)}, bf16[2,16,192]{2,1,0:T(8,128)(2,1)S(1)}, u32[]{:S(2)}, u32[]{:S(2)}) collective-permute-start(bf16[2,16,192]{2,1,0:T(8,128)(2,1)S(1)} %pad_maximum_fusion), channel_id=1, source_target_pairs={{0,4},{2,6},{4,0},{6,2},{8,12},{10,14},{12,8},{14,10},{1,5},{3,7},... | collective-permute-start | bytes 36872 | tf_op jit(solution)/shard_map/ppermute | solution.py:315
  17.7 5.8 %collective-permute-start.2 = (bf16[2,16,192]{2,1,0:T(8,128)(2,1)S(1)}, bf16[2,16,192]{2,1,0:T(8,128)(2,1)S(1)}, u32[]{:S(2)}, u32[]{:S(2)}) collective-permute-start(bf16[2,16,192]{2,1,0:T(8,128)(2,1)S(1)} %pad_maximum_fusion), channel_id=1, source_target_pairs={{0,8},{2,10},{4,12},{6,14},{8,0},{10,2},{12,4},{14,6},{1,9},{3,11}... | collective-permute-start | bytes 36872 | tf_op jit(solution)/shard_map/ppermute | solution.py:315
  20.3 5.5 %collective-permute-start.1 = (bf16[2,16,192]{2,1,0:T(8,128)(2,1)S(1)}, bf16[2,16,192]{2,1,0:T(8,128)(2,1)S(1)}, u32[]{:S(2)}, u32[]{:S(2)}) collective-permute-start(bf16[2,16,192]{2,1,0:T(8,128)(2,1)S(1)} %pad_maximum_fusion), channel_id=1, source_target_pairs={{0,12},{2,14},{4,8},{6,10},{8,4},{10,6},{12,0},{14,2},{1,13},{3,15... | collective-permute-start | bytes 36872 | tf_op jit(solution)/shard_map/ppermute | solution.py:315
  26.8 5.7 %collective-permute-start.10 = (bf16[16,896]{1,0:T(8,128)(2,1)S(1)}, bf16[16,896]{1,0:T(8,128)(2,1)S(1)}, u32[]{:S(2)}, u32[]{:S(2)}) collective-permute-start(bf16[16,896]{1,0:T(8,128)(2,1)S(1)} %attend.1.refs_0_), channel_id=1, source_target_pairs={{0,12},{2,14},{4,8},{6,10},{8,4},{10,6},{12,0},{14,2},{1,13},{3,15... | collective-permute-start | bytes 86024 | tf_op jit(solution)/shard_map/ppermute | solution.py:315
  29.9 4.8 %collective-permute-start.9 = (bf16[16,896]{1,0:T(8,128)(2,1)S(1)}, bf16[16,896]{1,0:T(8,128)(2,1)S(1)}, u32[]{:S(2)}, u32[]{:S(2)}) collective-permute-start(bf16[16,896]{1,0:T(8,128)(2,1)S(1)} %attend.1.refs_0_), channel_id=1, source_target_pairs={{0,8},{2,10},{4,12},{6,14},{8,0},{10,2},{12,4},{14,6},{1,9},{3,11}... | collective-permute-start | bytes 86024 | tf_op jit(solution)/shard_map/ppermute | solution.py:315
  30.0 4.8 %collective-permute-start.8 = (bf16[16,896]{1,0:T(8,128)(2,1)S(1)}, bf16[16,896]{1,0:T(8,128)(2,1)S(1)}, u32[]{:S(2)}, u32[]{:S(2)}) collective-permute-start(bf16[16,896]{1,0:T(8,128)(2,1)S(1)} %attend.1.refs_0_), channel_id=1, source_target_pairs={{0,4},{2,6},{4,0},{6,2},{8,12},{10,14},{12,8},{14,10},{1,5},{3,7},... | collective-permute-start | bytes 86024 | tf_op jit(solution)/shard_map/ppermute | solution.py:315
